TPU v7x, 128 devices: a whole 4x4x4 slice. The times are simulated.
128 devices in a mesh: ctx: 8 (over z, x_hi), tp: 16 (over x_lo, y, core).
Axes of the slice: x: 4 (x_hi: 2, x_lo: 2; x = x_hi * 2 + x_lo), y: 4, z: 4, core: 2. Of those that a mesh axis runs over, the one named last changes fastest.
Arguments:
- residual_in: bfloat16 [1024, 8192], P('ctx', 'tp'), may hold values from -0.3 to 0.3
- dh_rest: bfloat16 [1024, 8192], P('ctx', 'tp'), may hold values from -0.29882812 to 0.29882812
- w_query: bfloat16 [8192, 8192], P(None, 'tp'), may hold values from -0.0625 to 0.0625
- w_key: bfloat16 [8192, 1024], P(None, 'tp'), may hold values from -0.0625 to 0.0625
- w_value: bfloat16 [8192, 1024], P(None, 'tp'), may hold values from -0.0625 to 0.0625
- q_raw: bfloat16 [1024, 8192], P('ctx', 'tp'), may hold values from -33 to 33
- k_raw: bfloat16 [1024, 1024], P('ctx'), may hold values from -33 to 33
- v_win: bfloat16 [1024, 1024], P('ctx'), may hold values from -6 to 6
- cache_k: bfloat16 [8192, 1024], P('ctx'), may hold values from -90 to 90
- cache_v: bfloat16 [8192, 1024], P('ctx'), may hold values from -6 to 6
- d_attn: bfloat16 [1024, 8192], P('ctx', 'tp'), may hold values from -6 to 6
- s_qk: float32 [128], replicated, may hold values from 0.8 to 5.5
- cache_live: int32 [1], replicated, may hold values from 4096 to 8192
Outputs:
- grad_input: float32 [1024, 8192], P('ctx', 'tp')
All inputs are finite; a program needn't handle non-finite values.
Results may differ from a plain program's by a relative error of at most 0.0025.
The roundings to bfloat16 on the way count: a program that leaves them out, or rounds other values in their place, can miss the bound.
Values may be sent and summed in bfloat16 or wider, within the bound.
No kernel may reach another device: no remote copies, remote signals or barrier semaphores. Data moves between devices by JAX's collectives and lax.ppermute only.
A program may use at most 128 MiB of HBM per device.

v0:
```python
import math

import jax
import jax.numpy as jnp
from jax import lax
from jax.sharding import PartitionSpec as P

D = 8192
KVH = 8
HD = 128


EPS = 1e-06


def swapped(block, axis, apart):
    count = lax.axis_size(axis)
    route = []
    for low in range(count):
        high = low | 1 << apart
        if high != low and high < count:
            route += [(low, high), (high, low)]
    return lax.ppermute(block, axis, route)


def unit_rows(values, qk_gain):
    width = values.shape[-1]
    mean_sq = jnp.mean(values * values, axis=-1, keepdims=True)
    return values * (lax.rsqrt(mean_sq + EPS) / math.sqrt(width)) * qk_gain


def unit_back(values, qk_gain, grad):
    width = values.shape[-1]
    mean_sq = jnp.mean(values * values, axis=-1, keepdims=True)
    factor = lax.rsqrt(mean_sq + EPS) / math.sqrt(width)
    weighted = qk_gain * grad
    inner = jnp.sum(weighted * values, axis=-1, keepdims=True)
    return factor * (weighted - values * inner / (width * (mean_sq + EPS)))


def contract_last(left, right):
    return lax.dot_general(
        left, right, (((1,), (1,)), ((), ())), preferred_element_type=jnp.float32
    )


def contract_first(left, right):
    return lax.dot_general(
        left, right, (((0,), (0,)), ((), ())), preferred_element_type=jnp.float32
    )


def on_device(
    residual_in,
    dh_rest,
    w_query,
    w_key,
    w_value,
    q_raw,
    k_raw,
    v_win,
    cache_k,
    cache_v,
    d_attn,
    s_qk,
    cache_live,
):
    tok_rows = q_raw.shape[0]
    ctx_count = lax.axis_size("ctx")
    tp_count = lax.axis_size("tp")
    head_count = q_raw.shape[1] // HD
    group_size = tp_count // KVH
    tp_index = lax.axis_index("tp")
    ctx_index = lax.axis_index("ctx")
    group_index = tp_index // group_size
    member = tp_index % group_size
    cache_rows = cache_k.shape[0]
    total_cache = cache_rows * ctx_count
    total_tokens = tok_rows * ctx_count
    score_scale = math.sqrt(HD)
    key_raw = lax.dynamic_slice_in_dim(k_raw, group_index * HD, HD, 1).astype(jnp.float32)
    window_pack = jnp.concatenate(
        [
            unit_rows(key_raw, s_qk).astype(jnp.bfloat16),
            lax.dynamic_slice_in_dim(v_win, group_index * HD, HD, 1),
        ],
        1,
    )
    raw_keys = lax.dynamic_slice(cache_k, (0, group_index * HD), (cache_rows, HD)).astype(
        jnp.float32
    )
    raw_values = lax.dynamic_slice(cache_v, (0, group_index * HD), (cache_rows, HD))
    all_cache = lax.all_gather(
        jnp.concatenate([unit_rows(raw_keys, s_qk).astype(jnp.bfloat16), raw_values], 1),
        "ctx",
        axis=0,
        tiled=True,
    )
    all_window = lax.all_gather(window_pack, "ctx", axis=0, tiled=True)
    query_raw = q_raw.astype(jnp.float32).reshape(tok_rows, head_count, HD)
    row_total = head_count * tok_rows
    query_rows = (
        unit_rows(query_raw, s_qk).astype(jnp.bfloat16).transpose(1, 0, 2).reshape(row_total, HD)
    )
    dout_rows = d_attn.reshape(tok_rows, head_count, HD).transpose(1, 0, 2).reshape(row_total, HD)
    query_pos = (
        total_cache + ctx_index * tok_rows + jnp.arange(row_total, dtype=jnp.int32) % tok_rows
    )
    floor_pos = total_cache - cache_live[0]
    all_keys = jnp.concatenate([all_cache, all_window], 0)
    block = math.gcd(math.gcd(1024, total_cache), total_tokens)
    key_blocks = all_keys[:, :HD].reshape(-1, block, HD)
    value_blocks = all_keys[:, HD:].reshape(-1, block, HD)
    block_starts = jnp.arange(key_blocks.shape[0], dtype=jnp.int32) * block
    cache_blocks = total_cache // block

    def block_scores(key_block, start):
        scores = contract_last(query_rows, key_block) * score_scale
        key_pos = start + jnp.arange(block, dtype=jnp.int32)
        visible = (key_pos[None, :] >= floor_pos) & (key_pos[None, :] <= query_pos[:, None])
        return (scores, visible)

    def stat_step(carry, inputs):
        row_max, row_sum, weighted = carry
        key_block, value_block, start = inputs
        scores, visible = block_scores(key_block, start)
        dprobs = contract_last(dout_rows, value_block)
        new_max = jnp.maximum(row_max, jnp.max(jnp.where(visible, scores, -1e30), axis=1))
        rescale = jnp.exp(row_max - new_max)
        expo = jnp.where(visible, jnp.exp(scores - new_max[:, None]), 0.0)
        row_sum = row_sum * rescale + jnp.sum(expo, axis=1)
        weighted = weighted * rescale + jnp.sum(expo * dprobs, axis=1)
        return ((new_max, row_sum, weighted), None)

    start_max = jnp.full((row_total,), -1e30, jnp.float32)
    start_zero = jnp.zeros((row_total,), jnp.float32)
    (row_max, row_sum, weighted), _ = lax.scan(
        stat_step, (start_max, start_zero, start_zero), (key_blocks, value_blocks, block_starts)
    )
    lse = row_max + jnp.log(row_sum)
    delta = weighted / row_sum

    def block_grads(key_block, value_block, start):
        scores, visible = block_scores(key_block, start)
        probs = jnp.where(visible, jnp.exp(scores - lse[:, None]), 0.0)
        dprobs = contract_last(dout_rows, value_block)
        dscores = (probs * (dprobs - delta[:, None])).astype(jnp.bfloat16)
        return (probs, dscores)

    def cache_step(dq_total, inputs):
        key_block, value_block, start = inputs
        probs, dscores = block_grads(key_block, value_block, start)
        return (
            dq_total
            + jnp.dot(dscores, key_block, preferred_element_type=jnp.float32) * score_scale,
            None,
        )

    def window_step(dq_total, inputs):
        key_block, value_block, start = inputs
        probs, dscores = block_grads(key_block, value_block, start)
        dq_total = (
            dq_total + jnp.dot(dscores, key_block, preferred_element_type=jnp.float32) * score_scale
        )
        key_grad = contract_first(dscores, query_rows) * score_scale
        value_grad = contract_first(probs.astype(jnp.bfloat16), dout_rows)
        return (dq_total, jnp.concatenate([key_grad, value_grad], 1))

    dq_rows = jnp.zeros((row_total, HD), jnp.float32)
    dq_rows, _ = lax.scan(
        cache_step,
        dq_rows,
        (key_blocks[:cache_blocks], value_blocks[:cache_blocks], block_starts[:cache_blocks]),
    )
    dq_rows, window_parts = lax.scan(
        window_step,
        dq_rows,
        (key_blocks[cache_blocks:], value_blocks[cache_blocks:], block_starts[cache_blocks:]),
    )
    window_grads = window_parts.reshape(total_tokens, 2 * HD)
    own_grads = lax.psum_scatter(window_grads, "ctx", scatter_dimension=0, tiled=True)
    own_grads = own_grads + swapped(own_grads, "tp", 0)
    key_cols = w_key.shape[1]
    grad_k_full = unit_back(key_raw, s_qk, own_grads[:, :HD]).astype(jnp.bfloat16)
    grad_v_full = own_grads[:, HD:].astype(jnp.bfloat16)
    grad_k = lax.dynamic_slice_in_dim(grad_k_full, member * key_cols, key_cols, 1)
    grad_v = lax.dynamic_slice_in_dim(grad_v_full, member * key_cols, key_cols, 1)
    dq_heads = dq_rows.reshape(head_count, tok_rows, HD).transpose(1, 0, 2)
    grad_q = (
        unit_back(query_raw, s_qk, dq_heads).astype(jnp.bfloat16).reshape(tok_rows, head_count * HD)
    )
    slab = lax.psum_scatter(
        contract_last(w_query, grad_q)
        + contract_last(w_key, grad_k)
        + contract_last(w_value, grad_v),
        "tp",
        scatter_dimension=0,
        tiled=True,
    )
    grad_total = slab.T + dh_rest.astype(jnp.float32)
    resid = residual_in.astype(jnp.float32)
    square_sum, inner_sum = lax.psum(
        (jnp.sum(resid * resid, axis=1), jnp.sum(grad_total * resid, axis=1)), "tp"
    )
    mean_sq = square_sum / D
    factor = lax.rsqrt(mean_sq + EPS) / math.sqrt(D)
    correction = inner_sum / (D * (mean_sq + EPS))
    return factor[:, None] * (grad_total - resid * correction[:, None])


def solution(mesh):
    return jax.shard_map(
        on_device,
        mesh=mesh,
        in_specs=(
            P("ctx", "tp"),
            P("ctx", "tp"),
            P(None, "tp"),
            P(None, "tp"),
            P(None, "tp"),
            P("ctx", "tp"),
            P("ctx", None),
            P("ctx", None),
            P("ctx", None),
            P("ctx", None),
            P("ctx", "tp"),
            P(),
            P(),
        ),
        out_specs=P("ctx", "tp"),
        check_vma=False,
    )
```

profile of v0, /device:TPU:1, one launch (start us, length us, event | category | flops | bytes accessed | tf_op | source)
XLA Modules:
  0.0 376.6 jit_solution(14605620880003129420)
XLA Ops:
  6.5 1.3 fusion.63
  12.9 32.4 %all_gather.7 = bf16[1024,256]{0,1:T(8,128)(2,1)S(1)} all-gather(bf16[128,256]{0,1:T(8,128)(2,1)S(1)} %pad_maximum_fusion.3), channel_id=1, replica_groups=mesh['ctx'=8,'tp'=16] {'ctx'}, dimensions={0}, use_global_device_ids=true | all-gather | bytes 589824 | tf_op jit(solution)/shard_map/all_gather | solution.py:99
  53.2 34.4 %all-gather.2.cloned.1.call-done = bf16[8192,256]{1,0:T(8,128)(2,1)} async-done(((bf16[1024,256]{1,0:T(8,128)(2,1)}), bf16[8192,256]{1,0:T(8,128)(2,1)}) %all-gather.2.cloned.1.call-update) | async-done | bytes 4194320 | tf_op jit(solution)/shard_map/all_gather | solution.py:93
  87.6 7.5 %pad_maximum_fusion = (bf16[9216,128]{1,0:T(8,128)(2,1)}, bf16[9216,128]{1,0:T(8,128)(2,1)}) fusion(bf16[1024,256]{1,0:T(8,128)(2,1)S(1)} %copy.39, bf16[8192,256]{1,0:T(8,128)(2,1)} %all-gather.2.cloned.1.call-done), kind=kLoop, calls=%fused_computation.71 | loop fusion | flops 9437184 | bytes 9437184 | tf_op jit(solution)/shard_map/concatenate | solution.py:110
  95.1 84.7 %while.31 = (s32[]{:T(128)}, f32[512]{0:T(512)S(1)}, f32[512]{0:T(512)S(1)}, f32[512]{0:T(512)S(1)}, s32[9]{0:T(128)}, /*index=5*/s32[]{:T(128)}, bf16[9,1024,12...) while((s32[]{:T(128)}, f32[512]{0:T(512)S(1)}, ...), condition=%wide.region_9.10_spmd.clone, body=%wide.region_5.9_spmd.clone.sunk | while | flops 277882880 | bytes 15533248 | solution.py:137
  97.4 2.9 fusion.133
  100.3 2.3 fusion.135
  102.6 1.8 fusion.134
  106.8 2.9 fusion.133
  109.7 2.3 fusion.135
  112.0 1.8 fusion.134
  116.2 2.9 fusion.133
  119.1 2.3 fusion.135
  121.4 1.8 fusion.134
  125.6 2.9 fusion.133
  128.5 2.3 fusion.135
  130.8 1.8 fusion.134
  135.0 2.9 fusion.133
  137.9 2.3 fusion.135
  140.3 1.8 fusion.134
  144.5 2.9 fusion.133
  147.4 2.3 fusion.135
  149.7 1.8 fusion.134
  153.9 2.9 fusion.133
  156.8 2.3 fusion.135
  159.1 1.8 fusion.134
  163.3 2.9 fusion.133
  166.2 2.3 fusion.135
  168.5 1.8 fusion.134
  172.7 2.9 fusion.133
  175.6 2.3 fusion.135
  177.9 1.8 fusion.134
  183.6 4.5 %fusion.95 = (bf16[8192,128]{1,0:T(8,128)(2,1)}, bf16[8192,128]{1,0:T(8,128)(2,1)}) fusion(bf16[8192,256]{1,0:T(8,128)(2,1)} %all-gather.2.cloned.1.call-done), kind=kLoop, calls=%fused_computation.154 | loop fusion | bytes 8388608 | tf_op jit(solution)/shard_map/slice | solution.py:173
  188.1 72.3 %while.32 = (s32[]{:T(128)}, f32[512,128]{1,0:T(8,128)}, s32[8]{0:T(128)}, s32[]{:T(128)}, bf16[8,1024,128]{2,1,0:T(8,128)(2,1)}, /*index=5*/bf16[512,128]{1,0:T...) while((s32[]{:T(128)}, f32[512,128]{1,0:T(8,128)}, ...), condition=%wide.region_11.12_spmd.clone, body=%wide.region_10.11_spmd.clone.sunk | while | flops 407050752 | bytes 5787299 | solution.py:170
  188.1 2.7 fusion.142
  190.8 1.3 dynamic_slice.118
  193.4 3.7 fusion.144
  197.1 2.7 fusion.142
  199.8 1.3 dynamic_slice.118
  202.3 3.8 %fusion.144 = f32[512,128]{1,0:T(8,128)} fusion(f32[1024,512]{1,0:T(8,128)} %fusion.142, bf16[512,128]{1,0:T(8,128)(2,1)S(1)} %get-tuple-element.522, f32[512]{0:T(512)} %get-tuple-element.523, f32[512]{0:T(512)} %get-tuple-element.520, s32[512]{0:T(512)S(1)} %fusion.143, s32[1024]{0:T(1024)S(1)} %iota_add_fusion.6, ...), kind=kOutput, calls=%fused_computation.37.clone.1 | convolution fusion | flops 272826368 | bytes 3289089 | tf_op jit(solution)/shard_map/while/body/eval_jaxpr/dot_general | solution.py:155
  206.2 2.7 fusion.142
  208.9 1.3 dynamic_slice.118
  211.4 3.8 %fusion.144 = f32[512,128]{1,0:T(8,128)} fusion(f32[1024,512]{1,0:T(8,128)} %fusion.142, bf16[512,128]{1,0:T(8,128)(2,1)S(1)} %get-tuple-element.522, f32[512]{0:T(512)} %get-tuple-element.523, f32[512]{0:T(512)} %get-tuple-element.520, s32[512]{0:T(512)S(1)} %fusion.143, s32[1024]{0:T(1024)S(1)} %iota_add_fusion.6, ...), kind=kOutput, calls=%fused_computation.37.clone.1 | convolution fusion | flops 272826368 | bytes 3289089 | tf_op jit(solution)/shard_map/while/body/eval_jaxpr/dot_general | solution.py:155
  215.2 2.7 fusion.142
  218.0 1.3 dynamic_slice.118
  220.5 3.8 fusion.144
  224.3 2.7 fusion.142
  227.0 1.3 dynamic_slice.118
  229.5 3.8 fusion.144
  233.3 2.7 fusion.142
  236.0 1.3 dynamic_slice.118
  238.6 3.8 %fusion.144 = f32[512,128]{1,0:T(8,128)} fusion(f32[1024,512]{1,0:T(8,128)} %fusion.142, bf16[512,128]{1,0:T(8,128)(2,1)S(1)} %get-tuple-element.522, f32[512]{0:T(512)} %get-tuple-element.523, f32[512]{0:T(512)} %get-tuple-element.520, s32[512]{0:T(512)S(1)} %fusion.143, s32[1024]{0:T(1024)S(1)} %iota_add_fusion.6, ...), kind=kOutput, calls=%fused_computation.37.clone.1 | convolution fusion | flops 272826368 | bytes 3289089 | tf_op jit(solution)/shard_map/while/body/eval_jaxpr/dot_general | solution.py:155
  242.3 2.7 fusion.142
  245.0 1.3 dynamic_slice.118
  247.6 3.8 %fusion.144 = f32[512,128]{1,0:T(8,128)} fusion(f32[1024,512]{1,0:T(8,128)} %fusion.142, bf16[512,128]{1,0:T(8,128)(2,1)S(1)} %get-tuple-element.522, f32[512]{0:T(512)} %get-tuple-element.523, f32[512]{0:T(512)} %get-tuple-element.520, s32[512]{0:T(512)S(1)} %fusion.143, s32[1024]{0:T(1024)S(1)} %iota_add_fusion.6, ...), kind=kOutput, calls=%fused_computation.37.clone.1 | convolution fusion | flops 272826368 | bytes 3289089 | tf_op jit(solution)/shard_map/while/body/eval_jaxpr/dot_general | solution.py:155
  251.4 2.7 fusion.142
  256.6 3.8 fusion.144
  260.4 2.2 fusion.59
  263.9 1.4 collective-permute-start
  265.3 6.3 %fusion.97 = f32[128,8192]{1,0:T(8,128)S(1)} fusion(bf16[128,512]{0,1:T(8,128)(2,1)S(1)} %bitcast.155, bf16[8192,512]{1,0:T(8,128)(2,1)} %param.19), kind=kOutput, calls=%fused_computation.156 | convolution fusion | flops 1073741824 | bytes 12713984 | tf_op jit(solution)/shard_map/dot_general | solution.py:42
  273.1 2.7 fusion.52
  275.8 60.3 %reduce-scatter.5.cloned.1.call-done = f32[512,128]{0,1:T(8,128)} async-done(((f32[8192,128]{0,1:T(8,128)}), f32[512,128]{0,1:T(8,128)}) %reduce-scatter.5.cloned.1.call-update) | async-done | bytes 262160 | tf_op jit(solution)/shard_map/reduce_scatter | solution.py:192
  337.2 31.0 %all-reduce = (f32[128]{0:T(128)S(1)}, f32[128]{0:T(128)S(1)}) all-reduce(f32[128]{0:T(128)S(1)} %get-tuple-element.240, f32[128]{0:T(128)S(1)} %get-tuple-element.239), channel_id=1, replica_groups=mesh['ctx'=8,'tp'=16] {'tp'}, use_global_device_ids=true, to_apply=%region_17.18 | all-reduce | flops 256 | bytes 2048 | tf_op jit(solution)/shard_map/psum | solution.py:202
  368.3 1.8 fusion.70
  (202 shorter events, 51.7 us)
Async XLA Ops:
  6.5 1.7 copy-start
  6.5 6.2 %copy-start.14 = (f32[128]{0:T(128)S(1)}, f32[128]{0:T(128)}, u32[]{:S(2)}) copy-start(f32[128]{0:T(128)} %param.28) | copy-start | bytes 1540
  6.5 81.1 %all-gather.2.cloned.1.call-start = ((), (), s32[]{:S(2)}) async-start(), calls=%async_computation.2 | async-start | bytes 4718592 | tf_op jit(solution)/shard_map/all_gather | solution.py:93
  8.3 37.2 %copy-start.12 = (bf16[128,512]{1,0:T(8,128)(2,1)S(1)}, bf16[128,512]{1,0:T(8,128)(2,1)}, u32[]{:S(2)}) copy-start(bf16[128,512]{1,0:T(8,128)(2,1)} %param.22) | copy-start | bytes 393220
  10.4 253.5 %reduce-scatter.3.cloned.1.call-start = ((), (), s32[]{:S(2)}) async-start(), calls=%async_computation.3 | async-start | bytes 1179648 | tf_op jit(solution)/shard_map/reduce_scatter | solution.py:181
  11.4 1.4 copy-start.6
  12.7 32.5 %copy-start.20 = (f32[128]{0:T(128)}, f32[128]{0:T(128)S(1)}, u32[]{:S(2)}) copy-start(f32[128]{0:T(128)S(1)} %get-tuple-element.304) | copy-start | bytes 1540
  45.3 134.5 %copy-start.2 = (bf16[1024,256]{0,1:T(8,128)(2,1)}, bf16[1024,256]{0,1:T(8,128)(2,1)S(1)}, u32[]{:S(2)}) copy-start(bf16[1024,256]{0,1:T(8,128)(2,1)S(1)} %all_gather.7) | copy-start | bytes 1572868
  95.1 84.7 %copy-start.16 = (s32[1024]{0:T(1024)S(1)}, s32[1024]{0:T(1024)}, u32[]{:S(2)}) copy-start(s32[1024]{0:T(1024)} %iota_add_fusion.2) | copy-start | bytes 12292
  95.1 84.7 %copy-start.19 = (s32[512]{0:T(512)S(1)}, s32[512]{0:T(512)}, u32[]{:S(2)}) copy-start(s32[512]{0:T(512)} %fusion.88) | copy-start | bytes 6148
  95.1 84.7 %copy-start.22 = (pred[1024]{0:T(1024)(128)(4,1)S(1)}, pred[1024]{0:T(1024)(128)(4,1)}, u32[]{:S(2)}) copy-start(pred[1024]{0:T(1024)(128)(4,1)} %broadcast_compare_fusion.2) | copy-start | bytes 3076
  100.3 2.3 copy-start.1
  109.7 2.3 copy-start.1
  119.1 2.3 copy-start.1
  128.5 2.3 copy-start.1
  137.9 2.3 copy-start.1
  147.3 2.3 copy-start.1
  156.7 2.3 copy-start.1
  166.2 2.3 copy-start.1
  175.6 2.3 copy-start.1
  179.8 1.2 copy-start.18
  179.8 1.2 copy-start.13
  180.6 1.0 copy-start.3
  183.6 152.6 %reduce-scatter.5.cloned.1.call-start = ((), (), s32[]{:S(2)}) async-start(), calls=%async_computation.4 | async-start | bytes 4456448 | tf_op jit(solution)/shard_map/reduce_scatter | solution.py:192
  260.4 3.3 copy-start.15
  260.4 3.3 copy-start.17
  263.9 7.7 %collective-permute-start = (f32[128,256]{0,1:T(8,128)}, f32[128,256]{0,1:T(8,128)S(1)}, u32[]{:S(2)}, u32[]{:S(2)}) collective-permute-start(f32[128,256]{0,1:T(8,128)} %reduce-scatter.3.cloned.1.call-done), channel_id=1, source_target_pairs={{0,1},{1,0},{2,3},{3,2},{4,5},{5,4},{6,7},{7,6},{8,9},{9,8},{10,11... | collective-permute-start | bytes 393224 | tf_op jit(solution)/shard_map/ppermute | solution.py:23
  265.3 6.4 %copy-start.11 = (f32[128,256]{0,1:T(8,128)S(1)}, f32[128,256]{0,1:T(8,128)}, u32[]{:S(2)}) copy-start(f32[128,256]{0,1:T(8,128)} %reduce-scatter.3.cloned.1.call-done) | copy-start | bytes 393220
  265.3 6.4 %copy-start.7 = (bf16[128,128]{0,1:T(8,128)(2,1)S(1)}, bf16[128,128]{0,1:T(8,128)(2,1)}, u32[]{:S(2)}) copy-start(bf16[128,128]{0,1:T(8,128)(2,1)} %copy-done.6) | copy-start | bytes 98308
  265.3 6.5 %copy-start.5 = (bf16[8192,64]{0,1:T(8,128)(2,1)S(1)}, bf16[8192,64]{0,1:T(8,128)(2,1)}, u32[]{:S(2)}) copy-start(bf16[8192,64]{0,1:T(8,128)(2,1)} %param.20) | copy-start | bytes 3145732
  265.3 6.5 %copy-start.10 = (f32[128,128]{0,1:T(8,128)S(1)}, f32[128,128]{0,1:T(8,128)}, u32[]{:S(2)}) copy-start(f32[128,128]{0,1:T(8,128)} %convert_element_type.44) | copy-start | bytes 196612
  265.3 6.5 %copy-start.21 = (f32[128]{0:T(128)S(1)}, f32[128]{0:T(128)}, u32[]{:S(2)}) copy-start(f32[128]{0:T(128)} %copy-done.20) | copy-start | bytes 1540
  265.3 6.5 %copy-start.23 = (f32[128]{0:T(128)S(1)}, f32[128]{0:T(128)}, u32[]{:S(2)}) copy-start(f32[128]{0:T(128)} %get-tuple-element.303) | copy-start | bytes 1540
  271.9 1.2 copy-start.4
  275.8 60.4 %copy-start.8 = (bf16[128,512]{1,0:T(8,128)(2,1)S(1)}, bf16[128,512]{1,0:T(8,128)(2,1)}, u32[]{:S(2)}) copy-start(bf16[128,512]{1,0:T(8,128)(2,1)} %param.17) | copy-start | bytes 393220
  275.8 60.4 %copy-start.9 = (bf16[128,512]{1,0:T(8,128)(2,1)S(1)}, bf16[128,512]{1,0:T(8,128)(2,1)}, u32[]{:S(2)}) copy-start(bf16[128,512]{1,0:T(8,128)(2,1)} %param.18) | copy-start | bytes 393220
Sparse Core Ops, SparseCore 0:
  10.5 77.0 all-gather.1
  183.7 68.0 reduce-scatter.2
  275.9 60.1 reduce-scatter.4
where the time goes:
time: 379 us; the launch traced here: 377 us
  matrix products  108 us (28%)
  waiting for transfers between devices  94.8 us (25%)
  blocking collectives  63.5 us (17%)
  other arithmetic  62 us (16%)
  local copies, waits for them, and re-layouts  31.5 us (8%)
  between operations  14.2 us (4%)
    dot_general x31, matrix products, contract_last(): lax.dot_general(left, right, (((1,), (1,)), ((), ())), preferred_element_...  75.3 us
    reduce_scatter x1, waiting for transfers between devices, on_device(): lax.psum_scatter(contract_last(w_query, grad_q) + contract_last(w_key, gr...  60.3 us
    all_gather x1, waiting for transfers between devices, on_device(): lax.all_gather(jnp.concatenate([unit_rows(raw_keys, s_qk).astype(jnp.bflo...  34.4 us
    all_gather x1, blocking collectives, on_device(): all_window = lax.all_gather(window_pack, 'ctx', axis=0, tiled=True)  32.4 us
    psum x1, blocking collectives, on_device(): lax.psum((jnp.sum(resid * resid, axis=1), jnp.sum(grad_total * resid, axi...  31 us
    dot_general x8, matrix products, cache_step(): jnp.dot(dscores, key_block, preferred_element_type=jnp.float32)  30.1 us
    reduce_sum x9, other arithmetic, stat_step(): row_sum = row_sum * rescale + jnp.sum(expo, axis=1)  20.7 us
    add x18, other arithmetic, block_scores(): key_pos = start + jnp.arange(block, dtype=jnp.int32)  11.1 us
  transfers between devices with their start and end apart: 4, of which 2 were waited for; matrix products, arithmetic and copies ran while one was open for 25% of the time, Pallas kernels for 0%

commit v1 on v0

v1 whole, which is shorter than its diff:
```python
import functools
import math

import jax
import jax.numpy as jnp
from jax import lax
from jax.experimental import pallas as pl
from jax.experimental.pallas import tpu as pltpu
from jax.sharding import Mesh
from jax.sharding import PartitionSpec as P

D = 8192
KVH = 8
HD = 128
CACHE = 8192
TOKENS = 1024
KEYS = CACHE + TOKENS
CTX = 8
TOK = TOKENS // CTX
HEADS = 4
ROWS = HEADS * TOK
HALF_CACHE = CACHE // CTX // 2
HALF_WIN = TOK // 2
HALF = HALF_CACHE + HALF_WIN
CUT = HALF // 2
KB = 512
CACHE_BLOCKS = CACHE // KB
WIN_BLOCKS = TOKENS // KB
EPS = 1e-06
SCALE = math.sqrt(HD)
EXP_SCALE = SCALE * math.log2(math.e)
NEG = -1e30
VMEM_LIMIT = 56 * 1024 * 1024
TP_AXES = ("xl", "y", "c")
CTX_AXES = ("z", "xh")
CHIP_AXES = ("xl", "y")


def contract_last(left, right):
    return lax.dot_general(
        left, right, (((1,), (1,)), ((), ())), preferred_element_type=jnp.float32
    )


def contract_first(left, right):
    return lax.dot_general(
        left, right, (((0,), (0,)), ((), ())), preferred_element_type=jnp.float32
    )


def unit_rows(values, qk_gain):
    width = values.shape[-1]
    mean_sq = jnp.mean(values * values, axis=-1, keepdims=True)
    return values * (lax.rsqrt(mean_sq + EPS) / math.sqrt(width)) * qk_gain


def unit_back(values, qk_gain, grad):
    width = values.shape[-1]
    mean_sq = jnp.mean(values * values, axis=-1, keepdims=True)
    factor = lax.rsqrt(mean_sq + EPS) / math.sqrt(width)
    weighted = qk_gain * grad
    inner = jnp.sum(weighted * values, axis=-1, keepdims=True)
    return factor * (weighted - values * inner / (width * (mean_sq + EPS)))


def head_cols(h):
    return slice(h * HD, (h + 1) * HD)


def head_rows(h):
    return slice(h * TOK, (h + 1) * TOK)


def pack_kernel(idx_ref, ck_ref, cv_ref, kr_ref, vw_ref, gain_ref, out_ref):
    gain = gain_ref[...]
    out_ref[:HALF_CACHE, :HD] = unit_rows(ck_ref[...].astype(jnp.float32), gain).astype(
        jnp.bfloat16
    )
    out_ref[:HALF_CACHE, HD:] = cv_ref[...]
    out_ref[HALF_CACHE:, :HD] = unit_rows(kr_ref[...].astype(jnp.float32), gain).astype(
        jnp.bfloat16
    )
    out_ref[HALF_CACHE:, HD:] = vw_ref[...]


def pack_rows(idx, cache_k, cache_v, k_raw, v_win, gain):
    def at(i, idx):
        return (idx[1], idx[0])

    return pl.pallas_call(
        pack_kernel,
        out_shape=jax.ShapeDtypeStruct((HALF, 2 * HD), jnp.bfloat16),
        grid_spec=pltpu.PrefetchScalarGridSpec(
            num_scalar_prefetch=1,
            grid=(1,),
            in_specs=[
                pl.BlockSpec((HALF_CACHE, HD), at),
                pl.BlockSpec((HALF_CACHE, HD), at),
                pl.BlockSpec((HALF_WIN, HD), at),
                pl.BlockSpec((HALF_WIN, HD), at),
                pl.BlockSpec((1, HD), lambda i, idx: (0, 0)),
            ],
            out_specs=pl.BlockSpec((HALF, 2 * HD), lambda i, idx: (0, 0)),
        ),
        name="pack_rows",
    )(idx, cache_k, cache_v, k_raw, v_win, gain)


def visible_mask(info_ref, start):
    kpos = start + lax.broadcasted_iota(jnp.int32, (ROWS, KB), 1)
    qpos = (
        CACHE
        + info_ref[9] * TOK
        + lax.rem(lax.broadcasted_iota(jnp.int32, (ROWS, KB), 0), jnp.int32(TOK))
    )
    return (kpos >= info_ref[8]) & (kpos <= qpos)


def stack_rows(src_ref, dst_ref):
    for h in range(HEADS):
        dst_ref[head_rows(h), :] = src_ref[:, head_cols(h)]


def block_pair(info_ref, q_s, do_s, k_ref, v_ref, b):
    start = pl.multiple_of(b * KB, KB)
    keys = k_ref[pl.ds(start, KB), :]
    scores = contract_last(q_s[...], keys)
    dprobs = contract_last(do_s[...], v_ref[pl.ds(start, KB), :])
    return start, keys, scores, dprobs


def grads_block(info_ref, q_s, do_s, k_ref, v_ref, lse_ref, delta_ref, b, masked):
    start, keys, scores, dprobs = block_pair(info_ref, q_s, do_s, k_ref, v_ref, b)
    lse = lse_ref[...]
    delta = delta_ref[...]
    probs = []
    dscores = []
    mask = visible_mask(info_ref, start) if masked else None
    for g in range(KB // HD):
        cols = head_cols(g)
        p = jnp.exp2(scores[:, cols] * EXP_SCALE - lse)
        if masked:
            p = jnp.where(mask[:, cols], p, 0.0)
            probs.append(p.astype(jnp.bfloat16))
        dscores.append((p * (dprobs[:, cols] - delta)).astype(jnp.bfloat16))
    dscores = jnp.concatenate(dscores, 1)
    probs = jnp.concatenate(probs, 1) if masked else None
    return start, keys, probs, dscores


def stats_kernel(info_ref, *refs):
    pieces = refs[:20]
    q_ref, do_ref, gain_ref = refs[20:23]
    k_ref, v_ref, lse_ref, delta_ref, dq_ref, dkv_ref = refs[23:29]
    q_s, do_s, m_s, l_s, w_s = refs[29:]
    core = info_ref[10]

    def place(piece, source, half, first):
        rows = piece.shape[0]
        cache_rows = min(rows, HALF_CACHE - first)
        at = pl.multiple_of(source * (2 * HALF_CACHE) + half * HALF_CACHE + first, 32)
        k_ref[pl.ds(at, cache_rows), :] = piece[:cache_rows, :HD]
        v_ref[pl.ds(at, cache_rows), :] = piece[:cache_rows, HD:]
        if rows > cache_rows:
            at = pl.multiple_of(CACHE + source * TOK + half * HALF_WIN, HALF_WIN)
            k_ref[pl.ds(at, HALF_WIN), :] = piece[cache_rows:, :HD]
            v_ref[pl.ds(at, HALF_WIN), :] = piece[cache_rows:, HD:]

    for side in range(2):
        half = core if side == 0 else 1 - core
        part = pieces[side * 10 : side * 10 + 10]
        for n in range(6):
            place(part[n], info_ref[n], half, 0)
        for n in range(2):
            place(part[6 + 2 * n], info_ref[6 + n], half, 0)
            place(part[7 + 2 * n], info_ref[6 + n], half, CUT)

    gain = gain_ref[...]
    for h in range(HEADS):
        raw = q_ref[:, head_cols(h)].astype(jnp.float32)
        q_s[head_rows(h), :] = unit_rows(raw, gain).astype(jnp.bfloat16)
    stack_rows(do_ref, do_s)
    m_s[...] = jnp.full((ROWS, HD), NEG, jnp.float32)
    l_s[...] = jnp.zeros((ROWS, HD), jnp.float32)
    w_s[...] = jnp.zeros((ROWS, HD), jnp.float32)

    def stat_block(b, masked):
        start, _, scores, dprobs = block_pair(info_ref, q_s, do_s, k_ref, v_ref, b)
        if masked:
            mask = visible_mask(info_ref, start)
            scores = jnp.where(mask, scores, NEG)
        old = m_s[...]
        top = old
        for g in range(KB // HD):
            top = jnp.maximum(top, scores[:, head_cols(g)])
        keep = jnp.exp2((old - top) * EXP_SCALE)
        total = l_s[...] * keep
        weighted = w_s[...] * keep
        for g in range(KB // HD):
            e = jnp.exp2((scores[:, head_cols(g)] - top) * EXP_SCALE)
            if masked:
                e = jnp.where(mask[:, head_cols(g)], e, 0.0)
            total = total + e
            weighted = weighted + e * dprobs[:, head_cols(g)]
        m_s[...] = top
        l_s[...] = total
        w_s[...] = weighted

    first = info_ref[8] // KB
    win_blocks = info_ref[9] * TOK // KB + 1
    stat_block(first, True)

    @pl.loop(first + 1, CACHE_BLOCKS)
    def _(b):
        stat_block(b, False)

    @pl.loop(CACHE_BLOCKS, CACHE_BLOCKS + win_blocks)
    def _(b):
        stat_block(b, True)

    row_max = jnp.max(m_s[...], axis=1, keepdims=True)
    fix = jnp.exp2((m_s[...] - row_max) * EXP_SCALE)
    total = jnp.sum(l_s[...] * fix, axis=1, keepdims=True)
    weighted = jnp.sum(w_s[...] * fix, axis=1, keepdims=True)
    lse = row_max * EXP_SCALE + jnp.log2(total)
    lse_ref[...] = jnp.broadcast_to(lse, (ROWS, HD))
    delta_ref[...] = jnp.broadcast_to(weighted / total, (ROWS, HD))
    dq_ref[...] = jnp.zeros((ROWS, HD), jnp.float32)
    dkv_ref[...] = jnp.zeros((TOKENS, 2 * HD), jnp.float32)

    @pl.loop(0, win_blocks)
    def _(w):
        start, keys, probs, dscores = grads_block(
            info_ref, q_s, do_s, k_ref, v_ref, lse_ref, delta_ref, CACHE_BLOCKS + w, True
        )
        dq_ref[...] += jnp.dot(dscores, keys, preferred_element_type=jnp.float32)
        at = pl.multiple_of(w * KB, KB)
        dkv_ref[pl.ds(at, KB), :HD] = contract_first(dscores, q_s[...]) * SCALE
        dkv_ref[pl.ds(at, KB), HD:] = contract_first(probs, do_s[...])


def stats_call(info, pieces, q_raw, d_attn, gain):
    shape = jax.ShapeDtypeStruct
    return pl.pallas_call(
        stats_kernel,
        out_shape=(
            shape((KEYS, HD), jnp.bfloat16),
            shape((KEYS, HD), jnp.bfloat16),
            shape((ROWS, HD), jnp.float32),
            shape((ROWS, HD), jnp.float32),
            shape((ROWS, HD), jnp.float32),
            shape((TOKENS, 2 * HD), jnp.float32),
        ),
        in_specs=[pl.BlockSpec(memory_space=pltpu.SMEM)]
        + [pl.BlockSpec(memory_space=pltpu.VMEM)] * 23,
        out_specs=[pl.BlockSpec(memory_space=pltpu.VMEM)] * 6,
        scratch_shapes=[
            pltpu.VMEM((ROWS, HD), jnp.bfloat16),
            pltpu.VMEM((ROWS, HD), jnp.bfloat16),
            pltpu.VMEM((ROWS, HD), jnp.float32),
            pltpu.VMEM((ROWS, HD), jnp.float32),
            pltpu.VMEM((ROWS, HD), jnp.float32),
        ],
        compiler_params=pltpu.CompilerParams(vmem_limit_bytes=VMEM_LIMIT),
        name="attn_stats",
    )(info, *pieces, q_raw, d_attn, gain)


def cache_kernel(
    info_ref,
    k_ref,
    v_ref,
    lse_ref,
    delta_ref,
    dq_in,
    q_ref,
    do_ref,
    gain_ref,
    out_ref,
    q_s,
    do_s,
    dq_s,
):
    gain = gain_ref[...]
    for h in range(HEADS):
        raw = q_ref[:, head_cols(h)].astype(jnp.float32)
        q_s[head_rows(h), :] = unit_rows(raw, gain).astype(jnp.bfloat16)
    stack_rows(do_ref, do_s)
    dq_s[...] = dq_in[...]

    def step(b, masked):
        _, keys, _, dscores = grads_block(
            info_ref, q_s, do_s, k_ref, v_ref, lse_ref, delta_ref, b, masked
        )
        dq_s[...] += jnp.dot(dscores, keys, preferred_element_type=jnp.float32)

    first = info_ref[8] // KB
    step(first, True)

    @pl.loop(first + 1, CACHE_BLOCKS)
    def _(b):
        step(b, False)

    for h in range(HEADS):
        raw = q_ref[:, head_cols(h)].astype(jnp.float32)
        grad = unit_back(raw, gain, dq_s[head_rows(h), :] * SCALE)
        out_ref[:, head_cols(h)] = grad.astype(jnp.bfloat16)


def cache_call(info, keys, values, lse, delta, dq, q_raw, d_attn, gain):
    return pl.pallas_call(
        cache_kernel,
        out_shape=jax.ShapeDtypeStruct((TOK, HEADS * HD), jnp.bfloat16),
        in_specs=[pl.BlockSpec(memory_space=pltpu.SMEM)]
        + [pl.BlockSpec(memory_space=pltpu.VMEM)] * 8,
        out_specs=pl.BlockSpec(memory_space=pltpu.VMEM),
        scratch_shapes=[
            pltpu.VMEM((ROWS, HD), jnp.bfloat16),
            pltpu.VMEM((ROWS, HD), jnp.bfloat16),
            pltpu.VMEM((ROWS, HD), jnp.float32),
        ],
        compiler_params=pltpu.CompilerParams(vmem_limit_bytes=VMEM_LIMIT),
        name="attn_cache",
    )(info, keys, values, lse, delta, dq, q_raw, d_attn, gain)


COLS = HEADS * HD
SIDE = HD // 2
CHIPS = 8
FEAT = D // 16


def project_kernel(idx_ref, gq_ref, gkv_ref, pq_ref, pkv_ref, wq_ref, wkv_ref, wr_ref, out_ref):
    total = contract_last(gq_ref[...], wq_ref[...])
    total += contract_last(gkv_ref[...], wkv_ref[...])
    total += contract_last(pq_ref[...], wr_ref[0, :, :COLS])
    total += contract_last(pkv_ref[...], wr_ref[0, :, COLS:])
    out_ref[0] = total.astype(jnp.bfloat16)


def project(idx, grad_q, grad_kv, pair_q, pair_kv, w_query, w_kv, w_pair):
    def whole(j, idx):
        return (0, 0)

    def own(j, idx):
        return (2 * j + idx[1], 0)

    return pl.pallas_call(
        project_kernel,
        out_shape=jax.ShapeDtypeStruct((CHIPS, TOK, FEAT), jnp.bfloat16),
        grid_spec=pltpu.PrefetchScalarGridSpec(
            num_scalar_prefetch=1,
            grid=(CHIPS,),
            in_specs=[
                pl.BlockSpec((TOK, COLS), whole),
                pl.BlockSpec((TOK, HD), whole),
                pl.BlockSpec((TOK, COLS), whole),
                pl.BlockSpec((TOK, HD), whole),
                pl.BlockSpec((FEAT, COLS), own),
                pl.BlockSpec((FEAT, HD), own),
                pl.BlockSpec((1, FEAT, COLS + HD), lambda j, idx: (j, 0, 0)),
            ],
            out_specs=pl.BlockSpec((1, TOK, FEAT), lambda j, idx: (j, 0, 0)),
        ),
        compiler_params=pltpu.CompilerParams(vmem_limit_bytes=VMEM_LIMIT),
        name="project",
    )(idx, grad_q, grad_kv, pair_q, pair_kv, w_query, w_kv, w_pair)


def shift(block, axis, by):
    count = lax.axis_size(axis)
    return lax.ppermute(block, axis, [(i, (i + by) % count) for i in range(count)])


def swap(block, axis):
    return shift(block, axis, 1)


def on_device(
    residual_in,
    dh_rest,
    w_query,
    w_key,
    w_value,
    q_raw,
    k_raw,
    v_win,
    cache_k,
    cache_v,
    d_attn,
    s_qk,
    cache_live,
):
    z = lax.axis_index("z")
    xh = lax.axis_index("xh")
    chip = lax.axis_index("xl") * 4 + lax.axis_index("y")
    core = lax.axis_index("c")
    ctx = z * 2 + xh
    idx = jnp.stack([chip, core]).astype(jnp.int32)
    gain = s_qk.reshape(1, HD)

    here = pack_rows(idx, cache_k, cache_v, k_raw, v_win, gain)
    there = swap(here, "xh")
    up = shift(here, "z", -1)
    down = shift(here, "z", 1)
    up_there = shift(there, "z", -1)
    down_there = shift(there, "z", 1)
    far_a = shift(up[:CUT], "z", -1)
    far_b = shift(down[CUT:], "z", 1)
    far_there_a = shift(up_there[:CUT], "z", -1)
    far_there_b = shift(down_there[CUT:], "z", 1)
    mine = [here, there, up, down, up_there, down_there, far_a, far_b, far_there_a, far_there_b]
    other = [swap(piece, "c") for piece in mine]

    def source(dz, dx):
        return ((z + dz) % 4) * 2 + (xh + dx) % 2

    hops = [(0, 0), (0, 1), (1, 0), (3, 0), (1, 1), (3, 1), (2, 0), (2, 1)]
    info = jnp.stack(
        [source(dz, dx) for dz, dx in hops] + [CACHE - cache_live[0], ctx, core]
    ).astype(jnp.int32)

    w_kv = jnp.concatenate([w_key, w_value], 1)
    w_blocks = jnp.concatenate(
        [w_query.reshape(CHIPS, 2, FEAT, COLS), w_kv.reshape(CHIPS, 2, FEAT, HD)], 3
    )
    w_pair = swap(
        lax.dynamic_index_in_dim(w_blocks, 1 - core, 1, keepdims=False), "c"
    )

    keys, values, lse, delta, dq, dkv = stats_call(info, mine + other, q_raw, d_attn, gain)
    dkv = dkv.reshape(CTX, TOK, 2 * HD)
    dkv_own = lax.dynamic_index_in_dim(dkv, ctx, 0, keepdims=False)
    arrived = []
    for dz, dx in hops[1:]:
        part = lax.dynamic_index_in_dim(dkv, source(dz, dx), 0, keepdims=False)
        route = []
        for a in range(4):
            for b in range(2):
                route.append((a * 2 + b, ((a + dz) % 4) * 2 + (b + dx) % 2))
        arrived.append(lax.ppermute(part, CTX_AXES, route))
    grad_q = cache_call(info, keys, values, lse, delta, dq, q_raw, d_attn, gain)
    for part in arrived:
        dkv_own = dkv_own + part
    dkv_own = dkv_own + swap(dkv_own, "c")
    key_raw = lax.dynamic_slice_in_dim(k_raw, chip * HD, HD, 1).astype(jnp.float32)
    grad_k = unit_back(key_raw, s_qk, dkv_own[:, :HD]).astype(jnp.bfloat16)
    grad_v = dkv_own[:, HD:].astype(jnp.bfloat16)
    low = jnp.concatenate([grad_k[:, :SIDE], grad_v[:, :SIDE]], 1)
    high = jnp.concatenate([grad_k[:, SIDE:], grad_v[:, SIDE:]], 1)
    own_kv = jnp.where(core == 0, low, high)
    pair_kv = jnp.where(core == 0, high, low)
    pair_q = swap(grad_q, "c")

    partial = project(idx, grad_q, own_kv, pair_q, pair_kv, w_query, w_kv, w_pair)
    pieces = lax.all_to_all(partial, CHIP_AXES, 0, 0)
    grad_total = jnp.sum(pieces.astype(jnp.float32), axis=0) + dh_rest.astype(jnp.float32)
    resid = residual_in.astype(jnp.float32)
    sums = jnp.stack([jnp.sum(resid * resid, axis=1), jnp.sum(grad_total * resid, axis=1)])
    everyone = lax.all_to_all(
        jnp.broadcast_to(sums[None], (16, 2, TOK)), TP_AXES, 0, 0
    )
    square_sum, inner_sum = jnp.sum(everyone, axis=0)
    mean_sq = square_sum / D
    factor = lax.rsqrt(mean_sq + EPS) / math.sqrt(D)
    correction = inner_sum / (D * (mean_sq + EPS))
    return factor[:, None] * (grad_total - resid * correction[:, None])


def solution(mesh):
    fine = Mesh(mesh.devices.reshape(4, 2, 2, 4, 2), ("z", "xh", "xl", "y", "c"))
    both = P(CTX_AXES, TP_AXES)
    cols = P(None, TP_AXES)
    rows = P(CTX_AXES, None)
    return jax.shard_map(
        on_device,
        mesh=fine,
        in_specs=(both, both, cols, cols, cols, both, rows, rows, rows, rows, both, P(), P()),
        out_specs=both,
        check_vma=False,
    )
```

time: 379 us -> 156 us (0.41)
  matrix products: 108 us -> 0 us
  waiting for transfers between devices: 94.8 us -> 14.8 us
  other arithmetic: 62 us -> 13.9 us
  starting transfers between devices: 1.47 us -> 48 us
  Pallas kernels: 0 us -> 38.3 us
  blocking collectives: 63.5 us -> 29.2 us
  local copies, waits for them, and re-layouts: 31.5 us -> 8.74 us
  between operations: 14.2 us -> 0.94 us
    dot_general x42 -> x0, matrix products: 108 us -> none  [the longest x31 75.3 us: contract_last(): lax.dot_general(left, right, (((1,), (1,)), ((), ())), preferred_element_...]
    reduce_scatter x2 -> x0, waiting for transfers between devices: 60.4 us -> none  [the longest x1 60.3 us: on_device(): lax.psum_scatter(contract_last(w_query, grad_q) + contract_last(w_key, gr...]
    ppermute x1 -> x29, starting transfers between devices: 1.39 us -> 48 us  [the longest x22 29.3 us: shift(): lax.ppermute(block, axis, [(i, (i + by) % count) for i in range(count)])]
    pallas_call x0 -> x4, Pallas kernels: none -> 38.3 us  [the longest x1 14.4 us: stats_call(): pl.pallas_call(stats_kernel, out_shape=(shape((KEYS, HD), jnp.bfloat16),...]
    all_gather x1 -> x0, waiting for transfers between devices: 34.4 us -> none  [on_device(): lax.all_gather(jnp.concatenate([unit_rows(raw_keys, s_qk).astype(jnp.bflo...]
    all_gather x1 -> x0, blocking collectives: 32.4 us -> none  [on_device(): all_window = lax.all_gather(window_pack, 'ctx', axis=0, tiled=True)]
    psum x1 -> x0, blocking collectives: 31 us -> none  [on_device(): lax.psum((jnp.sum(resid * resid, axis=1), jnp.sum(grad_total * resid, axi...]
    all_to_all x0 -> x2, blocking collectives: none -> 29.2 us  [the longest x1 18.5 us: on_device(): pieces = lax.all_to_all(partial, CHIP_AXES, 0, 0)]
  transfers between devices with their start and end apart: 4 -> 29, of which waited for: 2 -> 11; matrix products, arithmetic and copies ran while one was open for 25% -> 4% of each run, Pallas kernels for 0% -> 18%
where the time goes in v1:
time: 156 us; the launch traced here: 154 us
  starting transfers between devices  48 us (31%)
  Pallas kernels  38.3 us (25%)
  blocking collectives  29.2 us (19%)
  waiting for transfers between devices  14.8 us (9%)
  other arithmetic  13.9 us (9%)
  local copies, waits for them, and re-layouts  8.74 us (6%)
    ppermute x22, starting transfers between devices, shift(): lax.ppermute(block, axis, [(i, (i + by) % count) for i in range(count)])  29.3 us
    ppermute x7, starting transfers between devices, on_device(): arrived.append(lax.ppermute(part, CTX_AXES, route))  18.7 us
    all_to_all x1, blocking collectives, on_device(): pieces = lax.all_to_all(partial, CHIP_AXES, 0, 0)  18.5 us
    pallas_call x1, Pallas kernels, stats_call(): pl.pallas_call(stats_kernel, out_shape=(shape((KEYS, HD), jnp.bfloat16),...  14.4 us
    pallas_call x1, Pallas kernels, cache_call(): pl.pallas_call(cache_kernel, out_shape=jax.ShapeDtypeStruct((TOK, HEADS *...  11.2 us
    all_to_all x1, blocking collectives, on_device(): lax.all_to_all(jnp.broadcast_to(sums[None], (16, 2, TOK)), TP_AXES, 0, 0)  10.6 us
    ppermute x22, waiting for transfers between devices, shift(): lax.ppermute(block, axis, [(i, (i + by) % count) for i in range(count)])  10.4 us
    pallas_call x1, Pallas kernels, project(): pl.pallas_call(project_kernel, out_shape=jax.ShapeDtypeStruct((CHIPS, TOK...  10.2 us
  transfers between devices with their start and end apart: 29, of which 11 were waited for; matrix products, arithmetic and copies ran while one was open for 4% of the time, Pallas kernels for 18%

profile of v1, /device:TPU:1, one launch (start us, length us, event | category | flops | bytes accessed | tf_op | source)
XLA Modules:
  0.0 153.8 jit_solution(14696013339886135858)
XLA Ops:
  0.0 2.0 %copy.22 = bf16[8192,64]{1,0:T(8,128)(2,1)S(1)} copy(bf16[8192,64]{0,1:T(8,128)(2,1)} %param.16) | data formatting | bytes 2097152 | tf_op args[3]
  2.0 2.8 %copy.23 = bf16[8192,64]{1,0:T(8,128)(2,1)} copy(bf16[8192,64]{0,1:T(8,128)(2,1)} %param.17) | data formatting | bytes 2097152 | tf_op args[4]
  4.8 2.7 %pad_maximum_fusion.wkv_ref = bf16[8192,128]{1,0:T(8,128)(2,1)S(1)} fusion(bf16[8192,64]{1,0:T(8,128)(2,1)} %copy.23, bf16[8192,64]{1,0:T(8,128)(2,1)S(1)} %copy.22), kind=kLoop, calls=%fused_computation.4 | loop fusion | flops 4194304 | bytes 4194304 | tf_op jit(solution)/shard_map/concatenate | solution.py:423
  7.5 5.8 %fusion.1 = bf16[8,512,640]{2,1,0:T(8,128)(2,1)} fusion(s32[]{:T(128)S(6)} %select_n.137, bf16[8,2,512,512]{3,2,1,0:T(8,128)(2,1)} %bitcast.53, bf16[8,2,512,128]{3,2,1,0:T(8,128)(2,1)S(1)} %bitcast.54), kind=kLoop, calls=%fused_computation.3 | loop fusion | flops 10485760 | bytes 15728644 | tf_op jit(solution)/shard_map/jit(dynamic_index_in_dim)/squeeze | solution.py:428
  13.4 1.4 collective-permute-start.28
  14.8 0.7 pad_add_fusion.idx_ref
  15.5 2.5 %pack_rows.1.refs_0_ = bf16[576,256]{1,0:T(8,128)(2,1)} custom-call(s32[2]{0:T(128)} %pad_add_fusion.idx_ref, bf16[1024,1024]{1,0:T(8,128)(2,1)} %ck_ref.1, bf16[1024,1024]{1,0:T(8,128)(2,1)} %cv_ref.1, bf16[128,1024]{1,0:T(8,128)(2,1)} %kr_ref.1, bf16[128,1024]{1,0:T(8,128)(2,1)} %vw_ref.1, f32[1,128]{1,0:T(1,128)} %bitcast.57), custom_call_target="tpu_custom_call" | custom-call | tf_op jit(solution)/shard_map/pack_rows/pallas_call | solution.py:90
  18.0 1.7 %collective-permute-start.2 = (bf16[576,256]{1,0:T(8,128)(2,1)}, bf16[576,256]{1,0:T(8,128)(2,1)S(1)}, u32[]{:S(2)}, u32[]{:S(2)}) collective-permute-start(bf16[576,256]{1,0:T(8,128)(2,1)} %pack_rows.1.refs_0_), channel_id=1, source_target_pairs={{0,32},{32,64},{64,96},{96,0},{1,33},{33,65},{65,97},{97,1},{2,34}... | collective-permute-start | bytes 884744 | tf_op jit(solution)/shard_map/ppermute | solution.py:372
  19.7 2.7 %collective-permute-start = (bf16[576,256]{1,0:T(8,128)(2,1)}, bf16[576,256]{1,0:T(8,128)(2,1)S(1)}, u32[]{:S(2)}, u32[]{:S(2)}) collective-permute-start(bf16[576,256]{1,0:T(8,128)(2,1)} %pack_rows.1.refs_0_), channel_id=1, source_target_pairs={{0,16},{16,0},{1,17},{17,1},{2,18},{18,2},{3,19},{19,3},{4,20},{20... | collective-permute-start | bytes 884744 | tf_op jit(solution)/shard_map/ppermute | solution.py:372
  22.5 2.1 %collective-permute-start.1 = (bf16[576,256]{1,0:T(8,128)(2,1)}, bf16[576,256]{1,0:T(8,128)(2,1)S(1)}, u32[]{:S(2)}, u32[]{:S(2)}) collective-permute-start(bf16[576,256]{1,0:T(8,128)(2,1)} %pack_rows.1.refs_0_), channel_id=1, source_target_pairs={{0,96},{32,0},{64,32},{96,64},{1,97},{33,1},{65,33},{97,65},{2,98}... | collective-permute-start | bytes 884744 | tf_op jit(solution)/shard_map/ppermute | solution.py:372
  24.6 0.6 collective-permute-start.9
  25.2 4.3 %collective-permute-done.2.refs_3_ = bf16[576,256]{1,0:T(8,128)(2,1)S(1)} collective-permute-done((bf16[576,256]{1,0:T(8,128)(2,1)}, bf16[576,256]{1,0:T(8,128)(2,1)S(1)}, u32[]{:S(2)}, u32[]{:S(2)}) %collective-permute-start.2) | collective-permute-done | bytes 294944 | tf_op jit(solution)/shard_map/ppermute | solution.py:372
  29.5 0.1 collective-permute-start.6
  29.5 0.2 collective-permute-done.refs_1_
  29.8 1.6 %collective-permute-start.4 = (bf16[576,256]{1,0:T(8,128)(2,1)S(1)}, bf16[576,256]{1,0:T(8,128)(2,1)S(1)}, u32[]{:S(2)}, u32[]{:S(2)}) collective-permute-start(bf16[576,256]{1,0:T(8,128)(2,1)S(1)} %collective-permute-done.refs_1_), channel_id=1, source_target_pairs={{0,32},{32,64},{64,96},{96,0},{1,33},{33,65},{65,97},{97,1},{2,34}... | collective-permute-start | bytes 884744 | tf_op jit(solution)/shard_map/ppermute | solution.py:372
  31.4 3.0 %collective-permute-start.5 = (bf16[288,256]{1,0:T(8,128)(2,1)S(1)}, bf16[288,256]{1,0:T(8,128)(2,1)S(1)}, u32[]{:S(2)}, u32[]{:S(2)}) collective-permute-start(bf16[288,256]{1,0:T(8,128)(2,1)S(1)} %slice.40), channel_id=1, source_target_pairs={{0,96},{32,0},{64,32},{96,64},{1,97},{33,1},{65,33},{97,65},{2,98}... | collective-permute-start | bytes 442376 | tf_op jit(solution)/shard_map/ppermute | solution.py:372
  34.4 0.1 collective-permute-start.3
  34.5 1.0 collective-permute-done.6.refs_7_
  35.6 2.5 %collective-permute-start.16 = (bf16[288,256]{1,0:T(8,128)(2,1)S(1)}, bf16[288,256]{1,0:T(8,128)(2,1)}, u32[]{:S(2)}, u32[]{:S(2)}) collective-permute-start(bf16[288,256]{1,0:T(8,128)(2,1)S(1)} %collective-permute-done.6.refs_7_), channel_id=1, source_target_pairs={{0,1},{1,0},{2,3},{3,2},{4,5},{5,4},{6,7},{7,6},{8,9},{9,8},{10,11... | collective-permute-start | bytes 442376 | tf_op jit(solution)/shard_map/ppermute | solution.py:372
  38.0 2.1 %collective-permute-start.12 = (bf16[576,256]{1,0:T(8,128)(2,1)S(1)}, bf16[576,256]{1,0:T(8,128)(2,1)S(1)}, u32[]{:S(2)}, u32[]{:S(2)}) collective-permute-start(bf16[576,256]{1,0:T(8,128)(2,1)S(1)} %collective-permute-done.2.refs_3_), channel_id=1, source_target_pairs={{0,1},{1,0},{2,3},{3,2},{4,5},{5,4},{6,7},{7,6},{8,9},{9,8},{10,11... | collective-permute-start | bytes 884744 | tf_op jit(solution)/shard_map/ppermute | solution.py:372
  40.1 0.1 collective-permute-start.11
  40.2 1.7 %collective-permute-done.4.refs_5_ = bf16[576,256]{1,0:T(8,128)(2,1)S(1)} collective-permute-done((bf16[576,256]{1,0:T(8,128)(2,1)S(1)}, bf16[576,256]{1,0:T(8,128)(2,1)S(1)}, u32[]{:S(2)}, u32[]{:S(2)}) %collective-permute-start.4) | collective-permute-done | bytes 294944 | tf_op jit(solution)/shard_map/ppermute | solution.py:372
  41.9 1.4 collective-permute-start.10
  43.3 1.5 collective-permute-start.15
  44.9 0.7 collective-permute-start.8
  45.5 0.3 collective-permute-done.15.refs_16_
  45.8 3.4 %collective-permute-start.7 = (bf16[288,256]{1,0:T(8,128)(2,1)S(1)}, bf16[288,256]{1,0:T(8,128)(2,1)}, u32[]{:S(2)}, u32[]{:S(2)}) collective-permute-start(bf16[288,256]{1,0:T(8,128)(2,1)S(1)} %slice.42), channel_id=1, source_target_pairs={{0,96},{32,0},{64,32},{96,64},{1,97},{33,1},{65,33},{97,65},{2,98}... | collective-permute-start | bytes 442376 | tf_op jit(solution)/shard_map/ppermute | solution.py:372
  49.2 0.7 collective-permute-start.14
  50.0 0.1 collective-permute-start.13
  50.1 2.6 %collective-permute-done.8.refs_9_ = bf16[288,256]{1,0:T(8,128)(2,1)} collective-permute-done((bf16[288,256]{1,0:T(8,128)(2,1)S(1)}, bf16[288,256]{1,0:T(8,128)(2,1)}, u32[]{:S(2)}, u32[]{:S(2)}) %collective-permute-start.8) | collective-permute-done | bytes 147488 | tf_op jit(solution)/shard_map/ppermute | solution.py:372
  52.7 0.6 collective-permute-start.18
  53.3 0.0 collective-permute-start.17
  54.0 0.7 stack.63.info_ref
  54.7 0.3 collective-permute-done.17.refs_18_
  55.1 0.3 copy-done.12
  55.4 0.7 copy-done.13
  56.1 14.4 %attn_stats.1 = (bf16[9216,128]{1,0:T(8,128)(2,1)}, bf16[9216,128]{1,0:T(8,128)(2,1)}, f32[512,128]{1,0:T(8,128)}, f32[512,128]{1,0:T(8,128)}, f32[512,128]{1,0:T(8,128)}, /*index=5*/f32[1024,256]{1,0:T(8,128)}) custom-call(s32[11]{0:T(128)} %stack.63.info_ref, bf16[576,256]{1,0:T(8,128)(2,1)} %pack_rows.1.refs_0_, bf16[576,256]{1,0:T(8,128)(2,1)} %copy-done.7, ...), custom_call_target="tpu_custom_call" | custom-call | tf_op jit(solution)/shard_map/attn_stats/pallas_call | solution.py:244
  70.5 1.3 dynamic-slice_bitcast_fusion.6
  71.8 0.0 copy-start.18
  71.8 1.5 collective-permute-start.19
  73.3 5.5 %collective-permute-start.25 = (f32[128,256]{1,0:T(8,128)S(1)}, f32[128,256]{1,0:T(8,128)S(1)}, u32[]{:S(2)}, u32[]{:S(2)}) collective-permute-start(f32[128,256]{1,0:T(8,128)S(1)} %get-tuple-element.24), channel_id=1, source_target_pairs={{0,80},{16,64},{32,112},{48,96},{64,16},{80,0},{96,48},{112,32},{1... | collective-permute-start | bytes 393224 | tf_op jit(solution)/shard_map/ppermute | solution.py:441
  78.8 4.5 %collective-permute-start.23 = (f32[128,256]{1,0:T(8,128)S(1)}, f32[128,256]{1,0:T(8,128)S(1)}, u32[]{:S(2)}, u32[]{:S(2)}) collective-permute-start(f32[128,256]{1,0:T(8,128)S(1)} %get-tuple-element.26), channel_id=1, source_target_pairs={{0,112},{16,96},{32,16},{48,0},{64,48},{80,32},{96,80},{112,64},{1... | collective-permute-start | bytes 393224 | tf_op jit(solution)/shard_map/ppermute | solution.py:441
  83.2 2.0 %collective-permute-done.25 = f32[128,256]{1,0:T(8,128)S(1)} collective-permute-done((f32[128,256]{1,0:T(8,128)S(1)}, f32[128,256]{1,0:T(8,128)S(1)}, u32[]{:S(2)}, u32[]{:S(2)}) %collective-permute-start.25) | collective-permute-done | bytes 131104 | tf_op jit(solution)/shard_map/ppermute | solution.py:441
  85.3 2.5 %collective-permute-start.21 = (f32[128,256]{1,0:T(8,128)S(1)}, f32[128,256]{1,0:T(8,128)S(1)}, u32[]{:S(2)}, u32[]{:S(2)}) collective-permute-start(f32[128,256]{1,0:T(8,128)S(1)} %get-tuple-element.28), channel_id=1, source_target_pairs={{0,96},{16,112},{32,0},{48,16},{64,32},{80,48},{96,64},{112,80},{1... | collective-permute-start | bytes 393224 | tf_op jit(solution)/shard_map/ppermute | solution.py:441
  87.8 0.4 collective-permute-done.24
  88.1 4.8 %collective-permute-start.20 = (f32[128,256]{1,0:T(8,128)S(1)}, f32[128,256]{1,0:T(8,128)S(1)}, u32[]{:S(2)}, u32[]{:S(2)}) collective-permute-start(f32[128,256]{1,0:T(8,128)S(1)} %get-tuple-element.29), channel_id=1, source_target_pairs={{0,32},{16,48},{32,64},{48,80},{64,96},{80,112},{96,0},{112,16},{1... | collective-permute-start | bytes 393224 | tf_op jit(solution)/shard_map/ppermute | solution.py:441
  92.9 0.4 collective-permute-done.21
  93.2 1.7 %collective-permute-done.20 = f32[128,256]{1,0:T(8,128)S(1)} collective-permute-done((f32[128,256]{1,0:T(8,128)S(1)}, f32[128,256]{1,0:T(8,128)S(1)}, u32[]{:S(2)}, u32[]{:S(2)}) %collective-permute-start.20) | collective-permute-done | bytes 131104 | tf_op jit(solution)/shard_map/ppermute | solution.py:441
  94.9 1.0 fusion.11
  95.9 2.8 %collective-permute-start.26 = (f32[128,256]{1,0:T(8,128)S(1)}, f32[128,256]{1,0:T(8,128)S(1)}, u32[]{:S(2)}, u32[]{:S(2)}) collective-permute-start(f32[128,256]{1,0:T(8,128)S(1)} %fusion.11), channel_id=1, source_target_pairs={{0,1},{1,0},{2,3},{3,2},{4,5},{5,4},{6,7},{7,6},{8,9},{9,8},{10,11... | collective-permute-start | bytes 393224 | tf_op jit(solution)/shard_map/ppermute | solution.py:372
  98.7 11.2 %attn_cache.1.gq_ref = bf16[128,512]{1,0:T(8,128)(2,1)} custom-call(s32[11]{0:T(128)} %stack.63.info_ref, bf16[9216,128]{1,0:T(8,128)(2,1)} %get-tuple-element.11.k_ref, bf16[9216,128]{1,0:T(8,128)(2,1)} %get-tuple-element.12.v_ref, f32[512,128]{1,0:T(8,128)} %get-tuple-element.13.lse_ref, f32[512,128]{1,0:T(8,128)} %get-tuple-element.14.delta_ref, ...), custom_call_target="tpu_custom_call" | custom-call | tf_op jit(solution)/shard_map/attn_cache/pallas_call | solution.py:311
  109.9 0.0 collective-permute-start.27
  109.9 0.9 fusion.13
  110.8 0.1 fusion.20
  110.9 0.9 fusion.17
  111.8 0.1 fusion.21
  111.9 0.7 broadcast_select_fusion
  112.6 0.6 copy-done.17
  113.3 10.2 %project.1 = bf16[8,128,512]{2,1,0:T(8,128)(2,1)} custom-call(s32[2]{0:T(128)} %pad_add_fusion.idx_ref, bf16[128,512]{1,0:T(8,128)(2,1)} %attn_cache.1.gq_ref, bf16[128,128]{1,0:T(8,128)(2,1)} %get-tuple-element.31.gkv_ref, bf16[128,512]{1,0:T(8,128)(2,1)} %copy-done.17, bf16[128,128]{1,0:T(8,128)(2,1)} %get-tuple-element.30.pkv_ref, ...), custom_call_target="tpu_custom_call" | custom-call | tf_op jit(solution)/shard_map/project/pallas_call | solution.py:348
  123.4 18.5 %all_to_all.10 = bf16[8,128,512]{2,1,0:T(8,128)(2,1)S(1)} all-to-all(bf16[8,128,512]{2,1,0:T(8,128)(2,1)} %project.1), channel_id=1, replica_groups=mesh['z'=4,'xh'=2,'xl'=2,'y'=4,'c'=2] {'xl','y'}, dimensions={0} | all-to-all | bytes 2097152 | tf_op jit(solution)/shard_map/all_to_all | solution.py:456
  142.0 0.1 convert_reduce_fusion
  142.2 0.1 fusion.2
  142.3 10.6 %all_to_all.11 = f32[16,2,128]{2,1,0:T(2,128)S(1)} all-to-all(f32[16,2,128]{2,1,0:T(2,128)S(1)} %broadcast_in_dim.2), channel_id=1, replica_groups=mesh['z'=4,'xh'=2,'xl'=2,'y'=4,'c'=2] {'xl','y','c'}, dimensions={0} | all-to-all | bytes 32768 | tf_op jit(solution)/shard_map/all_to_all | solution.py:460
  153.0 0.8 fusion.5
  (64 shorter events, 0.2 us)
Async XLA Ops:
  7.5 5.9 %copy-start = (bf16[8192,128]{1,0:T(8,128)(2,1)}, bf16[8192,128]{1,0:T(8,128)(2,1)S(1)}, u32[]{:S(2)}) copy-start(bf16[8192,128]{1,0:T(8,128)(2,1)S(1)} %pad_maximum_fusion.wkv_ref) | copy-start | bytes 6291460
  13.4 99.3 %collective-permute-start.28 = (bf16[8,512,640]{2,1,0:T(8,128)(2,1)}, bf16[8,512,640]{2,1,0:T(8,128)(2,1)}, u32[]{:S(2)}, u32[]{:S(2)}) collective-permute-start(bf16[8,512,640]{2,1,0:T(8,128)(2,1)} %fusion.1), channel_id=1, source_target_pairs={{0,1},{1,0},{2,3},{3,2},{4,5},{5,4},{6,7},{7,6},{8,9},{9,8},{10,11... | collective-permute-start | bytes 15728648 | tf_op jit(solution)/shard_map/ppermute | solution.py:372
  18.0 11.4 %collective-permute-start.2 = (bf16[576,256]{1,0:T(8,128)(2,1)}, bf16[576,256]{1,0:T(8,128)(2,1)S(1)}, u32[]{:S(2)}, u32[]{:S(2)}) collective-permute-start(bf16[576,256]{1,0:T(8,128)(2,1)} %pack_rows.1.refs_0_), channel_id=1, source_target_pairs={{0,32},{32,64},{64,96},{96,0},{1,33},{33,65},{65,97},{97,1},{2,34}... | collective-permute-start | bytes 884744 | tf_op jit(solution)/shard_map/ppermute | solution.py:372
  19.7 10.0 %collective-permute-start = (bf16[576,256]{1,0:T(8,128)(2,1)}, bf16[576,256]{1,0:T(8,128)(2,1)S(1)}, u32[]{:S(2)}, u32[]{:S(2)}) collective-permute-start(bf16[576,256]{1,0:T(8,128)(2,1)} %pack_rows.1.refs_0_), channel_id=1, source_target_pairs={{0,16},{16,0},{1,17},{17,1},{2,18},{18,2},{3,19},{19,3},{4,20},{20... | collective-permute-start | bytes 884744 | tf_op jit(solution)/shard_map/ppermute | solution.py:372
  22.5 8.9 %collective-permute-start.1 = (bf16[576,256]{1,0:T(8,128)(2,1)}, bf16[576,256]{1,0:T(8,128)(2,1)S(1)}, u32[]{:S(2)}, u32[]{:S(2)}) collective-permute-start(bf16[576,256]{1,0:T(8,128)(2,1)} %pack_rows.1.refs_0_), channel_id=1, source_target_pairs={{0,96},{32,0},{64,32},{96,64},{1,97},{33,1},{65,33},{97,65},{2,98}... | collective-permute-start | bytes 884744 | tf_op jit(solution)/shard_map/ppermute | solution.py:372
  24.6 9.8 %collective-permute-start.9 = (bf16[576,256]{1,0:T(8,128)(2,1)}, bf16[576,256]{1,0:T(8,128)(2,1)S(1)}, u32[]{:S(2)}, u32[]{:S(2)}) collective-permute-start(bf16[576,256]{1,0:T(8,128)(2,1)} %pack_rows.1.refs_0_), channel_id=1, source_target_pairs={{0,1},{1,0},{2,3},{3,2},{4,5},{5,4},{6,7},{7,6},{8,9},{9,8},{10,11... | collective-permute-start | bytes 884744 | tf_op jit(solution)/shard_map/ppermute | solution.py:372
  29.4 25.5 %copy-start.1 = (bf16[576,256]{1,0:T(8,128)(2,1)}, bf16[576,256]{1,0:T(8,128)(2,1)S(1)}, u32[]{:S(2)}) copy-start(bf16[576,256]{1,0:T(8,128)(2,1)S(1)} %collective-permute-done.2.refs_3_) | copy-start | bytes 884740
  29.5 6.1 %collective-permute-start.6 = (bf16[288,256]{1,0:T(8,128)(2,1)S(1)}, bf16[288,256]{1,0:T(8,128)(2,1)S(1)}, u32[]{:S(2)}, u32[]{:S(2)}) collective-permute-start(bf16[288,256]{1,0:T(8,128)(2,1)S(1)} %slice.41), channel_id=1, source_target_pairs={{0,32},{32,64},{64,96},{96,0},{1,33},{33,65},{65,97},{97,1},{2,34}... | collective-permute-start | bytes 442376 | tf_op jit(solution)/shard_map/ppermute | solution.py:372
  29.8 25.2 %copy-start.7 = (bf16[576,256]{1,0:T(8,128)(2,1)}, bf16[576,256]{1,0:T(8,128)(2,1)S(1)}, u32[]{:S(2)}) copy-start(bf16[576,256]{1,0:T(8,128)(2,1)S(1)} %collective-permute-done.refs_1_) | copy-start | bytes 884740
  29.8 12.1 %collective-permute-start.4 = (bf16[576,256]{1,0:T(8,128)(2,1)S(1)}, bf16[576,256]{1,0:T(8,128)(2,1)S(1)}, u32[]{:S(2)}, u32[]{:S(2)}) collective-permute-start(bf16[576,256]{1,0:T(8,128)(2,1)S(1)} %collective-permute-done.refs_1_), channel_id=1, source_target_pairs={{0,32},{32,64},{64,96},{96,0},{1,33},{33,65},{65,97},{97,1},{2,34}... | collective-permute-start | bytes 884744 | tf_op jit(solution)/shard_map/ppermute | solution.py:372
  31.4 23.6 %copy-start.2 = (bf16[576,256]{1,0:T(8,128)(2,1)}, bf16[576,256]{1,0:T(8,128)(2,1)S(1)}, u32[]{:S(2)}) copy-start(bf16[576,256]{1,0:T(8,128)(2,1)S(1)} %collective-permute-done.1.refs_2_) | copy-start | bytes 884740
  31.4 6.6 %collective-permute-start.5 = (bf16[288,256]{1,0:T(8,128)(2,1)S(1)}, bf16[288,256]{1,0:T(8,128)(2,1)S(1)}, u32[]{:S(2)}, u32[]{:S(2)}) collective-permute-start(bf16[288,256]{1,0:T(8,128)(2,1)S(1)} %slice.40), channel_id=1, source_target_pairs={{0,96},{32,0},{64,32},{96,64},{1,97},{33,1},{65,33},{97,65},{2,98}... | collective-permute-start | bytes 442376 | tf_op jit(solution)/shard_map/ppermute | solution.py:372
  34.4 20.6 %copy-start.8 = (bf16[576,256]{1,0:T(8,128)(2,1)}, bf16[576,256]{1,0:T(8,128)(2,1)S(1)}, u32[]{:S(2)}) copy-start(bf16[576,256]{1,0:T(8,128)(2,1)S(1)} %collective-permute-done.9.refs_10_) | copy-start | bytes 884740
  34.4 8.9 %collective-permute-start.3 = (bf16[576,256]{1,0:T(8,128)(2,1)S(1)}, bf16[576,256]{1,0:T(8,128)(2,1)S(1)}, u32[]{:S(2)}, u32[]{:S(2)}) collective-permute-start(bf16[576,256]{1,0:T(8,128)(2,1)S(1)} %collective-permute-done.refs_1_), channel_id=1, source_target_pairs={{0,96},{32,0},{64,32},{96,64},{1,97},{33,1},{65,33},{97,65},{2,98}... | collective-permute-start | bytes 884744 | tf_op jit(solution)/shard_map/ppermute | solution.py:372
  35.6 19.4 %copy-start.14 = (bf16[288,256]{1,0:T(8,128)(2,1)}, bf16[288,256]{1,0:T(8,128)(2,1)S(1)}, u32[]{:S(2)}) copy-start(bf16[288,256]{1,0:T(8,128)(2,1)S(1)} %collective-permute-done.6.refs_7_) | copy-start | bytes 442372
  35.6 4.6 %collective-permute-start.16 = (bf16[288,256]{1,0:T(8,128)(2,1)S(1)}, bf16[288,256]{1,0:T(8,128)(2,1)}, u32[]{:S(2)}, u32[]{:S(2)}) collective-permute-start(bf16[288,256]{1,0:T(8,128)(2,1)S(1)} %collective-permute-done.6.refs_7_), channel_id=1, source_target_pairs={{0,1},{1,0},{2,3},{3,2},{4,5},{5,4},{6,7},{7,6},{8,9},{9,8},{10,11... | collective-permute-start | bytes 442376 | tf_op jit(solution)/shard_map/ppermute | solution.py:372
  38.0 17.0 %copy-start.15 = (bf16[288,256]{1,0:T(8,128)(2,1)}, bf16[288,256]{1,0:T(8,128)(2,1)S(1)}, u32[]{:S(2)}) copy-start(bf16[288,256]{1,0:T(8,128)(2,1)S(1)} %collective-permute-done.5.refs_6_) | copy-start | bytes 442372
  38.0 6.8 %collective-permute-start.12 = (bf16[576,256]{1,0:T(8,128)(2,1)S(1)}, bf16[576,256]{1,0:T(8,128)(2,1)S(1)}, u32[]{:S(2)}, u32[]{:S(2)}) collective-permute-start(bf16[576,256]{1,0:T(8,128)(2,1)S(1)} %collective-permute-done.2.refs_3_), channel_id=1, source_target_pairs={{0,1},{1,0},{2,3},{3,2},{4,5},{5,4},{6,7},{7,6},{8,9},{9,8},{10,11... | collective-permute-start | bytes 884744 | tf_op jit(solution)/shard_map/ppermute | solution.py:372
  40.1 9.1 %collective-permute-start.11 = (bf16[576,256]{1,0:T(8,128)(2,1)S(1)}, bf16[576,256]{1,0:T(8,128)(2,1)S(1)}, u32[]{:S(2)}, u32[]{:S(2)}) collective-permute-start(bf16[576,256]{1,0:T(8,128)(2,1)S(1)} %collective-permute-done.1.refs_2_), channel_id=1, source_target_pairs={{0,1},{1,0},{2,3},{3,2},{4,5},{5,4},{6,7},{7,6},{8,9},{9,8},{10,11... | collective-permute-start | bytes 884744 | tf_op jit(solution)/shard_map/ppermute | solution.py:372
  41.9 13.1 %copy-start.3 = (bf16[576,256]{1,0:T(8,128)(2,1)}, bf16[576,256]{1,0:T(8,128)(2,1)S(1)}, u32[]{:S(2)}) copy-start(bf16[576,256]{1,0:T(8,128)(2,1)S(1)} %collective-permute-done.4.refs_5_) | copy-start | bytes 884740
  41.9 8.1 %collective-permute-start.10 = (bf16[576,256]{1,0:T(8,128)(2,1)S(1)}, bf16[576,256]{1,0:T(8,128)(2,1)S(1)}, u32[]{:S(2)}, u32[]{:S(2)}) collective-permute-start(bf16[576,256]{1,0:T(8,128)(2,1)S(1)} %collective-permute-done.refs_1_), channel_id=1, source_target_pairs={{0,1},{1,0},{2,3},{3,2},{4,5},{5,4},{6,7},{7,6},{8,9},{9,8},{10,11... | collective-permute-start | bytes 884744 | tf_op jit(solution)/shard_map/ppermute | solution.py:372
  43.3 11.7 %copy-start.4 = (bf16[576,256]{1,0:T(8,128)(2,1)}, bf16[576,256]{1,0:T(8,128)(2,1)S(1)}, u32[]{:S(2)}) copy-start(bf16[576,256]{1,0:T(8,128)(2,1)S(1)} %collective-permute-done.3.refs_4_) | copy-start | bytes 884740
  43.3 2.5 %collective-permute-start.15 = (bf16[288,256]{1,0:T(8,128)(2,1)S(1)}, bf16[288,256]{1,0:T(8,128)(2,1)S(1)}, u32[]{:S(2)}, u32[]{:S(2)}) collective-permute-start(bf16[288,256]{1,0:T(8,128)(2,1)S(1)} %collective-permute-done.5.refs_6_), channel_id=1, source_target_pairs={{0,1},{1,0},{2,3},{3,2},{4,5},{5,4},{6,7},{7,6},{8,9},{9,8},{10,11... | collective-permute-start | bytes 442376 | tf_op jit(solution)/shard_map/ppermute | solution.py:372
  44.9 10.2 %copy-start.9 = (bf16[576,256]{1,0:T(8,128)(2,1)}, bf16[576,256]{1,0:T(8,128)(2,1)S(1)}, u32[]{:S(2)}) copy-start(bf16[576,256]{1,0:T(8,128)(2,1)S(1)} %collective-permute-done.12.refs_13_) | copy-start | bytes 884740
  44.9 7.8 %collective-permute-start.8 = (bf16[288,256]{1,0:T(8,128)(2,1)S(1)}, bf16[288,256]{1,0:T(8,128)(2,1)}, u32[]{:S(2)}, u32[]{:S(2)}) collective-permute-start(bf16[288,256]{1,0:T(8,128)(2,1)S(1)} %slice.43), channel_id=1, source_target_pairs={{0,32},{32,64},{64,96},{96,0},{1,33},{33,65},{65,97},{97,1},{2,34}... | collective-permute-start | bytes 442376 | tf_op jit(solution)/shard_map/ppermute | solution.py:372
  45.8 3.4 %copy-start.16 = (bf16[288,256]{1,0:T(8,128)(2,1)}, bf16[288,256]{1,0:T(8,128)(2,1)S(1)}, u32[]{:S(2)}) copy-start(bf16[288,256]{1,0:T(8,128)(2,1)S(1)} %collective-permute-done.15.refs_16_) | copy-start | bytes 442372
  45.8 7.4 %collective-permute-start.7 = (bf16[288,256]{1,0:T(8,128)(2,1)S(1)}, bf16[288,256]{1,0:T(8,128)(2,1)}, u32[]{:S(2)}, u32[]{:S(2)}) collective-permute-start(bf16[288,256]{1,0:T(8,128)(2,1)S(1)} %slice.42), channel_id=1, source_target_pairs={{0,96},{32,0},{64,32},{96,64},{1,97},{33,1},{65,33},{97,65},{2,98}... | collective-permute-start | bytes 442376 | tf_op jit(solution)/shard_map/ppermute | solution.py:372
  49.2 5.8 %copy-start.10 = (bf16[576,256]{1,0:T(8,128)(2,1)}, bf16[576,256]{1,0:T(8,128)(2,1)S(1)}, u32[]{:S(2)}) copy-start(bf16[576,256]{1,0:T(8,128)(2,1)S(1)} %collective-permute-done.11.refs_12_) | copy-start | bytes 884740
  49.2 5.4 %collective-permute-start.14 = (bf16[576,256]{1,0:T(8,128)(2,1)S(1)}, bf16[576,256]{1,0:T(8,128)(2,1)S(1)}, u32[]{:S(2)}, u32[]{:S(2)}) collective-permute-start(bf16[576,256]{1,0:T(8,128)(2,1)S(1)} %collective-permute-done.4.refs_5_), channel_id=1, source_target_pairs={{0,1},{1,0},{2,3},{3,2},{4,5},{5,4},{6,7},{7,6},{8,9},{9,8},{10,11... | collective-permute-start | bytes 884744 | tf_op jit(solution)/shard_map/ppermute | solution.py:372
  50.0 5.1 %copy-start.11 = (bf16[576,256]{1,0:T(8,128)(2,1)}, bf16[576,256]{1,0:T(8,128)(2,1)S(1)}, u32[]{:S(2)}) copy-start(bf16[576,256]{1,0:T(8,128)(2,1)S(1)} %collective-permute-done.10.refs_11_) | copy-start | bytes 884740
  50.0 5.0 %collective-permute-start.13 = (bf16[576,256]{1,0:T(8,128)(2,1)S(1)}, bf16[576,256]{1,0:T(8,128)(2,1)S(1)}, u32[]{:S(2)}, u32[]{:S(2)}) collective-permute-start(bf16[576,256]{1,0:T(8,128)(2,1)S(1)} %collective-permute-done.3.refs_4_), channel_id=1, source_target_pairs={{0,1},{1,0},{2,3},{3,2},{4,5},{5,4},{6,7},{7,6},{8,9},{9,8},{10,11... | collective-permute-start | bytes 884744 | tf_op jit(solution)/shard_map/ppermute | solution.py:372
  52.7 2.0 %collective-permute-start.18 = (bf16[288,256]{1,0:T(8,128)(2,1)}, bf16[288,256]{1,0:T(8,128)(2,1)}, u32[]{:S(2)}, u32[]{:S(2)}) collective-permute-start(bf16[288,256]{1,0:T(8,128)(2,1)} %collective-permute-done.8.refs_9_), channel_id=1, source_target_pairs={{0,1},{1,0},{2,3},{3,2},{4,5},{5,4},{6,7},{7,6},{8,9},{9,8},{10,11... | collective-permute-start | bytes 442376 | tf_op jit(solution)/shard_map/ppermute | solution.py:372
  53.3 1.7 %collective-permute-start.17 = (bf16[288,256]{1,0:T(8,128)(2,1)}, bf16[288,256]{1,0:T(8,128)(2,1)}, u32[]{:S(2)}, u32[]{:S(2)}) collective-permute-start(bf16[288,256]{1,0:T(8,128)(2,1)} %collective-permute-done.7.refs_8_), channel_id=1, source_target_pairs={{0,1},{1,0},{2,3},{3,2},{4,5},{5,4},{6,7},{7,6},{8,9},{9,8},{10,11... | collective-permute-start | bytes 442376 | tf_op jit(solution)/shard_map/ppermute | solution.py:372
  54.7 0.7 copy-start.12
  55.4 0.7 copy-start.13
  71.8 38.1 %copy-start.18 = (f32[128]{0:T(128)S(1)}, f32[128]{0:T(128)}, u32[]{:S(2)}) copy-start(f32[128]{0:T(128)} %param.24) | copy-start | bytes 1540
  71.8 11.4 %collective-permute-start.19 = (f32[128,256]{1,0:T(8,128)S(1)}, f32[128,256]{1,0:T(8,128)S(1)}, u32[]{:S(2)}, u32[]{:S(2)}) collective-permute-start(f32[128,256]{1,0:T(8,128)S(1)} %get-tuple-element.23), channel_id=1, source_target_pairs={{0,16},{16,0},{32,48},{48,32},{64,80},{80,64},{96,112},{112,96},{1... | collective-permute-start | bytes 393224 | tf_op jit(solution)/shard_map/ppermute | solution.py:441
  73.3 11.9 %collective-permute-start.25 = (f32[128,256]{1,0:T(8,128)S(1)}, f32[128,256]{1,0:T(8,128)S(1)}, u32[]{:S(2)}, u32[]{:S(2)}) collective-permute-start(f32[128,256]{1,0:T(8,128)S(1)} %get-tuple-element.24), channel_id=1, source_target_pairs={{0,80},{16,64},{32,112},{48,96},{64,16},{80,0},{96,48},{112,32},{1... | collective-permute-start | bytes 393224 | tf_op jit(solution)/shard_map/ppermute | solution.py:441
  78.8 9.3 %collective-permute-start.24 = (f32[128,256]{1,0:T(8,128)S(1)}, f32[128,256]{1,0:T(8,128)S(1)}, u32[]{:S(2)}, u32[]{:S(2)}) collective-permute-start(f32[128,256]{1,0:T(8,128)S(1)} %get-tuple-element.25), channel_id=1, source_target_pairs={{0,64},{16,80},{32,96},{48,112},{64,0},{80,16},{96,32},{112,48},{1... | collective-permute-start | bytes 393224 | tf_op jit(solution)/shard_map/ppermute | solution.py:441
  78.8 14.1 %collective-permute-start.23 = (f32[128,256]{1,0:T(8,128)S(1)}, f32[128,256]{1,0:T(8,128)S(1)}, u32[]{:S(2)}, u32[]{:S(2)}) collective-permute-start(f32[128,256]{1,0:T(8,128)S(1)} %get-tuple-element.26), channel_id=1, source_target_pairs={{0,112},{16,96},{32,16},{48,0},{64,48},{80,32},{96,80},{112,64},{1... | collective-permute-start | bytes 393224 | tf_op jit(solution)/shard_map/ppermute | solution.py:441
  83.2 9.6 %collective-permute-start.22 = (f32[128,256]{1,0:T(8,128)S(1)}, f32[128,256]{1,0:T(8,128)S(1)}, u32[]{:S(2)}, u32[]{:S(2)}) collective-permute-start(f32[128,256]{1,0:T(8,128)S(1)} %get-tuple-element.27), channel_id=1, source_target_pairs={{0,48},{16,32},{32,80},{48,64},{64,112},{80,96},{96,16},{112,0},{1... | collective-permute-start | bytes 393224 | tf_op jit(solution)/shard_map/ppermute | solution.py:441
  85.3 8.0 %collective-permute-start.21 = (f32[128,256]{1,0:T(8,128)S(1)}, f32[128,256]{1,0:T(8,128)S(1)}, u32[]{:S(2)}, u32[]{:S(2)}) collective-permute-start(f32[128,256]{1,0:T(8,128)S(1)} %get-tuple-element.28), channel_id=1, source_target_pairs={{0,96},{16,112},{32,0},{48,16},{64,32},{80,48},{96,64},{112,80},{1... | collective-permute-start | bytes 393224 | tf_op jit(solution)/shard_map/ppermute | solution.py:441
  88.1 6.8 %collective-permute-start.20 = (f32[128,256]{1,0:T(8,128)S(1)}, f32[128,256]{1,0:T(8,128)S(1)}, u32[]{:S(2)}, u32[]{:S(2)}) collective-permute-start(f32[128,256]{1,0:T(8,128)S(1)} %get-tuple-element.29), channel_id=1, source_target_pairs={{0,32},{16,48},{32,64},{48,80},{64,96},{80,112},{96,0},{112,16},{1... | collective-permute-start | bytes 393224 | tf_op jit(solution)/shard_map/ppermute | solution.py:441
  95.9 14.0 %collective-permute-start.26 = (f32[128,256]{1,0:T(8,128)S(1)}, f32[128,256]{1,0:T(8,128)S(1)}, u32[]{:S(2)}, u32[]{:S(2)}) collective-permute-start(f32[128,256]{1,0:T(8,128)S(1)} %fusion.11), channel_id=1, source_target_pairs={{0,1},{1,0},{2,3},{3,2},{4,5},{5,4},{6,7},{7,6},{8,9},{9,8},{10,11... | collective-permute-start | bytes 393224 | tf_op jit(solution)/shard_map/ppermute | solution.py:372
  109.9 2.7 %collective-permute-start.27 = (bf16[128,512]{1,0:T(8,128)(2,1)}, bf16[128,512]{1,0:T(8,128)(2,1)S(1)}, u32[]{:S(2)}, u32[]{:S(2)}) collective-permute-start(bf16[128,512]{1,0:T(8,128)(2,1)} %attn_cache.1.gq_ref), channel_id=1, source_target_pairs={{0,1},{1,0},{2,3},{3,2},{4,5},{5,4},{6,7},{7,6},{8,9},{9,8},{10,11... | collective-permute-start | bytes 393224 | tf_op jit(solution)/shard_map/ppermute | solution.py:372
  112.6 0.7 copy-start.17
  113.3 28.9 %copy-start.5 = (bf16[128,512]{1,0:T(8,128)(2,1)S(1)}, bf16[128,512]{1,0:T(8,128)(2,1)}, u32[]{:S(2)}) copy-start(bf16[128,512]{1,0:T(8,128)(2,1)} %param.13) | copy-start | bytes 393220
  113.3 28.9 %copy-start.6 = (bf16[128,512]{1,0:T(8,128)(2,1)S(1)}, bf16[128,512]{1,0:T(8,128)(2,1)}, u32[]{:S(2)}) copy-start(bf16[128,512]{1,0:T(8,128)(2,1)} %param.14) | copy-start | bytes 393220

commit v2 on v0

v2 whole, which is shorter than its diff:
```python
import functools
import math

import jax
import jax.numpy as jnp
from jax import lax
from jax.experimental import pallas as pl
from jax.experimental.pallas import tpu as pltpu
from jax.sharding import Mesh
from jax.sharding import PartitionSpec as P

D = 8192
KVH = 8
HD = 128
CACHE = 8192
TOKENS = 1024
CTX = 8
TOK = TOKENS // CTX
HEADS = 4
ROWS = 2 * HEADS * TOK
COLS = HEADS * HD
SIDE = HD // 2
CHIPS = 8
FEAT = D // 16
HALF_CACHE = CACHE // CTX // 2
HALF_WIN = TOK // 2
HALF = HALF_CACHE + HALF_WIN
CUT = HALF // 2
KB = 512
CHUNK = 512
CHUNKS = ROWS // CHUNK
EPS = 1e-06
SCALE = math.sqrt(HD)
EXP_SCALE = SCALE * math.log2(math.e)
NEG = -1e30
VMEM_LIMIT = 28 * 1024 * 1024
TP_AXES = ("xl", "y", "c")
CTX_AXES = ("z", "xh")
CHIP_AXES = ("xl", "y")


def contract_last(left, right):
    return lax.dot_general(
        left, right, (((1,), (1,)), ((), ())), preferred_element_type=jnp.float32
    )


def contract_first(left, right):
    return lax.dot_general(
        left, right, (((0,), (0,)), ((), ())), preferred_element_type=jnp.float32
    )


def unit_rows(values, qk_gain):
    width = values.shape[-1]
    mean_sq = jnp.mean(values * values, axis=-1, keepdims=True)
    return values * (lax.rsqrt(mean_sq + EPS) / math.sqrt(width)) * qk_gain


def unit_back(values, qk_gain, grad):
    width = values.shape[-1]
    mean_sq = jnp.mean(values * values, axis=-1, keepdims=True)
    factor = lax.rsqrt(mean_sq + EPS) / math.sqrt(width)
    weighted = qk_gain * grad
    inner = jnp.sum(weighted * values, axis=-1, keepdims=True)
    return factor * (weighted - values * inner / (width * (mean_sq + EPS)))


def head_cols(h):
    return slice(h * HD, (h + 1) * HD)


def head_rows(h):
    return slice(h * TOK, (h + 1) * TOK)


def pack_kernel(idx_ref, ck_ref, cv_ref, kr_ref, vw_ref, gain_ref, out_ref):
    gain = gain_ref[...]
    out_ref[:HALF_CACHE, :HD] = unit_rows(ck_ref[...].astype(jnp.float32), gain).astype(
        jnp.bfloat16
    )
    out_ref[:HALF_CACHE, HD:] = cv_ref[...]
    out_ref[HALF_CACHE:, :HD] = unit_rows(kr_ref[...].astype(jnp.float32), gain).astype(
        jnp.bfloat16
    )
    out_ref[HALF_CACHE:, HD:] = vw_ref[...]


def pack_rows(idx, cache_k, cache_v, k_raw, v_win, gain):
    def at(i, idx):
        return (idx[CORE], idx[CHIP])

    return pl.pallas_call(
        pack_kernel,
        out_shape=jax.ShapeDtypeStruct((HALF, 2 * HD), jnp.bfloat16),
        grid_spec=pltpu.PrefetchScalarGridSpec(
            num_scalar_prefetch=1,
            grid=(1,),
            in_specs=[
                pl.BlockSpec((HALF_CACHE, HD), at),
                pl.BlockSpec((HALF_CACHE, HD), at),
                pl.BlockSpec((HALF_WIN, HD), at),
                pl.BlockSpec((HALF_WIN, HD), at),
                pl.BlockSpec((1, HD), lambda i, idx: (0, 0)),
            ],
            out_specs=pl.BlockSpec((HALF, 2 * HD), lambda i, idx: (0, 0)),
        ),
        compiler_params=pltpu.CompilerParams(vmem_limit_bytes=8 * 1024 * 1024),
        name="pack_rows",
    )(idx, cache_k, cache_v, k_raw, v_win, gain)


def cost(flops, exps, moved):
    return pl.CostEstimate(
        flops=int(flops), transcendentals=int(exps), bytes_accessed=int(moved)
    )


def block_cost(blocks, dots):
    return cost(
        blocks * dots * 2 * ROWS * KB * HD, blocks * ROWS * KB, blocks * 4 * KB * HD + 2 ** 21
    )


HOPS = ((0, 0), (0, 1), (1, 0), (3, 0), (1, 1), (3, 1), (2, 0), (2, 1))
Z, XH, CHIP, CORE, FLOOR = range(5)


def source(info_ref, dz, dx):
    return lax.bitwise_and(info_ref[Z] + dz, 3) * 2 + lax.bitwise_and(info_ref[XH] + dx, 1)


def source_at(info_ref, n):
    dz = jnp.where(n >= 6, 2, jnp.where(n < 2, 0, jnp.where(lax.bitwise_and(n, 1) == 0, 1, 3)))
    dx = jnp.where(n >= 6, n - 6, jnp.where(n < 2, n, jnp.where(n >= 4, 1, 0)))
    return source(info_ref, dz, dx)


def cache_mask(info_ref, start):
    return start + lax.broadcasted_iota(jnp.int32, (CHUNK, KB), 1) >= info_ref[FLOOR]


def window_mask(info_ref):
    local = lax.broadcasted_iota(jnp.int32, (CHUNK, KB), 1)
    key = (
        lax.shift_right_logical(local, 6) * TOK
        + info_ref[CORE] * HALF_WIN
        + lax.bitwise_and(local, jnp.int32(HALF_WIN - 1))
    )
    token = source(info_ref, 0, 0) * TOK + lax.bitwise_and(
        lax.broadcasted_iota(jnp.int32, (CHUNK, KB), 0), jnp.int32(TOK - 1)
    )
    return key <= token


def chunk(r):
    return pl.ds(pl.multiple_of(r * CHUNK, CHUNK), CHUNK)


def keys_at(n):
    return pl.ds(pl.multiple_of(n * KB, KB), KB)


def place_cache(pieces, k_s, v_s, at=0):
    for n, group in enumerate(pieces):
        row = (at + n) * KB
        for piece in group:
            rows = min(piece.shape[0], (at + n + 1) * KB - row)
            k_s[row : row + rows, :] = piece[:rows, :HD]
            v_s[row : row + rows, :] = piece[:rows, HD:]
            row += rows


def stat_block(scores, dprobs, mask, rows, m_s, l_s, w_s):
    if mask is not None:
        scores = jnp.where(mask, scores, NEG)
    old = m_s[rows, :]
    top = old
    for g in range(KB // HD):
        top = jnp.maximum(top, scores[:, head_cols(g)])
    keep = jnp.exp2((old - top) * EXP_SCALE)
    total = l_s[rows, :] * keep
    weighted = w_s[rows, :] * keep
    for g in range(KB // HD):
        e = jnp.exp2((scores[:, head_cols(g)] - top) * EXP_SCALE)
        if mask is not None:
            e = jnp.where(mask[:, head_cols(g)], e, 0.0)
        total = total + e
        weighted = weighted + e * dprobs[:, head_cols(g)]
    m_s[rows, :] = top
    l_s[rows, :] = total
    w_s[rows, :] = weighted


def cache_loop(info_ref, first, count, core, body):
    @pl.loop(0, count * CHUNKS)
    def _(i):
        n = i // CHUNKS
        r = lax.rem(i, CHUNKS)
        start = source_at(info_ref, first + n) * (2 * KB) + core * KB

        @pl.when((start + KB > info_ref[FLOOR]) & (start < info_ref[FLOOR]))
        def _():
            body(n, r, start, True)

        @pl.when(start >= info_ref[FLOOR])
        def _():
            body(n, r, start, False)


def stats_kernel(first, groups, last, info_ref, *refs):
    refs = list(refs)
    flat = [refs.pop(0) for _ in range(sum(groups))]
    pieces = []
    for size in groups:
        pieces.append([flat.pop(0) for _ in range(size)])
    core = info_ref[CORE]
    if first == 0:
        q_ref, do_ref, pair_q_ref, pair_do_ref, gain_ref = refs[:5]
        q_s, do_s, m_s, l_s, w_s = refs[5:10]
        scratch = refs[10:]
        gain = gain_ref[...]
        for side, (raw_ref, grad_ref) in enumerate(((q_ref, do_ref), (pair_q_ref, pair_do_ref))):
            for h in range(HEADS):
                rows = slice((side * HEADS + h) * TOK, (side * HEADS + h + 1) * TOK)
                raw = raw_ref[:, head_cols(h)].astype(jnp.float32)
                q_s[rows, :] = unit_rows(raw, gain).astype(jnp.bfloat16)
                do_s[rows, :] = grad_ref[:, head_cols(h)]
        m_s[...] = jnp.full((ROWS, HD), NEG, jnp.float32)
        l_s[...] = jnp.zeros((ROWS, HD), jnp.float32)
        w_s[...] = jnp.zeros((ROWS, HD), jnp.float32)
    else:
        wins = []
        if last:
            wins = [refs.pop(0) for _ in range(CTX - 1)]
        q_s, do_s, m_in, l_in, w_in = refs[:5]
        if last:
            stat_ref, wk_ref, wv_ref = refs[5:8]
            m_s, l_s, w_s = refs[8:11]
            scratch = refs[11:]
        else:
            m_s, l_s, w_s = refs[5:8]
            scratch = refs[8:]
        m_s[...] = m_in[...]
        l_s[...] = l_in[...]
        w_s[...] = w_in[...]
    k_s, v_s = scratch
    place_cache(pieces, k_s, v_s)

    def body(n, r, start, masked):
        scores = contract_last(q_s[chunk(r), :], k_s[keys_at(n), :])
        dprobs = contract_last(do_s[chunk(r), :], v_s[keys_at(n), :])
        mask = cache_mask(info_ref, start) if masked else None
        stat_block(scores, dprobs, mask, chunk(r), m_s, l_s, w_s)

    cache_loop(info_ref, first, len(groups), core, body)
    if last:
        for n, piece in enumerate(wins + [pieces[-1][-1]]):
            at = pl.multiple_of(source(info_ref, *HOPS[n]) * HALF_WIN, HALF_WIN)
            low = piece.shape[0] - HALF_WIN
            wk_ref[pl.ds(at, HALF_WIN), :] = piece[low:, :HD]
            wv_ref[pl.ds(at, HALF_WIN), :] = piece[low:, HD:]

        @pl.loop(0, CHUNKS)
        def _(r):
            scores = contract_last(q_s[chunk(r), :], wk_ref[...])
            dprobs = contract_last(do_s[chunk(r), :], wv_ref[...])
            stat_block(scores, dprobs, window_mask(info_ref), chunk(r), m_s, l_s, w_s)

        top = jnp.max(m_s[...], axis=1, keepdims=True)
        fix = jnp.exp2((m_s[...] - top) * EXP_SCALE)
        total = jnp.sum(l_s[...] * fix, axis=1, keepdims=True)
        weighted = jnp.sum(w_s[...] * fix, axis=1, keepdims=True)
        lane = lax.broadcasted_iota(jnp.int32, (ROWS, HD), 1)
        stat_ref[...] = jnp.where(lane == 0, top, jnp.where(lane == 1, total, weighted))


SHAPE = jax.ShapeDtypeStruct
STATE = [SHAPE((ROWS, HD), jnp.float32)] * 3
VM = pl.BlockSpec(memory_space=pltpu.VMEM)
SM = pl.BlockSpec(memory_space=pltpu.SMEM)


def stats_call(first, info, groups, rest, last=False):
    pieces = [piece for group in groups for piece in group]
    if first == 0:
        out = [SHAPE((ROWS, HD), jnp.bfloat16)] * 2 + STATE
    elif last:
        out = [SHAPE((ROWS, HD), jnp.float32)] + [SHAPE((KB, HD), jnp.bfloat16)] * 2
    else:
        out = STATE
    keys = len(groups) * KB
    scratch = [pltpu.VMEM((keys, HD), jnp.bfloat16)] * 2
    if last:
        scratch = [pltpu.VMEM((ROWS, HD), jnp.float32)] * 3 + scratch
    return pl.pallas_call(
        functools.partial(stats_kernel, first, [len(group) for group in groups], last),
        out_shape=out,
        in_specs=[SM] + [VM] * (len(pieces) + len(rest)),
        out_specs=[VM] * len(out),
        scratch_shapes=scratch,
        compiler_params=pltpu.CompilerParams(vmem_limit_bytes=VMEM_LIMIT),
        cost_estimate=block_cost(len(groups) + (1 if last else 0), 2),
        name="stats_" + str(first),
    )(info, *pieces, *rest)


def grad_block(scores, dprobs, mask, lse, delta):
    probs = []
    dscores = []
    for g in range(KB // HD):
        p = jnp.exp2(scores[:, head_cols(g)] * EXP_SCALE - lse)
        if mask is not None:
            p = jnp.where(mask[:, head_cols(g)], p, 0.0)
        probs.append(p.astype(jnp.bfloat16))
        dscores.append((p * (dprobs[:, head_cols(g)] - delta)).astype(jnp.bfloat16))
    return jnp.concatenate(probs, 1), jnp.concatenate(dscores, 1)


def window_kernel(
    info_ref, mine_ref, pair_ref, q_s, do_s, wk_ref, wv_ref, lse_ref, delta_ref, dq_ref, *rest
):
    parts, dkv_ref = rest[:4], rest[4]
    mine = mine_ref[...]
    half = ROWS // 2
    pair = jnp.concatenate([pair_ref[half:, :], pair_ref[:half, :]], 0)
    top = jnp.maximum(mine[:, 0:1], pair[:, 0:1])
    fix = jnp.exp2((mine[:, 0:1] - top) * EXP_SCALE)
    pair_fix = jnp.exp2((pair[:, 0:1] - top) * EXP_SCALE)
    total = mine[:, 1:2] * fix + pair[:, 1:2] * pair_fix
    weighted = mine[:, 2:3] * fix + pair[:, 2:3] * pair_fix
    lse_ref[...] = jnp.broadcast_to(top * EXP_SCALE + jnp.log2(total), (ROWS, HD))
    delta_ref[...] = jnp.broadcast_to(weighted / total, (ROWS, HD))
    dkv_ref[...] = jnp.zeros((KB, 2 * HD), jnp.float32)

    @pl.loop(0, CHUNKS)
    def _(r):
        rows = chunk(r)
        query = q_s[rows, :]
        dout = do_s[rows, :]
        scores = contract_last(query, wk_ref[...])
        dprobs = contract_last(dout, wv_ref[...])
        probs, dscores = grad_block(
            scores, dprobs, window_mask(info_ref), lse_ref[rows, :], delta_ref[rows, :]
        )
        dq_ref[rows, :] = jnp.dot(dscores, wk_ref[...], preferred_element_type=jnp.float32)
        dkv_ref[:, :HD] += contract_first(dscores, query)
        dkv_ref[:, HD:] += contract_first(probs, dout)

    for dz in range(4):
        at = pl.multiple_of(lax.bitwise_and(info_ref[Z] + dz, 3) * TOK, TOK)
        parts[dz][...] = dkv_ref[pl.ds(at, TOK), :]


def window_call(info, mine, pair, query, dout, win_k, win_v):
    out = STATE + [SHAPE((TOK, 2 * HD), jnp.float32)] * 4
    return pl.pallas_call(
        window_kernel,
        out_shape=out,
        in_specs=[SM] + [VM] * 6,
        out_specs=[VM] * 7,
        scratch_shapes=[pltpu.VMEM((KB, 2 * HD), jnp.float32)],
        compiler_params=pltpu.CompilerParams(vmem_limit_bytes=VMEM_LIMIT),
        cost_estimate=block_cost(1, 5),
        name="window_grads",
    )(info, mine, pair, query, dout, win_k, win_v)


def cache_kernel(first, groups, info_ref, *refs):
    refs = list(refs)
    pieces = []
    for size in groups:
        pieces.append([refs.pop(0) for _ in range(size)])
    q_s, do_s, lse_ref, delta_ref, dq_in, dq_ref, k_s, v_s = refs
    place_cache(pieces, k_s, v_s)
    dq_ref[...] = dq_in[...]

    def body(n, r, start, masked):
        rows = chunk(r)
        keys = k_s[keys_at(n), :]
        scores = contract_last(q_s[rows, :], keys)
        dprobs = contract_last(do_s[rows, :], v_s[keys_at(n), :])
        mask = cache_mask(info_ref, start) if masked else None
        _, dscores = grad_block(scores, dprobs, mask, lse_ref[rows, :], delta_ref[rows, :])
        dq_ref[rows, :] += jnp.dot(dscores, keys, preferred_element_type=jnp.float32)

    cache_loop(info_ref, first, len(groups), info_ref[CORE], body)


def cache_call(first, info, groups, query, dout, lse, delta, dq):
    pieces = [piece for group in groups for piece in group]
    return pl.pallas_call(
        functools.partial(cache_kernel, first, [len(group) for group in groups]),
        out_shape=STATE[0],
        in_specs=[SM] + [VM] * (len(pieces) + 5),
        out_specs=VM,
        scratch_shapes=[pltpu.VMEM((len(groups) * KB, HD), jnp.bfloat16)] * 2,
        compiler_params=pltpu.CompilerParams(vmem_limit_bytes=VMEM_LIMIT),
        cost_estimate=block_cost(len(groups), 3),
        name="cache_grads_" + str(first),
    )(info, *pieces, query, dout, lse, delta, dq)


SMALL = pltpu.CompilerParams(vmem_limit_bytes=8 * 1024 * 1024)


def sum_kernel(info_ref, a_ref, b_ref, c_ref, d_ref, keep_ref, send_ref):
    total = (a_ref[...] + b_ref[...]) + (c_ref[...] + d_ref[...])
    first = info_ref[XH] == 0
    keep_ref[...] = jnp.where(first, total[:HALF_WIN, :], total[HALF_WIN:, :])
    send_ref[...] = jnp.where(first, total[HALF_WIN:, :], total[:HALF_WIN, :])


def sum_parts(info, parts):
    return pl.pallas_call(
        sum_kernel,
        out_shape=[SHAPE((HALF_WIN, 2 * HD), jnp.float32)] * 2,
        in_specs=[SM] + [VM] * 4,
        out_specs=[VM] * 2,
        compiler_params=SMALL,
        name="sum_parts",
    )(info, *parts)


def own_kv_kernel(idx_ref, keep_ref, other_ref, raw_ref, gain_ref, out_ref):
    total = keep_ref[...] + other_ref[...]
    raw = raw_ref[...].astype(jnp.float32)
    out_ref[:, :HD] = unit_back(raw, gain_ref[...], total[:, :HD] * SCALE).astype(jnp.bfloat16)
    out_ref[:, HD:] = total[:, HD:].astype(jnp.bfloat16)


def own_kv(idx, keep, other, k_raw, gain):
    def whole(i, idx):
        return (0, 0)

    return pl.pallas_call(
        own_kv_kernel,
        out_shape=SHAPE((HALF_WIN, 2 * HD), jnp.bfloat16),
        grid_spec=pltpu.PrefetchScalarGridSpec(
            num_scalar_prefetch=1,
            grid=(1,),
            in_specs=[
                pl.BlockSpec((HALF_WIN, 2 * HD), whole),
                pl.BlockSpec((HALF_WIN, 2 * HD), whole),
                pl.BlockSpec((HALF_WIN, HD), lambda i, idx: (idx[CORE], idx[CHIP])),
                pl.BlockSpec((1, HD), whole),
            ],
            out_specs=pl.BlockSpec((HALF_WIN, 2 * HD), whole),
        ),
        compiler_params=SMALL,
        name="own_kv",
    )(idx, keep, other, k_raw, gain)


def project_kernel(
    idx_ref,
    dq_ref,
    pair_dq_ref,
    q_ref,
    pair_q_ref,
    gain_ref,
    kv_ref,
    pair_kv_ref,
    wq_ref,
    wk_ref,
    wv_ref,
    pair_wq_ref,
    pair_wk_ref,
    pair_wv_ref,
    out_ref,
    g_s,
):
    core = idx_ref[CORE]
    gain = gain_ref[...]
    for h in range(HEADS):
        rows = head_rows(h)
        low = slice(ROWS // 2 + h * TOK, ROWS // 2 + (h + 1) * TOK)
        for side, raw_ref, grad in (
            (0, q_ref, dq_ref[rows, :] + pair_dq_ref[low, :]),
            (1, pair_q_ref, dq_ref[low, :] + pair_dq_ref[rows, :]),
        ):
            raw = raw_ref[:, head_cols(h)].astype(jnp.float32)
            at = side * COLS + h * HD
            g_s[at : at + HD, :] = unit_back(raw, gain, grad * SCALE).T.astype(jnp.bfloat16)
    here = kv_ref[...].astype(jnp.float32)
    there = pair_kv_ref[...].astype(jnp.float32)
    top = jnp.where(core == 0, here, there)
    bottom = jnp.where(core == 0, there, here)
    kv = jnp.concatenate([top, bottom], 0)
    for n in range(2):
        both = kv[:, n * HD : (n + 1) * HD].T.astype(jnp.bfloat16)
        first = jnp.where(core == 0, both[:SIDE, :], both[SIDE:, :])
        second = jnp.where(core == 0, both[SIDE:, :], both[:SIDE, :])
        g_s[2 * COLS + n * SIDE : 2 * COLS + (n + 1) * SIDE, :] = first
        g_s[2 * COLS + (2 + n) * SIDE : 2 * COLS + (3 + n) * SIDE, :] = second

    @pl.loop(0, CHIPS)
    def _(j):
        rows = pl.ds(pl.multiple_of((2 * j + core) * FEAT, FEAT), FEAT)
        total = jnp.dot(wq_ref[rows, :], g_s[:COLS, :], preferred_element_type=jnp.float32)
        total += jnp.dot(
            pair_wq_ref[rows, :], g_s[COLS : 2 * COLS, :], preferred_element_type=jnp.float32
        )
        narrow = jnp.concatenate(
            [wk_ref[:, rows], wv_ref[:, rows], pair_wk_ref[:, rows], pair_wv_ref[:, rows]], 0
        )
        total += contract_first(narrow, g_s[2 * COLS :, :])
        out_ref[j] = total.astype(jnp.bfloat16)


def project(idx, dq, pair_dq, q_raw, pair_q, gain, kv, pair_kv, weights, pair_weights):
    return pl.pallas_call(
        project_kernel,
        out_shape=jax.ShapeDtypeStruct((CHIPS, FEAT, TOK), jnp.bfloat16),
        in_specs=[SM] + [VM] * 13,
        out_specs=VM,
        scratch_shapes=[pltpu.VMEM((2 * COLS + 2 * HD, TOK), jnp.bfloat16)],
        compiler_params=pltpu.CompilerParams(vmem_limit_bytes=VMEM_LIMIT),
        cost_estimate=cost(2 * TOK * D // 2 * 1280, 0, 3e6),
        name="project",
    )(idx, dq, pair_dq, q_raw, pair_q, gain, kv, pair_kv, *weights, *pair_weights)


def shift(block, axis, by):
    count = lax.axis_size(axis)
    return lax.ppermute(block, axis, [(i, (i + by) % count) for i in range(count)])


def swap(block, axis):
    return shift(block, axis, 1)


def on_device(
    residual_in,
    dh_rest,
    w_query,
    w_key,
    w_value,
    q_raw,
    k_raw,
    v_win,
    cache_k,
    cache_v,
    d_attn,
    s_qk,
    cache_live,
):
    info = jnp.stack(
        [
            lax.axis_index("z"),
            lax.axis_index("xh"),
            lax.axis_index("xl") * 4 + lax.axis_index("y"),
            lax.axis_index("c"),
            CACHE - cache_live[0],
        ]
    ).astype(jnp.int32)
    gain = s_qk.reshape(1, HD)

    here = pack_rows(info, cache_k, cache_v, k_raw, v_win, gain)
    there = swap(here, "xh")
    up = shift(here, "z", -1)
    down = shift(here, "z", 1)
    pair_q = swap(q_raw, "c")
    pair_do = swap(d_attn, "c")
    up_there = shift(there, "z", -1)
    down_there = shift(there, "z", 1)
    far = [shift(up[:CUT], "z", -1), shift(down[CUT:], "z", 1)]
    groups = [[here], [there], [up], [down]]
    weights = (w_query, w_key.T, w_value.T)
    pair_weights = [swap(w, "c") for w in weights]

    query, dout, *state = stats_call(
        0, info, groups[:4], [q_raw, d_attn, pair_q, pair_do, gain]
    )
    query, dout, state, up_there, down_there = lax.optimization_barrier(
        (query, dout, state, up_there, down_there)
    )
    far_there = [shift(up_there[:CUT], "z", -1), shift(down_there[CUT:], "z", 1)]
    groups += [[up_there], [down_there], far, far_there]
    state = stats_call(4, info, groups[4:7], [query, dout, *state])
    wins = [group[-1] for group in groups[:-1]]
    stat, win_k, win_v = stats_call(
        7, info, groups[7:], wins + [query, dout, *state], last=True
    )
    lse, delta, dq, *parts = window_call(
        info, stat, swap(stat, "c"), query, dout, win_k, win_v
    )
    parts = [parts[0]] + [shift(parts[dz], "z", dz) for dz in (1, 3, 2)]
    dq = cache_call(0, info, groups[:4], query, dout, lse, delta, dq)
    parts, dq = lax.optimization_barrier((parts, dq))
    keep, send = sum_parts(info, parts)
    other = swap(send, "xh")
    dq = cache_call(4, info, groups[4:], query, dout, lse, delta, dq)
    other, dq = lax.optimization_barrier((other, dq))
    pair_dq = swap(dq, "c")
    kv = own_kv(info, keep, other, k_raw, gain)
    pair_kv = swap(kv, "c")
    partial = project(
        info, dq, pair_dq, q_raw, pair_q, gain, kv, pair_kv, weights, pair_weights
    )
    pieces = lax.all_to_all(partial, CHIP_AXES, 0, 0)
    grad_total = jnp.sum(pieces.astype(jnp.float32), axis=0).T + dh_rest.astype(jnp.float32)
    resid = residual_in.astype(jnp.float32)
    sums = jnp.stack([jnp.sum(resid * resid, axis=1), jnp.sum(grad_total * resid, axis=1)])
    everyone = lax.all_to_all(
        jnp.broadcast_to(sums[None], (16, 2, TOK)), TP_AXES, 0, 0
    )
    square_sum, inner_sum = jnp.sum(everyone, axis=0)
    mean_sq = square_sum / D
    factor = lax.rsqrt(mean_sq + EPS) / math.sqrt(D)
    correction = inner_sum / (D * (mean_sq + EPS))
    return factor[:, None] * (grad_total - resid * correction[:, None])


def solution(mesh):
    fine = Mesh(mesh.devices.reshape(4, 2, 2, 4, 2), ("z", "xh", "xl", "y", "c"))
    both = P(CTX_AXES, TP_AXES)
    cols = P(None, TP_AXES)
    rows = P(CTX_AXES, None)
    return jax.shard_map(
        on_device,
        mesh=fine,
        in_specs=(both, both, cols, cols, cols, both, rows, rows, rows, rows, both, P(), P()),
        out_specs=both,
        check_vma=False,
    )
```

time: 379 us -> 116 us (0.31)
  matrix products: 108 us -> 0 us
  waiting for transfers between devices: 94.8 us -> 25.6 us
  other arithmetic: 62 us -> 0.34 us
  blocking collectives: 63.5 us -> 10 us
  Pallas kernels: 0 us -> 38.5 us
  starting transfers between devices: 1.47 us -> 33.2 us
  local copies, waits for them, and re-layouts: 31.5 us -> 6.99 us
  between operations: 14.2 us -> 0.91 us
    dot_general x42 -> x0, matrix products: 108 us -> none  [the longest x31 75.3 us: contract_last(): lax.dot_general(left, right, (((1,), (1,)), ((), ())), preferred_element_...]
    reduce_scatter x2 -> x0, waiting for transfers between devices: 60.4 us -> none  [the longest x1 60.3 us: on_device(): lax.psum_scatter(contract_last(w_query, grad_q) + contract_last(w_key, gr...]
    pallas_call x0 -> x10, Pallas kernels: none -> 38.5 us  [the longest x3 12.3 us: stats_call(): pl.pallas_call(functools.partial(stats_kernel, first, [len(group) for gro...]
    all_gather x1 -> x0, waiting for transfers between devices: 34.4 us -> none  [on_device(): lax.all_gather(jnp.concatenate([unit_rows(raw_keys, s_qk).astype(jnp.bflo...]
    all_gather x1 -> x0, blocking collectives: 32.4 us -> none  [on_device(): all_window = lax.all_gather(window_pack, 'ctx', axis=0, tiled=True)]
    psum x1 -> x0, blocking collectives: 31 us -> none  [on_device(): lax.psum((jnp.sum(resid * resid, axis=1), jnp.sum(grad_total * resid, axi...]
    ppermute x1 -> x21, starting transfers between devices: 1.39 us -> 28.9 us  [shift(): lax.ppermute(block, axis, [(i, (i + by) % count) for i in range(count)])]
    reduce_sum x13 -> x2, other arithmetic: 22.2 us -> 0.17 us  [the longest x1 0.15 us: on_device(): jnp.sum(pieces.astype(jnp.float32), axis=0).T + dh_rest.astype(jnp.float32)]
  transfers between devices with their start and end apart: 4 -> 22, of which waited for: 2 -> 8; matrix products, arithmetic and copies ran while one was open for 25% -> 0% of each run, Pallas kernels for 0% -> 25%
where the time goes in v2:
time: 116 us
  Pallas kernels  38.5 us (33%)
  starting transfers between devices  33.2 us (29%)
  waiting for transfers between devices  25.6 us (22%)
  blocking collectives  10 us (9%)
  local copies, waits for them, and re-layouts  6.99 us (6%)
    ppermute x21, starting transfers between devices, shift(): lax.ppermute(block, axis, [(i, (i + by) % count) for i in range(count)])  28.9 us
    all_to_all x1, waiting for transfers between devices, on_device(): pieces = lax.all_to_all(partial, CHIP_AXES, 0, 0)  14.7 us
    pallas_call x3, Pallas kernels, stats_call(): pl.pallas_call(functools.partial(stats_kernel, first, [len(group) for gro...  12.3 us
    pallas_call x2, Pallas kernels, cache_call(): pl.pallas_call(functools.partial(cache_kernel, first, [len(group) for gro...  11.4 us
    ppermute x21, waiting for transfers between devices, shift(): lax.ppermute(block, axis, [(i, (i + by) % count) for i in range(count)])  10.9 us
    all_to_all x1, blocking collectives, on_device(): lax.all_to_all(jnp.broadcast_to(sums[None], (16, 2, TOK)), TP_AXES, 0, 0)  10 us
    pallas_call x1, Pallas kernels, project(): pl.pallas_call(project_kernel, out_shape=jax.ShapeDtypeStruct((CHIPS, FEA...  9.05 us
    unnamed x32, local copies, waits for them, and re-layouts  6.01 us
  transfers between devices with their start and end apart: 22, of which 8 were waited for; matrix products, arithmetic and copies ran while one was open for 0% of the time, Pallas kernels for 25%

profile of v2, /device:TPU:1, one launch (start us, length us, event | category | flops | bytes accessed | tf_op | source)
XLA Modules:
  0.0 115.6 jit_solution(1969263614525961001)
XLA Ops:
  0.0 1.4 %collective-permute-start.18 = (bf16[8192,512]{1,0:T(8,128)(2,1)}, bf16[8192,512]{1,0:T(8,128)(2,1)}, u32[]{:S(2)}, u32[]{:S(2)}) collective-permute-start(bf16[8192,512]{1,0:T(8,128)(2,1)} %wq_ref.1), channel_id=1, source_target_pairs={{0,1},{1,0},{2,3},{3,2},{4,5},{5,4},{6,7},{7,6},{8,9},{9,8},{10,11... | collective-permute-start | bytes 25165832 | tf_op jit(solution)/shard_map/ppermute | solution.py:526
  2.1 0.1 stack.30.idx_ref.info_ref
  2.2 1.6 %copy-done = bf16[1024,1024]{1,0:T(8,128)(2,1)S(1)} copy-done((bf16[1024,1024]{1,0:T(8,128)(2,1)S(1)}, bf16[1024,1024]{1,0:T(8,128)(2,1)}, u32[]{:S(2)}) %copy-start) | copy-done | bytes 2097176
  3.8 1.6 %copy-done.1 = bf16[1024,1024]{1,0:T(8,128)(2,1)S(1)} copy-done((bf16[1024,1024]{1,0:T(8,128)(2,1)S(1)}, bf16[1024,1024]{1,0:T(8,128)(2,1)}, u32[]{:S(2)}) %copy-start.1) | copy-done | bytes 2097176
  5.3 0.9 copy-done.4
  6.3 0.9 copy-done.6
  7.2 0.7 copy-done.8
  7.9 0.8 pack_rows.1.refs_0_.refs_2_
  8.7 2.9 %collective-permute-start = (bf16[576,256]{1,0:T(8,128)(2,1)S(1)}, bf16[576,256]{1,0:T(8,128)(2,1)S(1)}, u32[]{:S(2)}, u32[]{:S(2)}) collective-permute-start(bf16[576,256]{1,0:T(8,128)(2,1)S(1)} %pack_rows.1.refs_0_.refs_2_), channel_id=1, source_target_pairs={{0,16},{16,0},{1,17},{17,1},{2,18},{18,2},{3,19},{19,3},{4,20},{20... | collective-permute-start | bytes 884744 | tf_op jit(solution)/shard_map/ppermute | solution.py:526
  11.6 3.8 %collective-permute-start.1 = (bf16[576,256]{1,0:T(8,128)(2,1)S(1)}, bf16[576,256]{1,0:T(8,128)(2,1)S(1)}, u32[]{:S(2)}, u32[]{:S(2)}) collective-permute-start(bf16[576,256]{1,0:T(8,128)(2,1)S(1)} %pack_rows.1.refs_0_.refs_2_), channel_id=1, source_target_pairs={{0,96},{32,0},{64,32},{96,64},{1,97},{33,1},{65,33},{97,65},{2,98}... | collective-permute-start | bytes 884744 | tf_op jit(solution)/shard_map/ppermute | solution.py:526
  15.3 0.0 collective-permute-start.2
  15.3 3.6 %collective-permute-done.refs_1_.refs_3_ = bf16[576,256]{1,0:T(8,128)(2,1)S(1)} collective-permute-done((bf16[576,256]{1,0:T(8,128)(2,1)S(1)}, bf16[576,256]{1,0:T(8,128)(2,1)S(1)}, u32[]{:S(2)}, u32[]{:S(2)}) %collective-permute-start) | collective-permute-done | bytes 294944 | tf_op jit(solution)/shard_map/ppermute | solution.py:526
  18.9 3.8 %collective-permute-start.5 = (bf16[576,256]{1,0:T(8,128)(2,1)S(1)}, bf16[576,256]{1,0:T(8,128)(2,1)S(1)}, u32[]{:S(2)}, u32[]{:S(2)}) collective-permute-start(bf16[576,256]{1,0:T(8,128)(2,1)S(1)} %collective-permute-done.refs_1_.refs_3_), channel_id=1, source_target_pairs={{0,96},{32,0},{64,32},{96,64},{1,97},{33,1},{65,33},{97,65},{2,98}... | collective-permute-start | bytes 884744 | tf_op jit(solution)/shard_map/ppermute | solution.py:526
  22.7 0.0 collective-permute-start.6
  22.7 0.0 collective-permute-done.1.refs_2_.refs_4_
  22.7 1.1 collective-permute-start.3
  23.9 0.7 collective-permute-done.2.refs_3_.refs_5_
  24.6 1.4 %collective-permute-start.4 = (bf16[128,512]{1,0:T(8,128)(2,1)S(1)}, bf16[128,512]{1,0:T(8,128)(2,1)S(1)}, u32[]{:S(2)}, u32[]{:S(2)}) collective-permute-start(bf16[128,512]{1,0:T(8,128)(2,1)S(1)} %copy-done.10), channel_id=1, source_target_pairs={{0,1},{1,0},{2,3},{3,2},{4,5},{5,4},{6,7},{7,6},{8,9},{9,8},{10,11... | collective-permute-start | bytes 393224 | tf_op jit(solution)/shard_map/ppermute | solution.py:526
  26.0 0.0 collective-permute-done.3.refs_6_.pair_q_ref
  26.0 0.1 collective-permute-start.9
  26.1 0.9 collective-permute-done.4.refs_7_
  27.0 1.8 %collective-permute-start.10 = (bf16[288,256]{1,0:T(8,128)(2,1)S(1)}, bf16[288,256]{1,0:T(8,128)(2,1)S(1)}, u32[]{:S(2)}, u32[]{:S(2)}) collective-permute-start(bf16[288,256]{1,0:T(8,128)(2,1)S(1)} %slice.17), channel_id=1, source_target_pairs={{0,96},{32,0},{64,32},{96,64},{1,97},{33,1},{65,33},{97,65},{2,98}... | collective-permute-start | bytes 442376 | tf_op jit(solution)/shard_map/ppermute | solution.py:526
  28.8 5.1 %stats_0.1 = (bf16[1024,128]{1,0:T(8,128)(2,1)S(1)}, bf16[1024,128]{1,0:T(8,128)(2,1)S(1)}, f32[1024,128]{1,0:T(8,128)S(1)}, f32[1024,128]{1,0:T(8,128)S(1)}, f32[1024,128]{1,0:T(8,128)S(1)}) custom-call(s32[5]{0:T(128)S(1)} %stack.30.idx_ref.info_ref, bf16[576,256]{1,0:T(8,128)(2,1)S(1)} %pack_rows.1.refs_0_.refs_2_, ...), custom_call_target="tpu_custom_call" | custom-call | flops 1073741824 | bytes 3145728 | tf_op jit(solution)/shard_map/stats_0/pallas_call | solution.py:296
  33.9 0.0 collective-permute-done.5.refs_0_.refs_6_
  33.9 0.0 collective-permute-done.6.refs_1_.refs_7_
  33.9 0.5 collective-permute-start.7
  34.5 1.1 collective-permute-start.8
  35.6 0.0 collective-permute-done.9.refs_3_.refs_8_
  35.6 3.8 %stats_4.1 = (f32[1024,128]{1,0:T(8,128)S(1)}, f32[1024,128]{1,0:T(8,128)S(1)}, f32[1024,128]{1,0:T(8,128)S(1)}) custom-call(s32[5]{0:T(128)S(1)} %stack.30.idx_ref.info_ref, bf16[576,256]{1,0:T(8,128)(2,1)S(1)} %collective-permute-done.5.refs_0_.refs_6_, bf16[576,256]{1,0:T(8,128)(2,1)S(1)} %collective-permute-done.6.refs_1_.refs_7_, ...), custom_call_target="tpu_custom_call" | custom-call | flops 805306368 | bytes 2883584 | tf_op jit(solution)/shard_map/stats_4/pallas_call | solution.py:296
  39.4 0.3 collective-permute-done.8.refs_1_.refs_5_
  39.8 3.4 %stats_7.1 = (f32[1024,128]{1,0:T(8,128)S(1)}, bf16[512,128]{1,0:T(8,128)(2,1)S(1)}, bf16[512,128]{1,0:T(8,128)(2,1)S(1)}) custom-call(s32[5]{0:T(128)S(1)} %stack.30.idx_ref.info_ref, bf16[288,256]{1,0:T(8,128)(2,1)S(1)} %collective-permute-done.7.refs_0_.refs_4_, bf16[288,256]{1,0:T(8,128)(2,1)S(1)} %collective-permute-done.8.refs_1_.refs_5_, ...), custom_call_target="tpu_custom_call" | custom-call | flops 536870912 | bytes 2621440 | tf_op jit(solution)/shard_map/stats_7/pallas_call | solution.py:296
  43.2 2.6 %collective-permute-start.11 = (f32[1024,128]{1,0:T(8,128)S(1)}, f32[1024,128]{1,0:T(8,128)S(1)}, u32[]{:S(2)}, u32[]{:S(2)}) collective-permute-start(f32[1024,128]{1,0:T(8,128)S(1)} %get-tuple-element.54.mine_ref), channel_id=1, source_target_pairs={{0,1},{1,0},{2,3},{3,2},{4,5},{5,4},{6,7},{7,6},{8,9},{9,8},{10,11... | collective-permute-start | bytes 1572872 | tf_op jit(solution)/shard_map/ppermute | solution.py:526
  45.7 0.1 collective-permute-start.19
  45.8 0.4 collective-permute-start.20
  46.2 1.0 collective-permute-done.11.pair_ref
  47.3 3.7 %window_grads.1 = (f32[1024,128]{1,0:T(8,128)S(1)}, f32[1024,128]{1,0:T(8,128)S(1)}, f32[1024,128]{1,0:T(8,128)S(1)}, f32[128,256]{1,0:T(8,128)S(1)}, f32[128,25...) custom-call(s32[5]{0:T(128)S(1)} %stack.30.idx_ref.info_ref, ...), custom_call_target="tpu_custom_call" | custom-call | flops 671088640 | bytes 2359296 | tf_op jit(solution)/shard_map/window_grads/pallas_call | solution.py:357
  51.0 0.1 collective-permute-start.12
  51.1 2.7 %collective-permute-start.13 = (f32[128,256]{1,0:T(8,128)S(1)}, f32[128,256]{1,0:T(8,128)S(1)}, u32[]{:S(2)}, u32[]{:S(2)}) collective-permute-start(f32[128,256]{1,0:T(8,128)S(1)} %get-tuple-element.59), channel_id=1, source_target_pairs={{0,96},{32,0},{64,32},{96,64},{1,97},{33,1},{65,33},{97,65},{2,98}... | collective-permute-start | bytes 393224 | tf_op jit(solution)/shard_map/ppermute | solution.py:526
  53.7 3.2 %collective-permute-done.12.b_ref = f32[128,256]{1,0:T(8,128)S(1)} collective-permute-done((f32[128,256]{1,0:T(8,128)S(1)}, f32[128,256]{1,0:T(8,128)S(1)}, u32[]{:S(2)}, u32[]{:S(2)}) %collective-permute-start.12) | collective-permute-done | bytes 131104 | tf_op jit(solution)/shard_map/ppermute | solution.py:526
  57.0 0.0 collective-permute-start.14
  57.0 5.7 %cache_grads_0.1.refs_10_ = f32[1024,128]{1,0:T(8,128)S(1)} custom-call(s32[5]{0:T(128)S(1)} %stack.30.idx_ref.info_ref, bf16[576,256]{1,0:T(8,128)(2,1)S(1)} %pack_rows.1.refs_0_.refs_2_, bf16[576,256]{1,0:T(8,128)(2,1)S(1)} %collective-permute-done.refs_1_.refs_3_, bf16[576,256]{1,0:T(8,128)(2,1)S(1)} %collective-permute-done.1.refs_2_.refs_4_, ...), custom_call_target="tpu_custom_call" | custom-call | flops 1610612736 | bytes 3145728 | tf_op jit(solution)/shard_map/cache_grads_0/pallas_call | solution.py:392
  62.7 0.0 collective-permute-done.13.c_ref
  62.7 0.0 collective-permute-done.14.d_ref
  62.7 0.6 sum_parts.1
  63.3 0.0 copy-start.5
  63.3 2.7 %collective-permute-start.15 = (f32[64,256]{1,0:T(8,128)S(1)}, f32[64,256]{1,0:T(8,128)S(1)}, u32[]{:S(2)}, u32[]{:S(2)}) collective-permute-start(f32[64,256]{1,0:T(8,128)S(1)} %get-tuple-element.68), channel_id=1, source_target_pairs={{0,16},{16,0},{1,17},{17,1},{2,18},{18,2},{3,19},{19,3},{4,20},{20... | collective-permute-start | bytes 196616 | tf_op jit(solution)/shard_map/ppermute | solution.py:526
  66.0 5.7 %cache_grads_4.1.dq_ref = f32[1024,128]{1,0:T(8,128)S(1)} custom-call(s32[5]{0:T(128)S(1)} %stack.30.idx_ref.info_ref, bf16[576,256]{1,0:T(8,128)(2,1)S(1)} %collective-permute-done.5.refs_0_.refs_6_, bf16[576,256]{1,0:T(8,128)(2,1)S(1)} %collective-permute-done.6.refs_1_.refs_7_, bf16[288,256]{1,0:T(8,128)(2,1)S(1)} %collective-permute-done.10.refs_2_, ...), custom_call_target="tpu_custom_call" | custom-call | flops 1610612736 | bytes 3145728 | tf_op jit(solution)/shard_map/cache_grads_4/pallas_call | solution.py:392
  71.7 0.0 collective-permute-done.15.other_ref
  71.7 2.3 %collective-permute-start.16 = (f32[1024,128]{1,0:T(8,128)S(1)}, f32[1024,128]{1,0:T(8,128)S(1)}, u32[]{:S(2)}, u32[]{:S(2)}) collective-permute-start(f32[1024,128]{1,0:T(8,128)S(1)} %cache_grads_4.1.dq_ref), channel_id=1, source_target_pairs={{0,1},{1,0},{2,3},{3,2},{4,5},{5,4},{6,7},{7,6},{8,9},{9,8},{10,11... | collective-permute-start | bytes 1572872 | tf_op jit(solution)/shard_map/ppermute | solution.py:526
  74.0 0.6 own_kv.1.kv_ref
  74.7 0.1 collective-permute-start.17
  74.8 1.2 %collective-permute-done.17.pair_kv_ref = bf16[64,256]{1,0:T(8,128)(2,1)S(1)} collective-permute-done((bf16[64,256]{1,0:T(8,128)(2,1)S(1)}, bf16[64,256]{1,0:T(8,128)(2,1)S(1)}, u32[]{:S(2)}, u32[]{:S(2)}) %collective-permute-start.17) | collective-permute-done | bytes 32800 | tf_op jit(solution)/shard_map/ppermute | solution.py:526
  76.0 0.0 collective-permute-done.16.pair_dq_ref
  76.0 0.0 collective-permute-done.18.pair_wq_ref
  76.0 9.1 %project.1 = bf16[8,512,128]{2,1,0:T(8,128)(2,1)} custom-call(s32[5]{0:T(128)S(1)} %stack.30.idx_ref.info_ref, f32[1024,128]{1,0:T(8,128)S(1)} %cache_grads_4.1.dq_ref, f32[1024,128]{1,0:T(8,128)S(1)} %collective-permute-done.16.pair_dq_ref, bf16[128,512]{1,0:T(8,128)(2,1)S(1)} %copy-done.7, bf16[128,512]{1,0:T(8,128)(2,1)S(1)} %collective-permute-done.3.refs_6_.pair_q_ref, ...), custom_call_target="tpu_custom_call" | custom-call | flops 1342177280 | bytes 3000000 | tf_op jit(solution)/shard_map/project/pallas_call | solution.py:512
  85.1 4.3 %all-to-all-start = ((bf16[8,512,128]{2,1,0:T(8,128)(2,1)}), bf16[8,512,128]{2,1,0:T(8,128)(2,1)S(1)}, u32[]{:S(2)}, u32[]{:S(2)}) async-start(bf16[8,512,128]{2,1,0:T(8,128)(2,1)} %project.1), calls=%async_computation | async-start | bytes 2097152 | tf_op jit(solution)/shard_map/all_to_all | solution.py:601
  89.4 0.1 copy.20
  89.5 0.1 copy.21
  89.7 14.7 %all-to-all-done = bf16[8,512,128]{2,1,0:T(8,128)(2,1)S(1)} async-done(((bf16[8,512,128]{2,1,0:T(8,128)(2,1)}), bf16[8,512,128]{2,1,0:T(8,128)(2,1)S(1)}, u32[]{:S(2)}, u32[]{:S(2)}) %all-to-all-start) | async-done | bytes 1048608 | tf_op jit(solution)/shard_map/all_to_all | solution.py:601
  104.4 0.1 convert_reduce_fusion
  104.5 0.1 fusion
  104.6 10.0 %all_to_all.10 = f32[16,2,128]{2,1,0:T(2,128)S(1)} all-to-all(f32[16,2,128]{2,1,0:T(2,128)S(1)} %broadcast_in_dim.2), channel_id=1, replica_groups=mesh['z'=4,'xh'=2,'xl'=2,'y'=4,'c'=2] {'xl','y','c'}, dimensions={0} | all-to-all | bytes 32768 | tf_op jit(solution)/shard_map/all_to_all | solution.py:605
  114.7 0.1 fusion.3
  114.7 0.8 copy.23
  (37 shorter events, 0.2 us)
Async XLA Ops:
  0.0 76.0 %collective-permute-start.18 = (bf16[8192,512]{1,0:T(8,128)(2,1)}, bf16[8192,512]{1,0:T(8,128)(2,1)}, u32[]{:S(2)}, u32[]{:S(2)}) collective-permute-start(bf16[8192,512]{1,0:T(8,128)(2,1)} %wq_ref.1), channel_id=1, source_target_pairs={{0,1},{1,0},{2,3},{3,2},{4,5},{5,4},{6,7},{7,6},{8,9},{9,8},{10,11... | collective-permute-start | bytes 25165832 | tf_op jit(solution)/shard_map/ppermute | solution.py:526
  2.2 1.6 %copy-start = (bf16[1024,1024]{1,0:T(8,128)(2,1)S(1)}, bf16[1024,1024]{1,0:T(8,128)(2,1)}, u32[]{:S(2)}) copy-start(bf16[1024,1024]{1,0:T(8,128)(2,1)} %ck_ref.1) | copy-start | bytes 6291460
  3.8 1.6 %copy-start.1 = (bf16[1024,1024]{1,0:T(8,128)(2,1)S(1)}, bf16[1024,1024]{1,0:T(8,128)(2,1)}, u32[]{:S(2)}) copy-start(bf16[1024,1024]{1,0:T(8,128)(2,1)} %cv_ref.1) | copy-start | bytes 6291460
  5.3 0.9 copy-start.4
  6.3 0.9 copy-start.6
  7.2 0.7 copy-start.8
  7.9 14.8 %copy-start.7 = (bf16[128,512]{1,0:T(8,128)(2,1)S(1)}, bf16[128,512]{1,0:T(8,128)(2,1)}, u32[]{:S(2)}) copy-start(bf16[128,512]{1,0:T(8,128)(2,1)} %q_ref.1) | copy-start | bytes 393220
  7.9 16.6 %copy-start.10 = (bf16[128,512]{1,0:T(8,128)(2,1)S(1)}, bf16[128,512]{1,0:T(8,128)(2,1)}, u32[]{:S(2)}) copy-start(bf16[128,512]{1,0:T(8,128)(2,1)} %refs_5_.1) | copy-start | bytes 393220
  7.9 20.9 %copy-start.9 = (f32[128]{0:T(128)S(1)}, f32[128]{0:T(128)}, u32[]{:S(2)}) copy-start(f32[128]{0:T(128)} %param.24) | copy-start | bytes 1540
  8.7 10.2 %collective-permute-start = (bf16[576,256]{1,0:T(8,128)(2,1)S(1)}, bf16[576,256]{1,0:T(8,128)(2,1)S(1)}, u32[]{:S(2)}, u32[]{:S(2)}) collective-permute-start(bf16[576,256]{1,0:T(8,128)(2,1)S(1)} %pack_rows.1.refs_0_.refs_2_), channel_id=1, source_target_pairs={{0,16},{16,0},{1,17},{17,1},{2,18},{18,2},{3,19},{19,3},{4,20},{20... | collective-permute-start | bytes 884744 | tf_op jit(solution)/shard_map/ppermute | solution.py:526
  11.6 11.2 %collective-permute-start.1 = (bf16[576,256]{1,0:T(8,128)(2,1)S(1)}, bf16[576,256]{1,0:T(8,128)(2,1)S(1)}, u32[]{:S(2)}, u32[]{:S(2)}) collective-permute-start(bf16[576,256]{1,0:T(8,128)(2,1)S(1)} %pack_rows.1.refs_0_.refs_2_), channel_id=1, source_target_pairs={{0,96},{32,0},{64,32},{96,64},{1,97},{33,1},{65,33},{97,65},{2,98}... | collective-permute-start | bytes 884744 | tf_op jit(solution)/shard_map/ppermute | solution.py:526
  15.3 9.2 %collective-permute-start.2 = (bf16[576,256]{1,0:T(8,128)(2,1)S(1)}, bf16[576,256]{1,0:T(8,128)(2,1)S(1)}, u32[]{:S(2)}, u32[]{:S(2)}) collective-permute-start(bf16[576,256]{1,0:T(8,128)(2,1)S(1)} %pack_rows.1.refs_0_.refs_2_), channel_id=1, source_target_pairs={{0,32},{32,64},{64,96},{96,0},{1,33},{33,65},{65,97},{97,1},{2,34}... | collective-permute-start | bytes 884744 | tf_op jit(solution)/shard_map/ppermute | solution.py:526
  18.9 15.0 %collective-permute-start.5 = (bf16[576,256]{1,0:T(8,128)(2,1)S(1)}, bf16[576,256]{1,0:T(8,128)(2,1)S(1)}, u32[]{:S(2)}, u32[]{:S(2)}) collective-permute-start(bf16[576,256]{1,0:T(8,128)(2,1)S(1)} %collective-permute-done.refs_1_.refs_3_), channel_id=1, source_target_pairs={{0,96},{32,0},{64,32},{96,64},{1,97},{33,1},{65,33},{97,65},{2,98}... | collective-permute-start | bytes 884744 | tf_op jit(solution)/shard_map/ppermute | solution.py:526
  22.7 11.2 %collective-permute-start.6 = (bf16[576,256]{1,0:T(8,128)(2,1)S(1)}, bf16[576,256]{1,0:T(8,128)(2,1)S(1)}, u32[]{:S(2)}, u32[]{:S(2)}) collective-permute-start(bf16[576,256]{1,0:T(8,128)(2,1)S(1)} %collective-permute-done.refs_1_.refs_3_), channel_id=1, source_target_pairs={{0,32},{32,64},{64,96},{96,0},{1,33},{33,65},{65,97},{97,1},{2,34}... | collective-permute-start | bytes 884744 | tf_op jit(solution)/shard_map/ppermute | solution.py:526
  22.7 3.3 %collective-permute-start.3 = (bf16[128,512]{1,0:T(8,128)(2,1)S(1)}, bf16[128,512]{1,0:T(8,128)(2,1)S(1)}, u32[]{:S(2)}, u32[]{:S(2)}) collective-permute-start(bf16[128,512]{1,0:T(8,128)(2,1)S(1)} %copy-done.7), channel_id=1, source_target_pairs={{0,1},{1,0},{2,3},{3,2},{4,5},{5,4},{6,7},{7,6},{8,9},{9,8},{10,11... | collective-permute-start | bytes 393224 | tf_op jit(solution)/shard_map/ppermute | solution.py:526
  24.6 2.4 %collective-permute-start.4 = (bf16[128,512]{1,0:T(8,128)(2,1)S(1)}, bf16[128,512]{1,0:T(8,128)(2,1)S(1)}, u32[]{:S(2)}, u32[]{:S(2)}) collective-permute-start(bf16[128,512]{1,0:T(8,128)(2,1)S(1)} %copy-done.10), channel_id=1, source_target_pairs={{0,1},{1,0},{2,3},{3,2},{4,5},{5,4},{6,7},{7,6},{8,9},{9,8},{10,11... | collective-permute-start | bytes 393224 | tf_op jit(solution)/shard_map/ppermute | solution.py:526
  26.0 9.5 %collective-permute-start.9 = (bf16[288,256]{1,0:T(8,128)(2,1)S(1)}, bf16[288,256]{1,0:T(8,128)(2,1)S(1)}, u32[]{:S(2)}, u32[]{:S(2)}) collective-permute-start(bf16[288,256]{1,0:T(8,128)(2,1)S(1)} %slice.16), channel_id=1, source_target_pairs={{0,32},{32,64},{64,96},{96,0},{1,33},{33,65},{65,97},{97,1},{2,34}... | collective-permute-start | bytes 442376 | tf_op jit(solution)/shard_map/ppermute | solution.py:526
  27.0 8.6 %collective-permute-start.10 = (bf16[288,256]{1,0:T(8,128)(2,1)S(1)}, bf16[288,256]{1,0:T(8,128)(2,1)S(1)}, u32[]{:S(2)}, u32[]{:S(2)}) collective-permute-start(bf16[288,256]{1,0:T(8,128)(2,1)S(1)} %slice.17), channel_id=1, source_target_pairs={{0,96},{32,0},{64,32},{96,64},{1,97},{33,1},{65,33},{97,65},{2,98}... | collective-permute-start | bytes 442376 | tf_op jit(solution)/shard_map/ppermute | solution.py:526
  33.9 5.5 %collective-permute-start.7 = (bf16[288,256]{1,0:T(8,128)(2,1)S(1)}, bf16[288,256]{1,0:T(8,128)(2,1)S(1)}, u32[]{:S(2)}, u32[]{:S(2)}) collective-permute-start(bf16[288,256]{1,0:T(8,128)(2,1)S(1)} %slice.12), channel_id=1, source_target_pairs={{0,96},{32,0},{64,32},{96,64},{1,97},{33,1},{65,33},{97,65},{2,98}... | collective-permute-start | bytes 442376 | tf_op jit(solution)/shard_map/ppermute | solution.py:526
  34.5 5.3 %collective-permute-start.8 = (bf16[288,256]{1,0:T(8,128)(2,1)S(1)}, bf16[288,256]{1,0:T(8,128)(2,1)S(1)}, u32[]{:S(2)}, u32[]{:S(2)}) collective-permute-start(bf16[288,256]{1,0:T(8,128)(2,1)S(1)} %slice.13), channel_id=1, source_target_pairs={{0,32},{32,64},{64,96},{96,0},{1,33},{33,65},{65,97},{97,1},{2,34}... | collective-permute-start | bytes 442376 | tf_op jit(solution)/shard_map/ppermute | solution.py:526
  39.7 6.0 %copy-start.2 = (bf16[8192,64]{0,1:T(8,128)(2,1)S(1)}, bf16[8192,64]{0,1:T(8,128)(2,1)}, u32[]{:S(2)}) copy-start(bf16[8192,64]{0,1:T(8,128)(2,1)} %param.16) | copy-start | bytes 3145732
  39.8 6.1 %copy-start.3 = (bf16[8192,64]{0,1:T(8,128)(2,1)S(1)}, bf16[8192,64]{0,1:T(8,128)(2,1)}, u32[]{:S(2)}) copy-start(bf16[8192,64]{0,1:T(8,128)(2,1)} %param.17) | copy-start | bytes 3145732
  43.2 4.1 %collective-permute-start.11 = (f32[1024,128]{1,0:T(8,128)S(1)}, f32[1024,128]{1,0:T(8,128)S(1)}, u32[]{:S(2)}, u32[]{:S(2)}) collective-permute-start(f32[1024,128]{1,0:T(8,128)S(1)} %get-tuple-element.54.mine_ref), channel_id=1, source_target_pairs={{0,1},{1,0},{2,3},{3,2},{4,5},{5,4},{6,7},{7,6},{8,9},{9,8},{10,11... | collective-permute-start | bytes 1572872 | tf_op jit(solution)/shard_map/ppermute | solution.py:526
  45.7 29.1 %collective-permute-start.19 = (bf16[64,8192]{1,0:T(8,128)(2,1)S(1)}, bf16[64,8192]{1,0:T(8,128)(2,1)S(1)}, u32[]{:S(2)}, u32[]{:S(2)}) collective-permute-start(bf16[64,8192]{1,0:T(8,128)(2,1)S(1)} %bitcast.21), channel_id=1, source_target_pairs={{0,1},{1,0},{2,3},{3,2},{4,5},{5,4},{6,7},{7,6},{8,9},{9,8},{10,11... | collective-permute-start | bytes 3145736 | tf_op jit(solution)/shard_map/ppermute | solution.py:526
  45.8 29.0 %collective-permute-start.20 = (bf16[64,8192]{1,0:T(8,128)(2,1)S(1)}, bf16[64,8192]{1,0:T(8,128)(2,1)S(1)}, u32[]{:S(2)}, u32[]{:S(2)}) collective-permute-start(bf16[64,8192]{1,0:T(8,128)(2,1)S(1)} %bitcast.23), channel_id=1, source_target_pairs={{0,1},{1,0},{2,3},{3,2},{4,5},{5,4},{6,7},{7,6},{8,9},{9,8},{10,11... | collective-permute-start | bytes 3145736 | tf_op jit(solution)/shard_map/ppermute | solution.py:526
  47.3 28.7 %slice-start = ((s8[8388608]{0:T(1024)(128)(4,1)}), s8[4194304]{0:T(1024)(128)(4,1)S(1)}, s32[]{:S(2)}) async-start(s8[8388608]{0:T(1024)(128)(4,1)} %bitcast.19), calls=%async_computation.2 | async-start | bytes 8388608
  51.0 6.0 %collective-permute-start.12 = (f32[128,256]{1,0:T(8,128)S(1)}, f32[128,256]{1,0:T(8,128)S(1)}, u32[]{:S(2)}, u32[]{:S(2)}) collective-permute-start(f32[128,256]{1,0:T(8,128)S(1)} %get-tuple-element.58), channel_id=1, source_target_pairs={{0,32},{32,64},{64,96},{96,0},{1,33},{33,65},{65,97},{97,1},{2,34}... | collective-permute-start | bytes 393224 | tf_op jit(solution)/shard_map/ppermute | solution.py:526
  51.1 11.6 %collective-permute-start.13 = (f32[128,256]{1,0:T(8,128)S(1)}, f32[128,256]{1,0:T(8,128)S(1)}, u32[]{:S(2)}, u32[]{:S(2)}) collective-permute-start(f32[128,256]{1,0:T(8,128)S(1)} %get-tuple-element.59), channel_id=1, source_target_pairs={{0,96},{32,0},{64,32},{96,64},{1,97},{33,1},{65,33},{97,65},{2,98}... | collective-permute-start | bytes 393224 | tf_op jit(solution)/shard_map/ppermute | solution.py:526
  57.0 5.7 %collective-permute-start.14 = (f32[128,256]{1,0:T(8,128)S(1)}, f32[128,256]{1,0:T(8,128)S(1)}, u32[]{:S(2)}, u32[]{:S(2)}) collective-permute-start(f32[128,256]{1,0:T(8,128)S(1)} %get-tuple-element.60), channel_id=1, source_target_pairs={{0,64},{32,96},{64,0},{96,32},{1,65},{33,97},{65,1},{97,33},{2,66}... | collective-permute-start | bytes 393224 | tf_op jit(solution)/shard_map/ppermute | solution.py:526
  57.0 19.0 %slice-start.1 = ((s8[8388608]{0:T(1024)(128)(4,1)}), s8[4194304]{0:T(1024)(128)(4,1)S(1)}, s32[]{:S(2)}) async-start(s8[8388608]{0:T(1024)(128)(4,1)} %bitcast.19), calls=%async_computation.3 | async-start | bytes 8388608
  63.3 10.7 %copy-start.5 = (bf16[128,1024]{1,0:T(8,128)(2,1)S(1)}, bf16[128,1024]{1,0:T(8,128)(2,1)}, u32[]{:S(2)}) copy-start(bf16[128,1024]{1,0:T(8,128)(2,1)} %raw_ref.1) | copy-start | bytes 786436
  63.3 8.4 %collective-permute-start.15 = (f32[64,256]{1,0:T(8,128)S(1)}, f32[64,256]{1,0:T(8,128)S(1)}, u32[]{:S(2)}, u32[]{:S(2)}) collective-permute-start(f32[64,256]{1,0:T(8,128)S(1)} %get-tuple-element.68), channel_id=1, source_target_pairs={{0,16},{16,0},{1,17},{17,1},{2,18},{18,2},{3,19},{19,3},{4,20},{20... | collective-permute-start | bytes 196616 | tf_op jit(solution)/shard_map/ppermute | solution.py:526
  71.7 4.3 %collective-permute-start.16 = (f32[1024,128]{1,0:T(8,128)S(1)}, f32[1024,128]{1,0:T(8,128)S(1)}, u32[]{:S(2)}, u32[]{:S(2)}) collective-permute-start(f32[1024,128]{1,0:T(8,128)S(1)} %cache_grads_4.1.dq_ref), channel_id=1, source_target_pairs={{0,1},{1,0},{2,3},{3,2},{4,5},{5,4},{6,7},{7,6},{8,9},{9,8},{10,11... | collective-permute-start | bytes 1572872 | tf_op jit(solution)/shard_map/ppermute | solution.py:526
  74.7 1.3 %collective-permute-start.17 = (bf16[64,256]{1,0:T(8,128)(2,1)S(1)}, bf16[64,256]{1,0:T(8,128)(2,1)S(1)}, u32[]{:S(2)}, u32[]{:S(2)}) collective-permute-start(bf16[64,256]{1,0:T(8,128)(2,1)S(1)} %own_kv.1.kv_ref), channel_id=1, source_target_pairs={{0,1},{1,0},{2,3},{3,2},{4,5},{5,4},{6,7},{7,6},{8,9},{9,8},{10,11... | collective-permute-start | bytes 98312 | tf_op jit(solution)/shard_map/ppermute | solution.py:526
  85.1 4.3 %copy-start.11 = (bf16[128,512]{1,0:T(8,128)(2,1)S(1)}, bf16[128,512]{1,0:T(8,128)(2,1)}, u32[]{:S(2)}) copy-start(bf16[128,512]{1,0:T(8,128)(2,1)} %param.13) | copy-start | bytes 393220
  85.1 4.5 %copy-start.12 = (bf16[128,512]{1,0:T(8,128)(2,1)S(1)}, bf16[128,512]{1,0:T(8,128)(2,1)}, u32[]{:S(2)}) copy-start(bf16[128,512]{1,0:T(8,128)(2,1)} %param.14) | copy-start | bytes 393220
  85.1 19.3 %all-to-all-start = ((bf16[8,512,128]{2,1,0:T(8,128)(2,1)}), bf16[8,512,128]{2,1,0:T(8,128)(2,1)S(1)}, u32[]{:S(2)}, u32[]{:S(2)}) async-start(bf16[8,512,128]{2,1,0:T(8,128)(2,1)} %project.1), calls=%async_computation | async-start | bytes 2097152 | tf_op jit(solution)/shard_map/all_to_all | solution.py:601

commit v3 on v2

--- a/solution.py
+++ b/solution.py
@@ -33,10 +33,20 @@
 SCALE = math.sqrt(HD)
 EXP_SCALE = SCALE * math.log2(math.e)
 NEG = -1e30
-VMEM_LIMIT = 28 * 1024 * 1024
+VMEM_LIMIT = 24 * 1024 * 1024
 TP_AXES = ("xl", "y", "c")
 CTX_AXES = ("z", "xh")
 CHIP_AXES = ("xl", "y")
+
+
+HOPS = ((0, 0), (0, 1), (1, 0), (3, 0), (1, 1), (3, 1), (2, 0), (2, 1))
+Z, XH, CHIP, CORE, FLOOR = range(5)
+SHAPE = jax.ShapeDtypeStruct
+STATE = [SHAPE((ROWS, HD), jnp.float32)] * 3
+VM = pl.BlockSpec(memory_space=pltpu.VMEM)
+SM = pl.BlockSpec(memory_space=pltpu.SMEM)
+HB = pl.BlockSpec(memory_space=pltpu.HBM)
+SMALL = pltpu.CompilerParams(vmem_limit_bytes=8 * 1024 * 1024)
 
 
 def contract_last(left, right):
@@ -74,40 +84,75 @@
     return slice(h * TOK, (h + 1) * TOK)
 
 
-def pack_kernel(idx_ref, ck_ref, cv_ref, kr_ref, vw_ref, gain_ref, out_ref):
+def pack_kernel(
+    info_ref,
+    ck_ref,
+    cv_ref,
+    kr_ref,
+    vw_ref,
+    resid_ref,
+    dh_ref,
+    gain_ref,
+    out_ref,
+    resid_out,
+    dh_out,
+    ck_s,
+    kr_s,
+    resid_s,
+    dh_s,
+    sems,
+):
+    cols = pl.ds(pl.multiple_of(info_ref[CHIP] * HD, HD), HD)
+    cache = pl.ds(pl.multiple_of(info_ref[CORE] * HALF_CACHE, HALF_CACHE), HALF_CACHE)
+    win = pl.ds(pl.multiple_of(info_ref[CORE] * HALF_WIN, HALF_WIN), HALF_WIN)
+    right = pl.ds(HD, HD)
+    copies = [
+        pltpu.make_async_copy(ck_ref.at[cache, cols], ck_s, sems.at[0]),
+        pltpu.make_async_copy(kr_ref.at[win, cols], kr_s, sems.at[1]),
+        pltpu.make_async_copy(
+            cv_ref.at[cache, cols], out_ref.at[pl.ds(0, HALF_CACHE), right], sems.at[2]
+        ),
+        pltpu.make_async_copy(
+            vw_ref.at[win, cols], out_ref.at[pl.ds(HALF_CACHE, HALF_WIN), right], sems.at[3]
+        ),
+        pltpu.make_async_copy(resid_ref, resid_s, sems.at[4]),
+        pltpu.make_async_copy(dh_ref, dh_s, sems.at[5]),
+    ]
+    for copy in copies:
+        copy.start()
     gain = gain_ref[...]
-    out_ref[:HALF_CACHE, :HD] = unit_rows(ck_ref[...].astype(jnp.float32), gain).astype(
-        jnp.bfloat16
-    )
-    out_ref[:HALF_CACHE, HD:] = cv_ref[...]
-    out_ref[HALF_CACHE:, :HD] = unit_rows(kr_ref[...].astype(jnp.float32), gain).astype(
-        jnp.bfloat16
-    )
-    out_ref[HALF_CACHE:, HD:] = vw_ref[...]
-
-
-def pack_rows(idx, cache_k, cache_v, k_raw, v_win, gain):
-    def at(i, idx):
-        return (idx[CORE], idx[CHIP])
-
+    copies[0].wait()
+    out_ref[:HALF_CACHE, :HD] = unit_rows(ck_s[...].astype(jnp.float32), gain).astype(jnp.bfloat16)
+    copies[1].wait()
+    out_ref[HALF_CACHE:, :HD] = unit_rows(kr_s[...].astype(jnp.float32), gain).astype(jnp.bfloat16)
+    copies[2].wait()
+    copies[3].wait()
+    copies[4].wait()
+    resid_out[...] = resid_s[...].astype(jnp.float32).T.astype(jnp.bfloat16)
+    copies[5].wait()
+    dh_out[...] = dh_s[...].astype(jnp.float32).T.astype(jnp.bfloat16)
+
+
+def pack_rows(info, cache_k, cache_v, k_raw, v_win, resid, dh, gain):
     return pl.pallas_call(
         pack_kernel,
-        out_shape=jax.ShapeDtypeStruct((HALF, 2 * HD), jnp.bfloat16),
-        grid_spec=pltpu.PrefetchScalarGridSpec(
-            num_scalar_prefetch=1,
-            grid=(1,),
-            in_specs=[
-                pl.BlockSpec((HALF_CACHE, HD), at),
-                pl.BlockSpec((HALF_CACHE, HD), at),
-                pl.BlockSpec((HALF_WIN, HD), at),
-                pl.BlockSpec((HALF_WIN, HD), at),
-                pl.BlockSpec((1, HD), lambda i, idx: (0, 0)),
-            ],
-            out_specs=pl.BlockSpec((HALF, 2 * HD), lambda i, idx: (0, 0)),
-        ),
-        compiler_params=pltpu.CompilerParams(vmem_limit_bytes=8 * 1024 * 1024),
+        out_shape=[
+            SHAPE((HALF, 2 * HD), jnp.bfloat16),
+            SHAPE((FEAT, TOK), jnp.bfloat16),
+            SHAPE((FEAT, TOK), jnp.bfloat16),
+        ],
+        in_specs=[SM] + [HB] * 6 + [VM],
+        out_specs=[VM] * 3,
+        scratch_shapes=[
+            pltpu.VMEM((HALF_CACHE, HD), jnp.bfloat16),
+            pltpu.VMEM((HALF_WIN, HD), jnp.bfloat16),
+            pltpu.VMEM((TOK, FEAT), jnp.bfloat16),
+            pltpu.VMEM((TOK, FEAT), jnp.bfloat16),
+            pltpu.SemaphoreType.DMA((6,)),
+        ],
+        compiler_params=SMALL,
         name="pack_rows",
-    )(idx, cache_k, cache_v, k_raw, v_win, gain)
+    )(info, cache_k, cache_v, k_raw, v_win, resid, dh, gain)
 
 
 def cost(flops, exps, moved):
@@ -120,10 +165,6 @@
     return cost(
         blocks * dots * 2 * ROWS * KB * HD, blocks * ROWS * KB, blocks * 4 * KB * HD + 2 ** 21
     )
-
-
-HOPS = ((0, 0), (0, 1), (1, 0), (3, 0), (1, 1), (3, 1), (2, 0), (2, 1))
-Z, XH, CHIP, CORE, FLOOR = range(5)
 
 
 def source(info_ref, dz, dx):
@@ -154,7 +195,7 @@
 
 
 def chunk(r):
-    return pl.ds(pl.multiple_of(r * CHUNK, CHUNK), CHUNK)
+    return slice(r * CHUNK, (r + 1) * CHUNK)
 
 
 def keys_at(n):
@@ -193,19 +234,25 @@
 
 
 def cache_loop(info_ref, first, count, core, body):
-    @pl.loop(0, count * CHUNKS)
-    def _(i):
-        n = i // CHUNKS
-        r = lax.rem(i, CHUNKS)
+    @pl.loop(0, count)
+    def _(n):
         start = source_at(info_ref, first + n) * (2 * KB) + core * KB
 
         @pl.when((start + KB > info_ref[FLOOR]) & (start < info_ref[FLOOR]))
         def _():
-            body(n, r, start, True)
+            body(n, start, True)
 
         @pl.when(start >= info_ref[FLOOR])
         def _():
-            body(n, r, start, False)
+            body(n, start, False)
+
+
+def pipelined(dots, rest):
+    ready = dots(0)
+    for r in range(CHUNKS):
+        following = dots(r + 1) if r + 1 < CHUNKS else None
+        rest(r, *ready)
+        ready = following
 
 
 def stats_kernel(first, groups, last, info_ref, *refs):
@@ -247,11 +294,21 @@
     k_s, v_s = scratch
     place_cache(pieces, k_s, v_s)
 
-    def body(n, r, start, masked):
-        scores = contract_last(q_s[chunk(r), :], k_s[keys_at(n), :])
-        dprobs = contract_last(do_s[chunk(r), :], v_s[keys_at(n), :])
+    def body(n, start, masked):
+        keys = k_s[keys_at(n), :]
+        values = v_s[keys_at(n), :]
         mask = cache_mask(info_ref, start) if masked else None
-        stat_block(scores, dprobs, mask, chunk(r), m_s, l_s, w_s)
+
+        def dots(r):
+            return (
+                contract_last(q_s[chunk(r), :], keys),
+                contract_last(do_s[chunk(r), :], values),
+            )
+
+        def rest(r, scores, dprobs):
+            stat_block(scores, dprobs, mask, chunk(r), m_s, l_s, w_s)
+
+        pipelined(dots, rest)
 
     cache_loop(info_ref, first, len(groups), core, body)
     if last:
@@ -261,11 +318,20 @@
             wk_ref[pl.ds(at, HALF_WIN), :] = piece[low:, :HD]
             wv_ref[pl.ds(at, HALF_WIN), :] = piece[low:, HD:]
 
-        @pl.loop(0, CHUNKS)
-        def _(r):
-            scores = contract_last(q_s[chunk(r), :], wk_ref[...])
-            dprobs = contract_last(do_s[chunk(r), :], wv_ref[...])
-            stat_block(scores, dprobs, window_mask(info_ref), chunk(r), m_s, l_s, w_s)
+        win_mask = window_mask(info_ref)
+        win_keys = wk_ref[...]
+        win_values = wv_ref[...]
+
+        def win_dots(r):
+            return (
+                contract_last(q_s[chunk(r), :], win_keys),
+                contract_last(do_s[chunk(r), :], win_values),
+            )
+
+        def win_rest(r, scores, dprobs):
+            stat_block(scores, dprobs, win_mask, chunk(r), m_s, l_s, w_s)
+
+        pipelined(win_dots, win_rest)
 
         top = jnp.max(m_s[...], axis=1, keepdims=True)
         fix = jnp.exp2((m_s[...] - top) * EXP_SCALE)
@@ -273,12 +339,6 @@
         weighted = jnp.sum(w_s[...] * fix, axis=1, keepdims=True)
         lane = lax.broadcasted_iota(jnp.int32, (ROWS, HD), 1)
         stat_ref[...] = jnp.where(lane == 0, top, jnp.where(lane == 1, total, weighted))
-
-
-SHAPE = jax.ShapeDtypeStruct
-STATE = [SHAPE((ROWS, HD), jnp.float32)] * 3
-VM = pl.BlockSpec(memory_space=pltpu.VMEM)
-SM = pl.BlockSpec(memory_space=pltpu.SMEM)
 
 
 def stats_call(first, info, groups, rest, last=False):
@@ -333,19 +393,21 @@
     delta_ref[...] = jnp.broadcast_to(weighted / total, (ROWS, HD))
     dkv_ref[...] = jnp.zeros((KB, 2 * HD), jnp.float32)
 
-    @pl.loop(0, CHUNKS)
-    def _(r):
+    mask = window_mask(info_ref)
+    keys = wk_ref[...]
+    values = wv_ref[...]
+
+    def dots(r):
+        return contract_last(q_s[chunk(r), :], keys), contract_last(do_s[chunk(r), :], values)
+
+    def rest(r, scores, dprobs):
         rows = chunk(r)
-        query = q_s[rows, :]
-        dout = do_s[rows, :]
-        scores = contract_last(query, wk_ref[...])
-        dprobs = contract_last(dout, wv_ref[...])
-        probs, dscores = grad_block(
-            scores, dprobs, window_mask(info_ref), lse_ref[rows, :], delta_ref[rows, :]
-        )
-        dq_ref[rows, :] = jnp.dot(dscores, wk_ref[...], preferred_element_type=jnp.float32)
-        dkv_ref[:, :HD] += contract_first(dscores, query)
-        dkv_ref[:, HD:] += contract_first(probs, dout)
+        probs, dscores = grad_block(scores, dprobs, mask, lse_ref[rows, :], delta_ref[rows, :])
+        dq_ref[rows, :] = jnp.dot(dscores, keys, preferred_element_type=jnp.float32)
+        dkv_ref[:, :HD] += contract_first(dscores, q_s[rows, :])
+        dkv_ref[:, HD:] += contract_first(probs, do_s[rows, :])
+
+    pipelined(dots, rest)
 
     for dz in range(4):
         at = pl.multiple_of(lax.bitwise_and(info_ref[Z] + dz, 3) * TOK, TOK)
@@ -366,8 +428,31 @@
     )(info, mine, pair, query, dout, win_k, win_v)
 
 
+def fetches(info_ref, weights, w_ref, kv_ref, sems):
+    wq_ref, wk_ref, wv_ref, pair_wq_ref, pair_wk_ref, pair_wv_ref = weights
+    copies = []
+    for j in range(CHIPS):
+        rows = pl.ds(pl.multiple_of((2 * j + info_ref[CORE]) * FEAT, FEAT), FEAT)
+        for n, ref in enumerate((wq_ref, pair_wq_ref)):
+            target = w_ref.at[j, :, pl.ds(n * COLS, COLS)]
+            copies.append(pltpu.make_async_copy(ref.at[rows, :], target, sems.at[j, n]))
+        for n, ref in enumerate((wk_ref, wv_ref, pair_wk_ref, pair_wv_ref)):
+            target = kv_ref.at[j, pl.ds(n * SIDE, SIDE), :]
+            copies.append(pltpu.make_async_copy(ref.at[:, rows], target, sems.at[j, 2 + n]))
+    return copies
+
+
 def cache_kernel(first, groups, info_ref, *refs):
     refs = list(refs)
+    copies = []
+    if first == 0:
+        sems = refs.pop()
+        weights = [refs.pop(0) for _ in range(6)]
+        w_ref, kv_ref = refs[-4], refs[-3]
+        del refs[-4:-2]
+        copies = fetches(info_ref, weights, w_ref, kv_ref, sems)
+    for copy in copies:
+        copy.start()
     pieces = []
     for size in groups:
         pieces.append([refs.pop(0) for _ in range(size)])
@@ -375,33 +460,46 @@
     place_cache(pieces, k_s, v_s)
     dq_ref[...] = dq_in[...]
 
-    def body(n, r, start, masked):
-        rows = chunk(r)
+    def body(n, start, masked):
         keys = k_s[keys_at(n), :]
-        scores = contract_last(q_s[rows, :], keys)
-        dprobs = contract_last(do_s[rows, :], v_s[keys_at(n), :])
+        values = v_s[keys_at(n), :]
         mask = cache_mask(info_ref, start) if masked else None
-        _, dscores = grad_block(scores, dprobs, mask, lse_ref[rows, :], delta_ref[rows, :])
-        dq_ref[rows, :] += jnp.dot(dscores, keys, preferred_element_type=jnp.float32)
+
+        def dots(r):
+            return contract_last(q_s[chunk(r), :], keys), contract_last(do_s[chunk(r), :], values)
+
+        def rest(r, scores, dprobs):
+            rows = chunk(r)
+            _, dscores = grad_block(scores, dprobs, mask, lse_ref[rows, :], delta_ref[rows, :])
+            dq_ref[rows, :] += jnp.dot(dscores, keys, preferred_element_type=jnp.float32)
+
+        pipelined(dots, rest)
 
     cache_loop(info_ref, first, len(groups), info_ref[CORE], body)
-
-
-def cache_call(first, info, groups, query, dout, lse, delta, dq):
+    for copy in copies:
+        copy.wait()
+
+
+def cache_call(first, info, groups, query, dout, lse, delta, dq, weights=()):
     pieces = [piece for group in groups for piece in group]
+    out = STATE[:1]
+    scratch = [pltpu.VMEM((len(groups) * KB, HD), jnp.bfloat16)] * 2
+    if weights:
+        out = out + [
+            SHAPE((CHIPS, FEAT, 2 * COLS), jnp.bfloat16),
+            SHAPE((CHIPS, 2 * HD, FEAT), jnp.bfloat16),
+        ]
+        scratch = scratch + [pltpu.SemaphoreType.DMA((CHIPS, 6))]
     return pl.pallas_call(
         functools.partial(cache_kernel, first, [len(group) for group in groups]),
-        out_shape=STATE[0],
-        in_specs=[SM] + [VM] * (len(pieces) + 5),
-        out_specs=VM,
-        scratch_shapes=[pltpu.VMEM((len(groups) * KB, HD), jnp.bfloat16)] * 2,
+        out_shape=out,
+        in_specs=[SM] + [HB] * len(weights) + [VM] * (len(pieces) + 5),
+        out_specs=[VM] * len(out),
+        scratch_shapes=scratch,
         compiler_params=pltpu.CompilerParams(vmem_limit_bytes=VMEM_LIMIT),
         cost_estimate=block_cost(len(groups), 3),
         name="cache_grads_" + str(first),
-    )(info, *pieces, query, dout, lse, delta, dq)
-
-
-SMALL = pltpu.CompilerParams(vmem_limit_bytes=8 * 1024 * 1024)
+    )(info, *weights, *pieces, query, dout, lse, delta, dq)
 
 
 def sum_kernel(info_ref, a_ref, b_ref, c_ref, d_ref, keep_ref, send_ref):
@@ -453,7 +551,7 @@
 
 
 def project_kernel(
-    idx_ref,
+    info_ref,
     dq_ref,
     pair_dq_ref,
     q_ref,
@@ -461,16 +559,12 @@
     gain_ref,
     kv_ref,
     pair_kv_ref,
-    wq_ref,
-    wk_ref,
-    wv_ref,
-    pair_wq_ref,
-    pair_wk_ref,
-    pair_wv_ref,
+    w_ref,
+    wkv_ref,
     out_ref,
     g_s,
 ):
-    core = idx_ref[CORE]
+    core = info_ref[CORE]
     gain = gain_ref[...]
     for h in range(HEADS):
         rows = head_rows(h)
@@ -493,32 +587,75 @@
         second = jnp.where(core == 0, both[SIDE:, :], both[:SIDE, :])
         g_s[2 * COLS + n * SIDE : 2 * COLS + (n + 1) * SIDE, :] = first
         g_s[2 * COLS + (2 + n) * SIDE : 2 * COLS + (3 + n) * SIDE, :] = second
-
-    @pl.loop(0, CHIPS)
-    def _(j):
-        rows = pl.ds(pl.multiple_of((2 * j + core) * FEAT, FEAT), FEAT)
-        total = jnp.dot(wq_ref[rows, :], g_s[:COLS, :], preferred_element_type=jnp.float32)
-        total += jnp.dot(
-            pair_wq_ref[rows, :], g_s[COLS : 2 * COLS, :], preferred_element_type=jnp.float32
-        )
-        narrow = jnp.concatenate(
-            [wk_ref[:, rows], wv_ref[:, rows], pair_wk_ref[:, rows], pair_wv_ref[:, rows]], 0
-        )
-        total += contract_first(narrow, g_s[2 * COLS :, :])
+    for j in range(CHIPS):
+        total = contract_first(wkv_ref[j], g_s[2 * COLS :, :])
+        total += jnp.dot(w_ref[j], g_s[: 2 * COLS, :], preferred_element_type=jnp.float32)
         out_ref[j] = total.astype(jnp.bfloat16)
 
 
-def project(idx, dq, pair_dq, q_raw, pair_q, gain, kv, pair_kv, weights, pair_weights):
+def project(info, *operands):
     return pl.pallas_call(
         project_kernel,
-        out_shape=jax.ShapeDtypeStruct((CHIPS, FEAT, TOK), jnp.bfloat16),
-        in_specs=[SM] + [VM] * 13,
+        out_shape=SHAPE((CHIPS, FEAT, TOK), jnp.bfloat16),
+        in_specs=[SM] + [VM] * 9,
         out_specs=VM,
         scratch_shapes=[pltpu.VMEM((2 * COLS + 2 * HD, TOK), jnp.bfloat16)],
         compiler_params=pltpu.CompilerParams(vmem_limit_bytes=VMEM_LIMIT),
-        cost_estimate=cost(2 * TOK * D // 2 * 1280, 0, 3e6),
+        cost_estimate=cost(2 * TOK * D // 2 * 1280, 0, 12e6),
         name="project",
-    )(idx, dq, pair_dq, q_raw, pair_q, gain, kv, pair_kv, *weights, *pair_weights)
+    )(info, *operands)
+
+
+def rows_kernel(pieces_ref, resid_ref, dh_ref, grad_ref, sums_ref):
+    inner = jnp.zeros((1, TOK), jnp.float32)
+    square = jnp.zeros((1, TOK), jnp.float32)
+    for n in range(FEAT // HD):
+        rows = head_cols(n)
+        grad = pieces_ref[0, rows, :].astype(jnp.float32)
+        for m in range(1, CHIPS):
+            grad += pieces_ref[m, rows, :].astype(jnp.float32)
+        grad += dh_ref[rows, :].astype(jnp.float32)
+        grad_ref[rows, :] = grad
+        resid = resid_ref[rows, :].astype(jnp.float32)
+        inner += jnp.sum(grad * resid, axis=0, keepdims=True)
+        square += jnp.sum(resid * resid, axis=0, keepdims=True)
+    row = lax.broadcasted_iota(jnp.int32, (8, TOK), 0)
+    sums_ref[...] = jnp.where(row == 0, inner, square)
+
+
+def row_sums(pieces, resid_t, dh_t):
+    return pl.pallas_call(
+        rows_kernel,
+        out_shape=[SHAPE((FEAT, TOK), jnp.float32), SHAPE((8, TOK), jnp.float32)],
+        in_specs=[VM] * 3,
+        out_specs=[VM] * 2,
+        compiler_params=SMALL,
+        name="row_sums",
+    )(pieces, resid_t, dh_t)
+
+
+def norm_kernel(grad_ref, sums_ref, resid_ref, out_ref):
+    sums = sums_ref[0]
+    for n in range(1, 2 * CHIPS):
+        sums += sums_ref[n]
+    mean_sq = sums[1:2, :] / D
+    factor = lax.rsqrt(mean_sq + EPS) / math.sqrt(D)
+    correction = sums[0:1, :] / (D * (mean_sq + EPS))
+    for n in range(FEAT // HD):
+        rows = head_cols(n)
+        resid = resid_ref[rows, :].astype(jnp.float32)
+        out_ref[:, rows] = (factor * (grad_ref[rows, :] - resid * correction)).T
+
+
+def last_norm(grad_t, sums, resid_t):
+    return pl.pallas_call(
+        norm_kernel,
+        out_shape=SHAPE((TOK, FEAT), jnp.float32),
+        in_specs=[VM] * 3,
+        out_specs=VM,
+        compiler_params=SMALL,
+        name="last_norm",
+    )(grad_t, sums, resid_t)
 
 
 def shift(block, axis, by):
@@ -556,19 +693,19 @@
     ).astype(jnp.int32)
     gain = s_qk.reshape(1, HD)
 
-    here = pack_rows(info, cache_k, cache_v, k_raw, v_win, gain)
+    sources = [cache_k, cache_v, k_raw, v_win, residual_in, dh_rest]
+    sources = [pltpu.with_memory_space_constraint(array, pltpu.HBM) for array in sources]
+    here, resid_t, dh_t = pack_rows(info, *sources, gain)
     there = swap(here, "xh")
     up = shift(here, "z", -1)
     down = shift(here, "z", 1)
+    pair_wide = swap(w_query, "c")
     pair_q = swap(q_raw, "c")
     pair_do = swap(d_attn, "c")
     up_there = shift(there, "z", -1)
     down_there = shift(there, "z", 1)
     far = [shift(up[:CUT], "z", -1), shift(down[CUT:], "z", 1)]
     groups = [[here], [there], [up], [down]]
-    weights = (w_query, w_key.T, w_value.T)
-    pair_weights = [swap(w, "c") for w in weights]
-
     query, dout, *state = stats_call(
         0, info, groups[:4], [q_raw, d_attn, pair_q, pair_do, gain]
     )
@@ -578,38 +715,35 @@
     far_there = [shift(up_there[:CUT], "z", -1), shift(down_there[CUT:], "z", 1)]
     groups += [[up_there], [down_there], far, far_there]
     state = stats_call(4, info, groups[4:7], [query, dout, *state])
+    narrow = [w_key.T, w_value.T]
+    state, narrow = lax.optimization_barrier((state, narrow))
+    weights = [w_query, *narrow]
+    pair_weights = [pair_wide] + [swap(w, "c") for w in narrow]
     wins = [group[-1] for group in groups[:-1]]
     stat, win_k, win_v = stats_call(
         7, info, groups[7:], wins + [query, dout, *state], last=True
     )
-    lse, delta, dq, *parts = window_call(
-        info, stat, swap(stat, "c"), query, dout, win_k, win_v
-    )
+    pair_stat, pair_weights = lax.optimization_barrier((swap(stat, "c"), pair_weights))
+    lse, delta, dq, *parts = window_call(info, stat, pair_stat, query, dout, win_k, win_v)
     parts = [parts[0]] + [shift(parts[dz], "z", dz) for dz in (1, 3, 2)]
-    dq = cache_call(0, info, groups[:4], query, dout, lse, delta, dq)
+    dq, w_own, w_kv = cache_call(
+        0, info, groups[:5], query, dout, lse, delta, dq, [*weights, *pair_weights]
+    )
     parts, dq = lax.optimization_barrier((parts, dq))
     keep, send = sum_parts(info, parts)
     other = swap(send, "xh")
-    dq = cache_call(4, info, groups[4:], query, dout, lse, delta, dq)
+    (dq,) = cache_call(5, info, groups[5:], query, dout, lse, delta, dq)
     other, dq = lax.optimization_barrier((other, dq))
     pair_dq = swap(dq, "c")
     kv = own_kv(info, keep, other, k_raw, gain)
     pair_kv = swap(kv, "c")
-    partial = project(
-        info, dq, pair_dq, q_raw, pair_q, gain, kv, pair_kv, weights, pair_weights
-    )
+    partial = project(info, dq, pair_dq, q_raw, pair_q, gain, kv, pair_kv, w_own, w_kv)
     pieces = lax.all_to_all(partial, CHIP_AXES, 0, 0)
-    grad_total = jnp.sum(pieces.astype(jnp.float32), axis=0).T + dh_rest.astype(jnp.float32)
-    resid = residual_in.astype(jnp.float32)
-    sums = jnp.stack([jnp.sum(resid * resid, axis=1), jnp.sum(grad_total * resid, axis=1)])
+    grad_t, sums = row_sums(pieces, resid_t, dh_t)
     everyone = lax.all_to_all(
-        jnp.broadcast_to(sums[None], (16, 2, TOK)), TP_AXES, 0, 0
-    )
-    square_sum, inner_sum = jnp.sum(everyone, axis=0)
-    mean_sq = square_sum / D
-    factor = lax.rsqrt(mean_sq + EPS) / math.sqrt(D)
-    correction = inner_sum / (D * (mean_sq + EPS))
-    return factor[:, None] * (grad_total - resid * correction[:, None])
+        jnp.broadcast_to(sums[None], (2 * CHIPS, 8, TOK)), TP_AXES, 0, 0
+    )
+    return last_norm(grad_t, everyone, resid_t)
 
 
 def solution(mesh):

time: 116 us -> 103 us (0.89)
  blocking collectives: 10 us -> 29 us
  waiting for transfers between devices: 25.6 us -> 12.8 us
  Pallas kernels: 38.5 us -> 28.5 us
  starting transfers between devices: 33.2 us -> 28.7 us
  local copies, waits for them, and re-layouts: 6.99 us -> 2.63 us
    all_to_all x1 -> x2, blocking collectives: 10 us -> 29 us  [the longest x1 18.4 us: on_device(): pieces = lax.all_to_all(partial, CHIP_AXES, 0, 0)]
    all_to_all x1 -> x0, waiting for transfers between devices: 14.7 us -> none  [on_device(): pieces = lax.all_to_all(partial, CHIP_AXES, 0, 0)]
    all_to_all x1 -> x0, starting transfers between devices: 4.34 us -> none  [on_device(): pieces = lax.all_to_all(partial, CHIP_AXES, 0, 0)]
    pallas_call x3, Pallas kernels: 12.3 us -> 8.4 us  [stats_call(): pl.pallas_call(functools.partial(stats_kernel, first, [len(group) for gro...]
    unnamed x32 -> x18, local copies, waits for them, and re-layouts: 6.01 us -> 2.49 us
    pallas_call x2, Pallas kernels: 11.4 us -> 8.48 us  [cache_call(): pl.pallas_call(functools.partial(cache_kernel, first, [len(group) for gro...]
    pallas_call x2 -> x4, Pallas kernels: 9.81 us -> 7.23 us  [the longest x1 3.91 us: project(): pl.pallas_call(project_kernel, out_shape=SHAPE((CHIPS, FEAT, TOK), jnp.bf...]
    ppermute x21, waiting for transfers between devices: 10.9 us -> 12.8 us  [shift(): lax.ppermute(block, axis, [(i, (i + by) % count) for i in range(count)])]
  transfers between devices with their start and end apart: 22 -> 21, of which waited for: 8 -> 8; matrix products, arithmetic and copies ran while one was open for 0% -> 0% of each run, Pallas kernels for 25% -> 19%
where the time goes in v3:
time: 103 us; the launch traced here: 102 us
  blocking collectives  29 us (28%)
  starting transfers between devices  28.7 us (28%)
  Pallas kernels  28.5 us (28%)
  waiting for transfers between devices  12.8 us (12%)
  local copies, waits for them, and re-layouts  2.63 us (3%)
    ppermute x21, starting transfers between devices, shift(): lax.ppermute(block, axis, [(i, (i + by) % count) for i in range(count)])  28.7 us
    all_to_all x1, blocking collectives, on_device(): pieces = lax.all_to_all(partial, CHIP_AXES, 0, 0)  18.4 us
    ppermute x21, waiting for transfers between devices, shift(): lax.ppermute(block, axis, [(i, (i + by) % count) for i in range(count)])  12.8 us
    all_to_all x1, blocking collectives, on_device(): lax.all_to_all(jnp.broadcast_to(sums[None], (2 * CHIPS, 8, TOK)), TP_AXES...  10.6 us
    pallas_call x2, Pallas kernels, cache_call(): pl.pallas_call(functools.partial(cache_kernel, first, [len(group) for gro...  8.48 us
    pallas_call x3, Pallas kernels, stats_call(): pl.pallas_call(functools.partial(stats_kernel, first, [len(group) for gro...  8.4 us
    pallas_call x1, Pallas kernels, project(): pl.pallas_call(project_kernel, out_shape=SHAPE((CHIPS, FEAT, TOK), jnp.bf...  3.91 us
    pallas_call x1, Pallas kernels, window_call(): pl.pallas_call(window_kernel, out_shape=out, in_specs=[SM] + [VM] * 6, ou...  3.19 us
  transfers between devices with their start and end apart: 21, of which 8 were waited for; matrix products, arithmetic and copies ran while one was open for 0% of the time, Pallas kernels for 19%

profile of v3, /device:TPU:1, one launch (start us, length us, event | category | flops | bytes accessed | tf_op | source)
XLA Modules:
  0.0 102.5 jit_solution(15873768301802758975)
XLA Ops:
  0.0 1.4 %collective-permute-start.12 = (bf16[8192,512]{1,0:T(8,128)(2,1)}, bf16[8192,512]{1,0:T(8,128)(2,1)}, u32[]{:S(2)}, u32[]{:S(2)}) collective-permute-start(bf16[8192,512]{1,0:T(8,128)(2,1)} %refs_0_.1), channel_id=1, source_target_pairs={{0,1},{1,0},{2,3},{3,2},{4,5},{5,4},{6,7},{7,6},{8,9},{9,8},{10,11... | collective-permute-start | bytes 25165832 | tf_op jit(solution)/shard_map/ppermute | solution.py:663
  2.1 0.1 stack.20.info_ref.idx_ref
  2.2 0.7 copy-done.5
  2.8 2.2 %pack_rows.1 = (bf16[576,256]{1,0:T(8,128)(2,1)S(1)}, bf16[512,128]{1,0:T(8,128)(2,1)S(1)}, bf16[512,128]{1,0:T(8,128)(2,1)S(1)}) custom-call(s32[5]{0:T(128)S(1)} %stack.20.info_ref.idx_ref, bf16[1024,1024]{1,0:T(8,128)(2,1)} %ck_ref.1, bf16[1024,1024]{1,0:T(8,128)(2,1)} %cv_ref.1, bf16[128,1024]{1,0:T(8,128)(2,1)} %raw_ref.1, bf16[128,1024]{1,0:T(8,128)(2,1)} %vw_ref.1, ...), custom_call_target="tpu_custom_call" | custom-call | tf_op jit(solution)/shard_map/pack_rows/pallas_call | solution.py:137
  5.1 2.9 %collective-permute-start = (bf16[576,256]{1,0:T(8,128)(2,1)S(1)}, bf16[576,256]{1,0:T(8,128)(2,1)S(1)}, u32[]{:S(2)}, u32[]{:S(2)}) collective-permute-start(bf16[576,256]{1,0:T(8,128)(2,1)S(1)} %get-tuple-element.56.refs_0_.refs_2_.refs_6_), channel_id=1, source_target_pairs={{0,16},{16,0},{1,17},{17,1},{2,18},{18,2},{3,19},{19,3},{4,20},{20... | collective-permute-start | bytes 884744 | tf_op jit(solution)/shard_map/ppermute | solution.py:663
  8.0 1.6 %collective-permute-start.2 = (bf16[576,256]{1,0:T(8,128)(2,1)S(1)}, bf16[576,256]{1,0:T(8,128)(2,1)S(1)}, u32[]{:S(2)}, u32[]{:S(2)}) collective-permute-start(bf16[576,256]{1,0:T(8,128)(2,1)S(1)} %get-tuple-element.56.refs_0_.refs_2_.refs_6_), channel_id=1, source_target_pairs={{0,32},{32,64},{64,96},{96,0},{1,33},{33,65},{65,97},{97,1},{2,34}... | collective-permute-start | bytes 884744 | tf_op jit(solution)/shard_map/ppermute | solution.py:663
  9.6 2.1 %collective-permute-start.1 = (bf16[576,256]{1,0:T(8,128)(2,1)S(1)}, bf16[576,256]{1,0:T(8,128)(2,1)S(1)}, u32[]{:S(2)}, u32[]{:S(2)}) collective-permute-start(bf16[576,256]{1,0:T(8,128)(2,1)S(1)} %get-tuple-element.56.refs_0_.refs_2_.refs_6_), channel_id=1, source_target_pairs={{0,96},{32,0},{64,32},{96,64},{1,97},{33,1},{65,33},{97,65},{2,98}... | collective-permute-start | bytes 884744 | tf_op jit(solution)/shard_map/ppermute | solution.py:663
  11.7 3.4 %collective-permute-done.refs_1_.refs_3_.refs_7_ = bf16[576,256]{1,0:T(8,128)(2,1)S(1)} collective-permute-done((bf16[576,256]{1,0:T(8,128)(2,1)S(1)}, bf16[576,256]{1,0:T(8,128)(2,1)S(1)}, u32[]{:S(2)}, u32[]{:S(2)}) %collective-permute-start) | collective-permute-done | bytes 294944 | tf_op jit(solution)/shard_map/ppermute | solution.py:663
  15.1 1.7 %collective-permute-start.6 = (bf16[576,256]{1,0:T(8,128)(2,1)S(1)}, bf16[576,256]{1,0:T(8,128)(2,1)S(1)}, u32[]{:S(2)}, u32[]{:S(2)}) collective-permute-start(bf16[576,256]{1,0:T(8,128)(2,1)S(1)} %collective-permute-done.refs_1_.refs_3_.refs_7_), channel_id=1, source_target_pairs={{0,32},{32,64},{64,96},{96,0},{1,33},{33,65},{65,97},{97,1},{2,34}... | collective-permute-start | bytes 884744 | tf_op jit(solution)/shard_map/ppermute | solution.py:663
  16.8 2.1 %collective-permute-start.5 = (bf16[576,256]{1,0:T(8,128)(2,1)S(1)}, bf16[576,256]{1,0:T(8,128)(2,1)S(1)}, u32[]{:S(2)}, u32[]{:S(2)}) collective-permute-start(bf16[576,256]{1,0:T(8,128)(2,1)S(1)} %collective-permute-done.refs_1_.refs_3_.refs_7_), channel_id=1, source_target_pairs={{0,96},{32,0},{64,32},{96,64},{1,97},{33,1},{65,33},{97,65},{2,98}... | collective-permute-start | bytes 884744 | tf_op jit(solution)/shard_map/ppermute | solution.py:663
  19.0 0.0 collective-permute-done.2.refs_3_.refs_5_.refs_9_
  19.0 1.2 %collective-permute-start.4 = (bf16[128,512]{1,0:T(8,128)(2,1)}, bf16[128,512]{1,0:T(8,128)(2,1)S(1)}, u32[]{:S(2)}, u32[]{:S(2)}) collective-permute-start(bf16[128,512]{1,0:T(8,128)(2,1)} %refs_5_.1), channel_id=1, source_target_pairs={{0,1},{1,0},{2,3},{3,2},{4,5},{5,4},{6,7},{7,6},{8,9},{9,8},{10,11... | collective-permute-start | bytes 393224 | tf_op jit(solution)/shard_map/ppermute | solution.py:663
  20.2 0.0 collective-permute-done.1.refs_2_.refs_4_.refs_8_
  20.2 0.1 collective-permute-start.3
  20.3 1.1 %collective-permute-done.4.refs_7_ = bf16[128,512]{1,0:T(8,128)(2,1)S(1)} collective-permute-done((bf16[128,512]{1,0:T(8,128)(2,1)}, bf16[128,512]{1,0:T(8,128)(2,1)S(1)}, u32[]{:S(2)}, u32[]{:S(2)}) %collective-permute-start.4) | collective-permute-done | bytes 131104 | tf_op jit(solution)/shard_map/ppermute | solution.py:663
  21.4 0.0 collective-permute-start.9
  21.4 0.4 collective-permute-done.3.refs_6_.pair_q_ref
  21.8 2.3 %collective-permute-start.10 = (bf16[288,256]{1,0:T(8,128)(2,1)S(1)}, bf16[288,256]{1,0:T(8,128)(2,1)S(1)}, u32[]{:S(2)}, u32[]{:S(2)}) collective-permute-start(bf16[288,256]{1,0:T(8,128)(2,1)S(1)} %slice.17), channel_id=1, source_target_pairs={{0,96},{32,0},{64,32},{96,64},{1,97},{33,1},{65,33},{97,65},{2,98}... | collective-permute-start | bytes 442376 | tf_op jit(solution)/shard_map/ppermute | solution.py:663
  24.1 0.9 copy-done.3
  25.0 0.9 copy-done.6
  25.9 2.0 %stats_0.1 = (bf16[1024,128]{1,0:T(8,128)(2,1)S(1)}, bf16[1024,128]{1,0:T(8,128)(2,1)S(1)}, f32[1024,128]{1,0:T(8,128)S(1)}, f32[1024,128]{1,0:T(8,128)S(1)}, f32[1024,128]{1,0:T(8,128)S(1)}) custom-call(s32[5]{0:T(128)S(1)} %stack.20.info_ref.idx_ref, bf16[576,256]{1,0:T(8,128)(2,1)S(1)} %get-tuple-element.56.refs_0_.refs_2_.refs_6_, ...), custom_call_target="tpu_custom_call" | custom-call | flops 1073741824 | bytes 3145728 | tf_op jit(solution)/shard_map/stats_0/pallas_call | solution.py:356
  27.9 0.0 collective-permute-done.6.refs_1_.refs_7_.refs_0_
  27.9 0.0 collective-permute-done.5.refs_0_.refs_6_.refs_10_
  27.9 0.0 slice-start.1
  27.9 0.6 collective-permute-done.9.refs_3_.refs_8_.refs_2_
  28.5 0.0 collective-permute-done.10.refs_2_.refs_1_
  28.5 3.4 %stats_4.1 = (f32[1024,128]{1,0:T(8,128)S(1)}, f32[1024,128]{1,0:T(8,128)S(1)}, f32[1024,128]{1,0:T(8,128)S(1)}) custom-call(s32[5]{0:T(128)S(1)} %stack.20.info_ref.idx_ref, bf16[576,256]{1,0:T(8,128)(2,1)S(1)} %collective-permute-done.5.refs_0_.refs_6_.refs_10_, bf16[576,256]{1,0:T(8,128)(2,1)S(1)} %collective-permute-done.6.refs_1_.refs_7_.refs_0_, ...), custom_call_target="tpu_custom_call" | custom-call | flops 805306368 | bytes 2883584 | tf_op jit(solution)/shard_map/stats_4/pallas_call | solution.py:356
  32.0 0.0 copy-done.1
  32.0 0.7 collective-permute-start.13
  32.7 0.1 collective-permute-start.14
  32.8 1.0 %collective-permute-start.8 = (bf16[288,256]{1,0:T(8,128)(2,1)S(1)}, bf16[288,256]{1,0:T(8,128)(2,1)S(1)}, u32[]{:S(2)}, u32[]{:S(2)}) collective-permute-start(bf16[288,256]{1,0:T(8,128)(2,1)S(1)} %slice.13), channel_id=1, source_target_pairs={{0,32},{32,64},{64,96},{96,0},{1,33},{33,65},{65,97},{97,1},{2,34}... | collective-permute-start | bytes 442376 | tf_op jit(solution)/shard_map/ppermute | solution.py:663
  33.8 1.7 %collective-permute-start.7 = (bf16[288,256]{1,0:T(8,128)(2,1)S(1)}, bf16[288,256]{1,0:T(8,128)(2,1)S(1)}, u32[]{:S(2)}, u32[]{:S(2)}) collective-permute-start(bf16[288,256]{1,0:T(8,128)(2,1)S(1)} %slice.12), channel_id=1, source_target_pairs={{0,96},{32,0},{64,32},{96,64},{1,97},{33,1},{65,33},{97,65},{2,98}... | collective-permute-start | bytes 442376 | tf_op jit(solution)/shard_map/ppermute | solution.py:663
  35.5 3.6 %collective-permute-done.8.refs_1_.refs_4_ = bf16[288,256]{1,0:T(8,128)(2,1)S(1)} collective-permute-done((bf16[288,256]{1,0:T(8,128)(2,1)S(1)}, bf16[288,256]{1,0:T(8,128)(2,1)S(1)}, u32[]{:S(2)}, u32[]{:S(2)}) %collective-permute-start.8) | collective-permute-done | bytes 147488 | tf_op jit(solution)/shard_map/ppermute | solution.py:663
  39.1 0.0 collective-permute-done.7.refs_0_.refs_3_
  39.1 3.0 %stats_7.1 = (f32[1024,128]{1,0:T(8,128)S(1)}, bf16[512,128]{1,0:T(8,128)(2,1)S(1)}, bf16[512,128]{1,0:T(8,128)(2,1)S(1)}) custom-call(s32[5]{0:T(128)S(1)} %stack.20.info_ref.idx_ref, bf16[288,256]{1,0:T(8,128)(2,1)S(1)} %collective-permute-done.7.refs_0_.refs_3_, bf16[288,256]{1,0:T(8,128)(2,1)S(1)} %collective-permute-done.8.refs_1_.refs_4_, ...), custom_call_target="tpu_custom_call" | custom-call | flops 536870912 | bytes 2621440 | tf_op jit(solution)/shard_map/stats_7/pallas_call | solution.py:356
  42.1 1.3 %collective-permute-start.11 = (f32[1024,128]{1,0:T(8,128)S(1)}, f32[1024,128]{1,0:T(8,128)S(1)}, u32[]{:S(2)}, u32[]{:S(2)}) collective-permute-start(f32[1024,128]{1,0:T(8,128)S(1)} %get-tuple-element.75.mine_ref), channel_id=1, source_target_pairs={{0,1},{1,0},{2,3},{3,2},{4,5},{5,4},{6,7},{7,6},{8,9},{9,8},{10,11... | collective-permute-start | bytes 1572872 | tf_op jit(solution)/shard_map/ppermute | solution.py:663
  43.4 1.5 %collective-permute-done.11.pair_ref = f32[1024,128]{1,0:T(8,128)S(1)} collective-permute-done((f32[1024,128]{1,0:T(8,128)S(1)}, f32[1024,128]{1,0:T(8,128)S(1)}, u32[]{:S(2)}, u32[]{:S(2)}) %collective-permute-start.11) | collective-permute-done | bytes 524320 | tf_op jit(solution)/shard_map/ppermute | solution.py:663
  45.0 0.0 collective-permute-done.13.refs_4_
  45.0 0.0 collective-permute-done.14.refs_5_
  45.0 0.0 collective-permute-done.12.refs_3_
  45.0 3.2 %window_grads.1 = (f32[1024,128]{1,0:T(8,128)S(1)}, f32[1024,128]{1,0:T(8,128)S(1)}, f32[1024,128]{1,0:T(8,128)S(1)}, f32[128,256]{1,0:T(8,128)S(1)}, f32[128,25...) custom-call(s32[5]{0:T(128)S(1)} %stack.20.info_ref.idx_ref, ...), custom_call_target="tpu_custom_call" | custom-call | flops 671088640 | bytes 2359296 | tf_op jit(solution)/shard_map/window_grads/pallas_call | solution.py:419
  48.2 0.4 collective-permute-start.15
  48.5 2.4 %collective-permute-start.16 = (f32[128,256]{1,0:T(8,128)S(1)}, f32[128,256]{1,0:T(8,128)S(1)}, u32[]{:S(2)}, u32[]{:S(2)}) collective-permute-start(f32[128,256]{1,0:T(8,128)S(1)} %get-tuple-element.83), channel_id=1, source_target_pairs={{0,96},{32,0},{64,32},{96,64},{1,97},{33,1},{65,33},{97,65},{2,98}... | collective-permute-start | bytes 393224 | tf_op jit(solution)/shard_map/ppermute | solution.py:663
  50.9 0.4 collective-permute-start.17
  51.3 0.0 copy-start.4
  51.3 4.6 %cache_grads_0.1 = (f32[1024,128]{1,0:T(8,128)S(1)}, bf16[8,512,1024]{2,1,0:T(8,128)(2,1)S(1)}, bf16[8,256,512]{2,1,0:T(8,128)(2,1)S(1)}) custom-call(s32[5]{0:T(128)S(1)} %stack.20.info_ref.idx_ref, bf16[8192,512]{1,0:T(8,128)(2,1)S(1)} %bitcast.8, bf16[64,8192]{1,0:T(8,128)(2,1)S(1)} %bitcast.10, bf16[64,8192]{1,0:T(8,128)(2,1)S(1)} %bitcast.12, ...), custom_call_target="tpu_custom_call" | custom-call | flops 2013265920 | bytes 3407872 | tf_op jit(solution)/shard_map/cache_grads_0/pallas_call | solution.py:493
  55.9 0.0 collective-permute-done.15.b_ref
  55.9 0.0 collective-permute-done.16.c_ref
  55.9 1.0 collective-permute-done.17.d_ref
  57.0 0.6 sum_parts.1
  57.5 2.8 %collective-permute-start.18 = (f32[64,256]{1,0:T(8,128)S(1)}, f32[64,256]{1,0:T(8,128)S(1)}, u32[]{:S(2)}, u32[]{:S(2)}) collective-permute-start(f32[64,256]{1,0:T(8,128)S(1)} %get-tuple-element.96), channel_id=1, source_target_pairs={{0,16},{16,0},{1,17},{17,1},{2,18},{18,2},{3,19},{19,3},{4,20},{20... | collective-permute-start | bytes 196616 | tf_op jit(solution)/shard_map/ppermute | solution.py:663
  60.4 3.9 %cache_grads_5.1.dq_ref = f32[1024,128]{1,0:T(8,128)S(1)} custom-call(s32[5]{0:T(128)S(1)} %stack.20.info_ref.idx_ref, bf16[576,256]{1,0:T(8,128)(2,1)S(1)} %collective-permute-done.6.refs_1_.refs_7_.refs_0_, bf16[288,256]{1,0:T(8,128)(2,1)S(1)} %collective-permute-done.10.refs_2_.refs_1_, ...), custom_call_target="tpu_custom_call" | custom-call | flops 1207959552 | bytes 2883584 | tf_op jit(solution)/shard_map/cache_grads_5/pallas_call | solution.py:493
  64.3 0.0 collective-permute-done.18.other_ref
  64.3 2.0 %collective-permute-start.19 = (f32[1024,128]{1,0:T(8,128)S(1)}, f32[1024,128]{1,0:T(8,128)S(1)}, u32[]{:S(2)}, u32[]{:S(2)}) collective-permute-start(f32[1024,128]{1,0:T(8,128)S(1)} %cache_grads_5.1.dq_ref), channel_id=1, source_target_pairs={{0,1},{1,0},{2,3},{3,2},{4,5},{5,4},{6,7},{7,6},{8,9},{9,8},{10,11... | collective-permute-start | bytes 1572872 | tf_op jit(solution)/shard_map/ppermute | solution.py:663
  66.3 0.0 copy-done
  66.3 0.6 own_kv.1.kv_ref
  66.9 0.3 collective-permute-start.20
  67.2 1.2 %collective-permute-done.20.pair_kv_ref = bf16[64,256]{1,0:T(8,128)(2,1)S(1)} collective-permute-done((bf16[64,256]{1,0:T(8,128)(2,1)S(1)}, bf16[64,256]{1,0:T(8,128)(2,1)S(1)}, u32[]{:S(2)}, u32[]{:S(2)}) %collective-permute-start.20) | collective-permute-done | bytes 32800 | tf_op jit(solution)/shard_map/ppermute | solution.py:663
  68.4 0.0 collective-permute-done.19.pair_dq_ref
  68.4 3.9 %project.1 = bf16[8,512,128]{2,1,0:T(8,128)(2,1)S(1)} custom-call(s32[5]{0:T(128)S(1)} %stack.20.info_ref.idx_ref, f32[1024,128]{1,0:T(8,128)S(1)} %cache_grads_5.1.dq_ref, f32[1024,128]{1,0:T(8,128)S(1)} %collective-permute-done.19.pair_dq_ref, bf16[128,512]{1,0:T(8,128)(2,1)S(1)} %copy-done.4, ...), custom_call_target="tpu_custom_call" | custom-call | flops 1342177280 | bytes 12000000 | tf_op jit(solution)/shard_map/project/pallas_call | solution.py:597
  72.3 18.4 %all_to_all.10.pieces_ref = bf16[8,512,128]{2,1,0:T(8,128)(2,1)S(1)} all-to-all(bf16[8,512,128]{2,1,0:T(8,128)(2,1)S(1)} %project.1), channel_id=1, replica_groups=mesh['z'=4,'xh'=2,'xl'=2,'y'=4,'c'=2] {'xl','y'}, dimensions={0} | all-to-all | bytes 2097152 | tf_op jit(solution)/shard_map/all_to_all | solution.py:741
  90.7 0.2 row_sums.1
  91.0 10.6 %all_to_all.11.sums_ref = f32[16,8,128]{2,1,0:T(8,128)S(1)} all-to-all(f32[16,8,128]{2,1,0:T(8,128)S(1)} %broadcast_in_dim.2), channel_id=1, replica_groups=mesh['z'=4,'xh'=2,'xl'=2,'y'=4,'c'=2] {'xl','y','c'}, dimensions={0} | all-to-all | bytes 131072 | tf_op jit(solution)/shard_map/all_to_all | solution.py:743
  101.6 0.9 last_norm.1
  (17 shorter events, 0.1 us)
Async XLA Ops:
  0.0 32.7 %copy-start.2 = (bf16[8192,64]{0,1:T(8,128)(2,1)S(1)}, bf16[8192,64]{0,1:T(8,128)(2,1)}, u32[]{:S(2)}) copy-start(bf16[8192,64]{0,1:T(8,128)(2,1)} %param.17) | copy-start | bytes 3145732
  0.0 32.0 %copy-start.1 = (bf16[8192,64]{0,1:T(8,128)(2,1)S(1)}, bf16[8192,64]{0,1:T(8,128)(2,1)}, u32[]{:S(2)}) copy-start(bf16[8192,64]{0,1:T(8,128)(2,1)} %param.16) | copy-start | bytes 3145732
  0.0 45.0 %collective-permute-start.12 = (bf16[8192,512]{1,0:T(8,128)(2,1)}, bf16[8192,512]{1,0:T(8,128)(2,1)}, u32[]{:S(2)}, u32[]{:S(2)}) collective-permute-start(bf16[8192,512]{1,0:T(8,128)(2,1)} %refs_0_.1), channel_id=1, source_target_pairs={{0,1},{1,0},{2,3},{3,2},{4,5},{5,4},{6,7},{7,6},{8,9},{9,8},{10,11... | collective-permute-start | bytes 25165832 | tf_op jit(solution)/shard_map/ppermute | solution.py:663
  2.2 0.7 copy-start.5
  2.8 48.5 %slice-start = ((s8[8388608]{0:T(1024)(128)(4,1)}), s8[4194304]{0:T(1024)(128)(4,1)S(1)}, s32[]{:S(2)}) async-start(s8[8388608]{0:T(1024)(128)(4,1)} %bitcast.7), calls=%async_computation.2 | async-start | bytes 8388608
  5.1 10.0 %collective-permute-start = (bf16[576,256]{1,0:T(8,128)(2,1)S(1)}, bf16[576,256]{1,0:T(8,128)(2,1)S(1)}, u32[]{:S(2)}, u32[]{:S(2)}) collective-permute-start(bf16[576,256]{1,0:T(8,128)(2,1)S(1)} %get-tuple-element.56.refs_0_.refs_2_.refs_6_), channel_id=1, source_target_pairs={{0,16},{16,0},{1,17},{17,1},{2,18},{18,2},{3,19},{19,3},{4,20},{20... | collective-permute-start | bytes 884744 | tf_op jit(solution)/shard_map/ppermute | solution.py:663
  8.0 11.0 %collective-permute-start.2 = (bf16[576,256]{1,0:T(8,128)(2,1)S(1)}, bf16[576,256]{1,0:T(8,128)(2,1)S(1)}, u32[]{:S(2)}, u32[]{:S(2)}) collective-permute-start(bf16[576,256]{1,0:T(8,128)(2,1)S(1)} %get-tuple-element.56.refs_0_.refs_2_.refs_6_), channel_id=1, source_target_pairs={{0,32},{32,64},{64,96},{96,0},{1,33},{33,65},{65,97},{97,1},{2,34}... | collective-permute-start | bytes 884744 | tf_op jit(solution)/shard_map/ppermute | solution.py:663
  9.6 10.6 %collective-permute-start.1 = (bf16[576,256]{1,0:T(8,128)(2,1)S(1)}, bf16[576,256]{1,0:T(8,128)(2,1)S(1)}, u32[]{:S(2)}, u32[]{:S(2)}) collective-permute-start(bf16[576,256]{1,0:T(8,128)(2,1)S(1)} %get-tuple-element.56.refs_0_.refs_2_.refs_6_), channel_id=1, source_target_pairs={{0,96},{32,0},{64,32},{96,64},{1,97},{33,1},{65,33},{97,65},{2,98}... | collective-permute-start | bytes 884744 | tf_op jit(solution)/shard_map/ppermute | solution.py:663
  15.1 12.7 %collective-permute-start.6 = (bf16[576,256]{1,0:T(8,128)(2,1)S(1)}, bf16[576,256]{1,0:T(8,128)(2,1)S(1)}, u32[]{:S(2)}, u32[]{:S(2)}) collective-permute-start(bf16[576,256]{1,0:T(8,128)(2,1)S(1)} %collective-permute-done.refs_1_.refs_3_.refs_7_), channel_id=1, source_target_pairs={{0,32},{32,64},{64,96},{96,0},{1,33},{33,65},{65,97},{97,1},{2,34}... | collective-permute-start | bytes 884744 | tf_op jit(solution)/shard_map/ppermute | solution.py:663
  16.8 11.0 %collective-permute-start.5 = (bf16[576,256]{1,0:T(8,128)(2,1)S(1)}, bf16[576,256]{1,0:T(8,128)(2,1)S(1)}, u32[]{:S(2)}, u32[]{:S(2)}) collective-permute-start(bf16[576,256]{1,0:T(8,128)(2,1)S(1)} %collective-permute-done.refs_1_.refs_3_.refs_7_), channel_id=1, source_target_pairs={{0,96},{32,0},{64,32},{96,64},{1,97},{33,1},{65,33},{97,65},{2,98}... | collective-permute-start | bytes 884744 | tf_op jit(solution)/shard_map/ppermute | solution.py:663
  19.0 2.4 %collective-permute-start.4 = (bf16[128,512]{1,0:T(8,128)(2,1)}, bf16[128,512]{1,0:T(8,128)(2,1)S(1)}, u32[]{:S(2)}, u32[]{:S(2)}) collective-permute-start(bf16[128,512]{1,0:T(8,128)(2,1)} %refs_5_.1), channel_id=1, source_target_pairs={{0,1},{1,0},{2,3},{3,2},{4,5},{5,4},{6,7},{7,6},{8,9},{9,8},{10,11... | collective-permute-start | bytes 393224 | tf_op jit(solution)/shard_map/ppermute | solution.py:663
  20.2 1.6 %collective-permute-start.3 = (bf16[128,512]{1,0:T(8,128)(2,1)}, bf16[128,512]{1,0:T(8,128)(2,1)S(1)}, u32[]{:S(2)}, u32[]{:S(2)}) collective-permute-start(bf16[128,512]{1,0:T(8,128)(2,1)} %q_ref.1), channel_id=1, source_target_pairs={{0,1},{1,0},{2,3},{3,2},{4,5},{5,4},{6,7},{7,6},{8,9},{9,8},{10,11... | collective-permute-start | bytes 393224 | tf_op jit(solution)/shard_map/ppermute | solution.py:663
  21.4 7.1 %collective-permute-start.9 = (bf16[288,256]{1,0:T(8,128)(2,1)S(1)}, bf16[288,256]{1,0:T(8,128)(2,1)S(1)}, u32[]{:S(2)}, u32[]{:S(2)}) collective-permute-start(bf16[288,256]{1,0:T(8,128)(2,1)S(1)} %slice.16), channel_id=1, source_target_pairs={{0,32},{32,64},{64,96},{96,0},{1,33},{33,65},{65,97},{97,1},{2,34}... | collective-permute-start | bytes 442376 | tf_op jit(solution)/shard_map/ppermute | solution.py:663
  21.8 6.7 %collective-permute-start.10 = (bf16[288,256]{1,0:T(8,128)(2,1)S(1)}, bf16[288,256]{1,0:T(8,128)(2,1)S(1)}, u32[]{:S(2)}, u32[]{:S(2)}) collective-permute-start(bf16[288,256]{1,0:T(8,128)(2,1)S(1)} %slice.17), channel_id=1, source_target_pairs={{0,96},{32,0},{64,32},{96,64},{1,97},{33,1},{65,33},{97,65},{2,98}... | collective-permute-start | bytes 442376 | tf_op jit(solution)/shard_map/ppermute | solution.py:663
  24.1 0.9 copy-start.3
  25.0 0.9 copy-start.6
  27.9 23.4 %slice-start.1 = ((s8[8388608]{0:T(1024)(128)(4,1)}), s8[4194304]{0:T(1024)(128)(4,1)S(1)}, s32[]{:S(2)}) async-start(s8[8388608]{0:T(1024)(128)(4,1)} %bitcast.7), calls=%async_computation.3 | async-start | bytes 8388608
  32.0 13.0 %collective-permute-start.13 = (bf16[64,8192]{1,0:T(8,128)(2,1)S(1)}, bf16[64,8192]{1,0:T(8,128)(2,1)S(1)}, u32[]{:S(2)}, u32[]{:S(2)}) collective-permute-start(bf16[64,8192]{1,0:T(8,128)(2,1)S(1)} %bitcast.9), channel_id=1, source_target_pairs={{0,1},{1,0},{2,3},{3,2},{4,5},{5,4},{6,7},{7,6},{8,9},{9,8},{10,11... | collective-permute-start | bytes 3145736 | tf_op jit(solution)/shard_map/ppermute | solution.py:663
  32.7 12.3 %collective-permute-start.14 = (bf16[64,8192]{1,0:T(8,128)(2,1)S(1)}, bf16[64,8192]{1,0:T(8,128)(2,1)S(1)}, u32[]{:S(2)}, u32[]{:S(2)}) collective-permute-start(bf16[64,8192]{1,0:T(8,128)(2,1)S(1)} %bitcast.11), channel_id=1, source_target_pairs={{0,1},{1,0},{2,3},{3,2},{4,5},{5,4},{6,7},{7,6},{8,9},{9,8},{10,11... | collective-permute-start | bytes 3145736 | tf_op jit(solution)/shard_map/ppermute | solution.py:663
  32.8 6.3 %collective-permute-start.8 = (bf16[288,256]{1,0:T(8,128)(2,1)S(1)}, bf16[288,256]{1,0:T(8,128)(2,1)S(1)}, u32[]{:S(2)}, u32[]{:S(2)}) collective-permute-start(bf16[288,256]{1,0:T(8,128)(2,1)S(1)} %slice.13), channel_id=1, source_target_pairs={{0,32},{32,64},{64,96},{96,0},{1,33},{33,65},{65,97},{97,1},{2,34}... | collective-permute-start | bytes 442376 | tf_op jit(solution)/shard_map/ppermute | solution.py:663
  33.8 5.3 %collective-permute-start.7 = (bf16[288,256]{1,0:T(8,128)(2,1)S(1)}, bf16[288,256]{1,0:T(8,128)(2,1)S(1)}, u32[]{:S(2)}, u32[]{:S(2)}) collective-permute-start(bf16[288,256]{1,0:T(8,128)(2,1)S(1)} %slice.12), channel_id=1, source_target_pairs={{0,96},{32,0},{64,32},{96,64},{1,97},{33,1},{65,33},{97,65},{2,98}... | collective-permute-start | bytes 442376 | tf_op jit(solution)/shard_map/ppermute | solution.py:663
  42.1 2.9 %collective-permute-start.11 = (f32[1024,128]{1,0:T(8,128)S(1)}, f32[1024,128]{1,0:T(8,128)S(1)}, u32[]{:S(2)}, u32[]{:S(2)}) collective-permute-start(f32[1024,128]{1,0:T(8,128)S(1)} %get-tuple-element.75.mine_ref), channel_id=1, source_target_pairs={{0,1},{1,0},{2,3},{3,2},{4,5},{5,4},{6,7},{7,6},{8,9},{9,8},{10,11... | collective-permute-start | bytes 1572872 | tf_op jit(solution)/shard_map/ppermute | solution.py:663
  48.2 7.8 %collective-permute-start.15 = (f32[128,256]{1,0:T(8,128)S(1)}, f32[128,256]{1,0:T(8,128)S(1)}, u32[]{:S(2)}, u32[]{:S(2)}) collective-permute-start(f32[128,256]{1,0:T(8,128)S(1)} %get-tuple-element.82), channel_id=1, source_target_pairs={{0,32},{32,64},{64,96},{96,0},{1,33},{33,65},{65,97},{97,1},{2,34}... | collective-permute-start | bytes 393224 | tf_op jit(solution)/shard_map/ppermute | solution.py:663
  48.5 7.4 %collective-permute-start.16 = (f32[128,256]{1,0:T(8,128)S(1)}, f32[128,256]{1,0:T(8,128)S(1)}, u32[]{:S(2)}, u32[]{:S(2)}) collective-permute-start(f32[128,256]{1,0:T(8,128)S(1)} %get-tuple-element.83), channel_id=1, source_target_pairs={{0,96},{32,0},{64,32},{96,64},{1,97},{33,1},{65,33},{97,65},{2,98}... | collective-permute-start | bytes 393224 | tf_op jit(solution)/shard_map/ppermute | solution.py:663
  50.9 6.0 %collective-permute-start.17 = (f32[128,256]{1,0:T(8,128)S(1)}, f32[128,256]{1,0:T(8,128)S(1)}, u32[]{:S(2)}, u32[]{:S(2)}) collective-permute-start(f32[128,256]{1,0:T(8,128)S(1)} %get-tuple-element.84), channel_id=1, source_target_pairs={{0,64},{32,96},{64,0},{96,32},{1,65},{33,97},{65,1},{97,33},{2,66}... | collective-permute-start | bytes 393224 | tf_op jit(solution)/shard_map/ppermute | solution.py:663
  51.3 14.9 %copy-start = (bf16[128,1024]{1,0:T(8,128)(2,1)S(1)}, bf16[128,1024]{1,0:T(8,128)(2,1)}, u32[]{:S(2)}) copy-start(bf16[128,1024]{1,0:T(8,128)(2,1)} %raw_ref.1) | copy-start | bytes 786436
  51.3 17.1 %copy-start.4 = (bf16[128,512]{1,0:T(8,128)(2,1)S(1)}, bf16[128,512]{1,0:T(8,128)(2,1)}, u32[]{:S(2)}) copy-start(bf16[128,512]{1,0:T(8,128)(2,1)} %q_ref.1) | copy-start | bytes 393220
  57.5 6.7 %collective-permute-start.18 = (f32[64,256]{1,0:T(8,128)S(1)}, f32[64,256]{1,0:T(8,128)S(1)}, u32[]{:S(2)}, u32[]{:S(2)}) collective-permute-start(f32[64,256]{1,0:T(8,128)S(1)} %get-tuple-element.96), channel_id=1, source_target_pairs={{0,16},{16,0},{1,17},{17,1},{2,18},{18,2},{3,19},{19,3},{4,20},{20... | collective-permute-start | bytes 196616 | tf_op jit(solution)/shard_map/ppermute | solution.py:663
  64.3 4.1 %collective-permute-start.19 = (f32[1024,128]{1,0:T(8,128)S(1)}, f32[1024,128]{1,0:T(8,128)S(1)}, u32[]{:S(2)}, u32[]{:S(2)}) collective-permute-start(f32[1024,128]{1,0:T(8,128)S(1)} %cache_grads_5.1.dq_ref), channel_id=1, source_target_pairs={{0,1},{1,0},{2,3},{3,2},{4,5},{5,4},{6,7},{7,6},{8,9},{9,8},{10,11... | collective-permute-start | bytes 1572872 | tf_op jit(solution)/shard_map/ppermute | solution.py:663
  66.9 1.5 %collective-permute-start.20 = (bf16[64,256]{1,0:T(8,128)(2,1)S(1)}, bf16[64,256]{1,0:T(8,128)(2,1)S(1)}, u32[]{:S(2)}, u32[]{:S(2)}) collective-permute-start(bf16[64,256]{1,0:T(8,128)(2,1)S(1)} %own_kv.1.kv_ref), channel_id=1, source_target_pairs={{0,1},{1,0},{2,3},{3,2},{4,5},{5,4},{6,7},{7,6},{8,9},{9,8},{10,11... | collective-permute-start | bytes 98312 | tf_op jit(solution)/shard_map/ppermute | solution.py:663

commit v4 on v3

--- a/solution.py
+++ b/solution.py
@@ -25,7 +25,6 @@
 HALF_CACHE = CACHE // CTX // 2
 HALF_WIN = TOK // 2
 HALF = HALF_CACHE + HALF_WIN
-CUT = HALF // 2
 KB = 512
 CHUNK = 512
 CHUNKS = ROWS // CHUNK
@@ -92,10 +91,14 @@
     vw_ref,
     resid_ref,
     dh_ref,
+    q_ref,
+    do_ref,
     gain_ref,
     out_ref,
     resid_out,
     dh_out,
+    q_out,
+    do_out,
     ck_s,
     kr_s,
     resid_s,
@@ -117,6 +120,8 @@
         ),
         pltpu.make_async_copy(resid_ref, resid_s, sems.at[4]),
         pltpu.make_async_copy(dh_ref, dh_s, sems.at[5]),
+        pltpu.make_async_copy(q_ref, q_out, sems.at[6]),
+        pltpu.make_async_copy(do_ref, do_out, sems.at[7]),
     ]
     for copy in copies:
         copy.start()
@@ -131,28 +136,32 @@
     resid_out[...] = resid_s[...].astype(jnp.float32).T.astype(jnp.bfloat16)
     copies[5].wait()
     dh_out[...] = dh_s[...].astype(jnp.float32).T.astype(jnp.bfloat16)
-
-
-def pack_rows(info, cache_k, cache_v, k_raw, v_win, resid, dh, gain):
+    copies[6].wait()
+    copies[7].wait()
+
+
+def pack_rows(info, *operands):
     return pl.pallas_call(
         pack_kernel,
         out_shape=[
             SHAPE((HALF, 2 * HD), jnp.bfloat16),
             SHAPE((FEAT, TOK), jnp.bfloat16),
             SHAPE((FEAT, TOK), jnp.bfloat16),
+            SHAPE((TOK, COLS), jnp.bfloat16),
+            SHAPE((TOK, COLS), jnp.bfloat16),
         ],
-        in_specs=[SM] + [HB] * 6 + [VM],
-        out_specs=[VM] * 3,
+        in_specs=[SM] + [HB] * 8 + [VM],
+        out_specs=[VM] * 5,
         scratch_shapes=[
             pltpu.VMEM((HALF_CACHE, HD), jnp.bfloat16),
             pltpu.VMEM((HALF_WIN, HD), jnp.bfloat16),
             pltpu.VMEM((TOK, FEAT), jnp.bfloat16),
             pltpu.VMEM((TOK, FEAT), jnp.bfloat16),
-            pltpu.SemaphoreType.DMA((6,)),
+            pltpu.SemaphoreType.DMA((8,)),
         ],
         compiler_params=SMALL,
         name="pack_rows",
-    )(info, cache_k, cache_v, k_raw, v_win, resid, dh, gain)
+    )(info, *operands)
 
 
 def cost(flops, exps, moved):
@@ -279,7 +288,7 @@
     else:
         wins = []
         if last:
-            wins = [refs.pop(0) for _ in range(CTX - 1)]
+            wins = [refs.pop(0) for _ in range(first)]
         q_s, do_s, m_in, l_in, w_in = refs[:5]
         if last:
             stat_ref, wk_ref, wv_ref = refs[5:8]
@@ -312,7 +321,7 @@
 
     cache_loop(info_ref, first, len(groups), core, body)
     if last:
-        for n, piece in enumerate(wins + [pieces[-1][-1]]):
+        for n, piece in enumerate(wins + [group[-1] for group in pieces]):
             at = pl.multiple_of(source(info_ref, *HOPS[n]) * HALF_WIN, HALF_WIN)
             low = piece.shape[0] - HALF_WIN
             wk_ref[pl.ds(at, HALF_WIN), :] = piece[low:, :HD]
@@ -693,36 +702,34 @@
     ).astype(jnp.int32)
     gain = s_qk.reshape(1, HD)
 
-    sources = [cache_k, cache_v, k_raw, v_win, residual_in, dh_rest]
+    sources = [cache_k, cache_v, k_raw, v_win, residual_in, dh_rest, q_raw, d_attn]
     sources = [pltpu.with_memory_space_constraint(array, pltpu.HBM) for array in sources]
-    here, resid_t, dh_t = pack_rows(info, *sources, gain)
+    here, resid_t, dh_t, q_own, do_own = pack_rows(info, *sources, gain)
     there = swap(here, "xh")
     up = shift(here, "z", -1)
     down = shift(here, "z", 1)
     pair_wide = swap(w_query, "c")
-    pair_q = swap(q_raw, "c")
-    pair_do = swap(d_attn, "c")
+    there, late_q, late_do = lax.optimization_barrier((there, q_own, do_own))
+    pair_q = swap(late_q, "c")
+    pair_do = swap(late_do, "c")
     up_there = shift(there, "z", -1)
     down_there = shift(there, "z", 1)
-    far = [shift(up[:CUT], "z", -1), shift(down[CUT:], "z", 1)]
+    far = shift(up, "z", -1)
     groups = [[here], [there], [up], [down]]
+    narrow = [w_key.T, w_value.T]
+    narrow, pair_do, pair_wide = lax.optimization_barrier((narrow, pair_do, pair_wide))
+    pair_weights = [pair_wide] + [swap(w, "c") for w in narrow]
     query, dout, *state = stats_call(
-        0, info, groups[:4], [q_raw, d_attn, pair_q, pair_do, gain]
-    )
-    query, dout, state, up_there, down_there = lax.optimization_barrier(
-        (query, dout, state, up_there, down_there)
-    )
-    far_there = [shift(up_there[:CUT], "z", -1), shift(down_there[CUT:], "z", 1)]
-    groups += [[up_there], [down_there], far, far_there]
-    state = stats_call(4, info, groups[4:7], [query, dout, *state])
-    narrow = [w_key.T, w_value.T]
-    state, narrow = lax.optimization_barrier((state, narrow))
-    weights = [w_query, *narrow]
-    pair_weights = [pair_wide] + [swap(w, "c") for w in narrow]
-    wins = [group[-1] for group in groups[:-1]]
+        0, info, groups[:4], [q_own, do_own, pair_q, pair_do, gain]
+    )
+    far_there = shift(down_there, "z", 1)
+    groups += [[up_there], [down_there], [far], [far_there]]
+    state = stats_call(4, info, groups[4:6], [query, dout, *state])
+    wins = [group[-1] for group in groups[:6]]
     stat, win_k, win_v = stats_call(
-        7, info, groups[7:], wins + [query, dout, *state], last=True
-    )
+        6, info, groups[6:], wins + [query, dout, *state], last=True
+    )
+    weights = [pltpu.with_memory_space_constraint(w_query, pltpu.HBM), *narrow]
     pair_stat, pair_weights = lax.optimization_barrier((swap(stat, "c"), pair_weights))
     lse, delta, dq, *parts = window_call(info, stat, pair_stat, query, dout, win_k, win_v)
     parts = [parts[0]] + [shift(parts[dz], "z", dz) for dz in (1, 3, 2)]
@@ -737,7 +744,7 @@
     pair_dq = swap(dq, "c")
     kv = own_kv(info, keep, other, k_raw, gain)
     pair_kv = swap(kv, "c")
-    partial = project(info, dq, pair_dq, q_raw, pair_q, gain, kv, pair_kv, w_own, w_kv)
+    partial = project(info, dq, pair_dq, q_own, pair_q, gain, kv, pair_kv, w_own, w_kv)
     pieces = lax.all_to_all(partial, CHIP_AXES, 0, 0)
     grad_t, sums = row_sums(pieces, resid_t, dh_t)
     everyone = lax.all_to_all(

time: 103 us -> 99.1 us (0.962)
  starting transfers between devices: 28.7 us -> 25 us
  waiting for transfers between devices: 12.8 us -> 14.7 us
  local copies, waits for them, and re-layouts: 2.63 us -> 1.42 us
    ppermute x21 -> x19, starting transfers between devices: 28.7 us -> 25 us  [shift(): lax.ppermute(block, axis, [(i, (i + by) % count) for i in range(count)])]
    ppermute x21 -> x19, waiting for transfers between devices: 12.8 us -> 14.7 us  [shift(): lax.ppermute(block, axis, [(i, (i + by) % count) for i in range(count)])]
    unnamed x18 -> x10, local copies, waits for them, and re-layouts: 2.49 us -> 1.32 us
  transfers between devices with their start and end apart: 21 -> 19, of which waited for: 8 -> 9; matrix products, arithmetic and copies ran while one was open for 0% -> 0% of each run, Pallas kernels for 19% -> 19%
where the time goes in v4:
time: 99.1 us; the launch traced here: 98.9 us
  blocking collectives  29 us (29%)
  Pallas kernels  27.9 us (28%)
  starting transfers between devices  25 us (25%)
  waiting for transfers between devices  14.7 us (15%)
  local copies, waits for them, and re-layouts  1.42 us (1%)
    ppermute x19, starting transfers between devices, shift(): lax.ppermute(block, axis, [(i, (i + by) % count) for i in range(count)])  25 us
    all_to_all x1, blocking collectives, on_device(): pieces = lax.all_to_all(partial, CHIP_AXES, 0, 0)  18.4 us
    ppermute x19, waiting for transfers between devices, shift(): lax.ppermute(block, axis, [(i, (i + by) % count) for i in range(count)])  14.7 us
    all_to_all x1, blocking collectives, on_device(): lax.all_to_all(jnp.broadcast_to(sums[None], (2 * CHIPS, 8, TOK)), TP_AXES...  10.6 us
    pallas_call x2, Pallas kernels, cache_call(): pl.pallas_call(functools.partial(cache_kernel, first, [len(group) for gro...  8.35 us
    pallas_call x3, Pallas kernels, stats_call(): pl.pallas_call(functools.partial(stats_kernel, first, [len(group) for gro...  8.06 us
    pallas_call x1, Pallas kernels, project(): pl.pallas_call(project_kernel, out_shape=SHAPE((CHIPS, FEAT, TOK), jnp.bf...  3.91 us
    pallas_call x1, Pallas kernels, window_call(): pl.pallas_call(window_kernel, out_shape=out, in_specs=[SM] + [VM] * 6, ou...  3.21 us
  transfers between devices with their start and end apart: 19, of which 9 were waited for; matrix products, arithmetic and copies ran while one was open for 0% of the time, Pallas kernels for 19%

profile of v4, /device:TPU:1, one launch (start us, length us, event | category | flops | bytes accessed | tf_op | source)
XLA Modules:
  0.0 98.9 jit_solution(5415629505121382201)
XLA Ops:
  0.0 1.4 %collective-permute-start.9 = (bf16[8192,512]{1,0:T(8,128)(2,1)}, bf16[8192,512]{1,0:T(8,128)(2,1)}, u32[]{:S(2)}, u32[]{:S(2)}) collective-permute-start(bf16[8192,512]{1,0:T(8,128)(2,1)} %refs_0_.1), channel_id=1, source_target_pairs={{0,1},{1,0},{2,3},{3,2},{4,5},{5,4},{6,7},{7,6},{8,9},{9,8},{10,11... | collective-permute-start | bytes 25165832 | tf_op jit(solution)/shard_map/ppermute | solution.py:672
  2.1 0.1 stack.20.info_ref.idx_ref
  2.2 0.0 copy-start.3
  2.2 0.7 copy-done.3
  2.8 0.0 copy-start.1
  2.8 0.0 copy-start.2
  2.8 2.1 %pack_rows.1 = (bf16[576,256]{1,0:T(8,128)(2,1)S(1)}, bf16[512,128]{1,0:T(8,128)(2,1)S(1)}, bf16[512,128]{1,0:T(8,128)(2,1)S(1)}, bf16[128,512]{1,0:T(8,128)(2,1)S(1)}, bf16[128,512]{1,0:T(8,128)(2,1)S(1)}) custom-call(s32[5]{0:T(128)S(1)} %stack.20.info_ref.idx_ref, bf16[1024,1024]{1,0:T(8,128)(2,1)} %ck_ref.1, bf16[1024,1024]{1,0:T(8,128)(2,1)} %cv_ref.1, ...), custom_call_target="tpu_custom_call" | custom-call | tf_op jit(solution)/shard_map/pack_rows/pallas_call | solution.py:144
  4.9 2.9 %collective-permute-start.2 = (bf16[576,256]{1,0:T(8,128)(2,1)S(1)}, bf16[576,256]{1,0:T(8,128)(2,1)S(1)}, u32[]{:S(2)}, u32[]{:S(2)}) collective-permute-start(bf16[576,256]{1,0:T(8,128)(2,1)S(1)} %get-tuple-element.53.refs_0_.refs_2_.refs_6_), channel_id=1, source_target_pairs={{0,16},{16,0},{1,17},{17,1},{2,18},{18,2},{3,19},{19,3},{4,20},{20... | collective-permute-start | bytes 884744 | tf_op jit(solution)/shard_map/ppermute | solution.py:672
  7.8 1.6 %collective-permute-start.5 = (bf16[576,256]{1,0:T(8,128)(2,1)S(1)}, bf16[576,256]{1,0:T(8,128)(2,1)S(1)}, u32[]{:S(2)}, u32[]{:S(2)}) collective-permute-start(bf16[576,256]{1,0:T(8,128)(2,1)S(1)} %get-tuple-element.53.refs_0_.refs_2_.refs_6_), channel_id=1, source_target_pairs={{0,32},{32,64},{64,96},{96,0},{1,33},{33,65},{65,97},{97,1},{2,34}... | collective-permute-start | bytes 884744 | tf_op jit(solution)/shard_map/ppermute | solution.py:672
  9.4 2.1 %collective-permute-start = (bf16[576,256]{1,0:T(8,128)(2,1)S(1)}, bf16[576,256]{1,0:T(8,128)(2,1)S(1)}, u32[]{:S(2)}, u32[]{:S(2)}) collective-permute-start(bf16[576,256]{1,0:T(8,128)(2,1)S(1)} %get-tuple-element.53.refs_0_.refs_2_.refs_6_), channel_id=1, source_target_pairs={{0,96},{32,0},{64,32},{96,64},{1,97},{33,1},{65,33},{97,65},{2,98}... | collective-permute-start | bytes 884744 | tf_op jit(solution)/shard_map/ppermute | solution.py:672
  11.6 3.6 %collective-permute-done.2.refs_1_.refs_3_.refs_7_ = bf16[576,256]{1,0:T(8,128)(2,1)S(1)} collective-permute-done((bf16[576,256]{1,0:T(8,128)(2,1)S(1)}, bf16[576,256]{1,0:T(8,128)(2,1)S(1)}, u32[]{:S(2)}, u32[]{:S(2)}) %collective-permute-start.2) | collective-permute-done | bytes 294944 | tf_op jit(solution)/shard_map/ppermute | solution.py:672
  15.1 1.7 %collective-permute-start.3 = (bf16[576,256]{1,0:T(8,128)(2,1)S(1)}, bf16[576,256]{1,0:T(8,128)(2,1)S(1)}, u32[]{:S(2)}, u32[]{:S(2)}) collective-permute-start(bf16[576,256]{1,0:T(8,128)(2,1)S(1)} %collective-permute-done.2.refs_1_.refs_3_.refs_7_), channel_id=1, source_target_pairs={{0,32},{32,64},{64,96},{96,0},{1,33},{33,65},{65,97},{97,1},{2,34}... | collective-permute-start | bytes 884744 | tf_op jit(solution)/shard_map/ppermute | solution.py:672
  16.8 1.1 %collective-permute-start.8 = (bf16[128,512]{1,0:T(8,128)(2,1)S(1)}, bf16[128,512]{1,0:T(8,128)(2,1)S(1)}, u32[]{:S(2)}, u32[]{:S(2)}) collective-permute-start(bf16[128,512]{1,0:T(8,128)(2,1)S(1)} %get-tuple-element.58.refs_5_), channel_id=1, source_target_pairs={{0,1},{1,0},{2,3},{3,2},{4,5},{5,4},{6,7},{7,6},{8,9},{9,8},{10,11... | collective-permute-start | bytes 393224 | tf_op jit(solution)/shard_map/ppermute | solution.py:672
  17.9 1.0 collective-permute-done.8.refs_7_
  18.9 0.0 collective-permute-done.9.refs_3_
  18.9 0.4 collective-permute-start.11
  19.3 0.1 collective-permute-start.12
  19.4 0.0 collective-permute-done.5.refs_3_.refs_5_.refs_9_
  19.4 0.4 collective-permute-start.7
  19.8 0.0 collective-permute-done.refs_2_.refs_4_.refs_8_
  19.8 1.8 %collective-permute-start.6 = (bf16[576,256]{1,0:T(8,128)(2,1)S(1)}, bf16[576,256]{1,0:T(8,128)(2,1)S(1)}, u32[]{:S(2)}, u32[]{:S(2)}) collective-permute-start(bf16[576,256]{1,0:T(8,128)(2,1)S(1)} %collective-permute-done.2.refs_1_.refs_3_.refs_7_), channel_id=1, source_target_pairs={{0,96},{32,0},{64,32},{96,64},{1,97},{33,1},{65,33},{97,65},{2,98}... | collective-permute-start | bytes 884744 | tf_op jit(solution)/shard_map/ppermute | solution.py:672
  21.6 0.3 collective-permute-done.7.refs_6_.pair_q_ref
  21.9 1.8 %collective-permute-start.1 = (bf16[576,256]{1,0:T(8,128)(2,1)S(1)}, bf16[576,256]{1,0:T(8,128)(2,1)S(1)}, u32[]{:S(2)}, u32[]{:S(2)}) collective-permute-start(bf16[576,256]{1,0:T(8,128)(2,1)S(1)} %collective-permute-done.refs_2_.refs_4_.refs_8_), channel_id=1, source_target_pairs={{0,96},{32,0},{64,32},{96,64},{1,97},{33,1},{65,33},{97,65},{2,98}... | collective-permute-start | bytes 884744 | tf_op jit(solution)/shard_map/ppermute | solution.py:672
  23.8 1.8 %collective-permute-done.3.refs_1_.refs_7_.refs_0_ = bf16[576,256]{1,0:T(8,128)(2,1)S(1)} collective-permute-done((bf16[576,256]{1,0:T(8,128)(2,1)S(1)}, bf16[576,256]{1,0:T(8,128)(2,1)S(1)}, u32[]{:S(2)}, u32[]{:S(2)}) %collective-permute-start.3) | collective-permute-done | bytes 294944 | tf_op jit(solution)/shard_map/ppermute | solution.py:672
  25.6 0.0 collective-permute-start.4
  25.6 0.0 copy-start.4
  25.6 0.7 copy-done.4
  26.2 2.0 %stats_0.1 = (bf16[1024,128]{1,0:T(8,128)(2,1)S(1)}, bf16[1024,128]{1,0:T(8,128)(2,1)S(1)}, f32[1024,128]{1,0:T(8,128)S(1)}, f32[1024,128]{1,0:T(8,128)S(1)}, f32[1024,128]{1,0:T(8,128)S(1)}) custom-call(s32[5]{0:T(128)S(1)} %stack.20.info_ref.idx_ref, bf16[576,256]{1,0:T(8,128)(2,1)S(1)} %get-tuple-element.53.refs_0_.refs_2_.refs_6_, ...), custom_call_target="tpu_custom_call" | custom-call | flops 1073741824 | bytes 3145728 | tf_op jit(solution)/shard_map/stats_0/pallas_call | solution.py:365
  28.2 0.4 collective-permute-done.6.refs_0_.refs_6_.refs_10_
  28.6 2.4 %stats_4.1 = (f32[1024,128]{1,0:T(8,128)S(1)}, f32[1024,128]{1,0:T(8,128)S(1)}, f32[1024,128]{1,0:T(8,128)S(1)}) custom-call(s32[5]{0:T(128)S(1)} %stack.20.info_ref.idx_ref, bf16[576,256]{1,0:T(8,128)(2,1)S(1)} %collective-permute-done.6.refs_0_.refs_6_.refs_10_, bf16[576,256]{1,0:T(8,128)(2,1)S(1)} %collective-permute-done.3.refs_1_.refs_7_.refs_0_, ...), custom_call_target="tpu_custom_call" | custom-call | flops 536870912 | bytes 2621440 | tf_op jit(solution)/shard_map/stats_4/pallas_call | solution.py:365
  31.0 3.9 %collective-permute-done.1.refs_0_.refs_1_ = bf16[576,256]{1,0:T(8,128)(2,1)S(1)} collective-permute-done((bf16[576,256]{1,0:T(8,128)(2,1)S(1)}, bf16[576,256]{1,0:T(8,128)(2,1)S(1)}, u32[]{:S(2)}, u32[]{:S(2)}) %collective-permute-start.1) | collective-permute-done | bytes 294944 | tf_op jit(solution)/shard_map/ppermute | solution.py:672
  34.9 0.0 collective-permute-done.4.refs_1_.refs_2_
  34.9 3.7 %stats_6.1 = (f32[1024,128]{1,0:T(8,128)S(1)}, bf16[512,128]{1,0:T(8,128)(2,1)S(1)}, bf16[512,128]{1,0:T(8,128)(2,1)S(1)}) custom-call(s32[5]{0:T(128)S(1)} %stack.20.info_ref.idx_ref, bf16[576,256]{1,0:T(8,128)(2,1)S(1)} %collective-permute-done.1.refs_0_.refs_1_, bf16[576,256]{1,0:T(8,128)(2,1)S(1)} %collective-permute-done.4.refs_1_.refs_2_, ...), custom_call_target="tpu_custom_call" | custom-call | flops 805306368 | bytes 2883584 | tf_op jit(solution)/shard_map/stats_6/pallas_call | solution.py:365
  38.6 1.5 %collective-permute-start.10 = (f32[1024,128]{1,0:T(8,128)S(1)}, f32[1024,128]{1,0:T(8,128)S(1)}, u32[]{:S(2)}, u32[]{:S(2)}) collective-permute-start(f32[1024,128]{1,0:T(8,128)S(1)} %get-tuple-element.68.mine_ref), channel_id=1, source_target_pairs={{0,1},{1,0},{2,3},{3,2},{4,5},{5,4},{6,7},{7,6},{8,9},{9,8},{10,11... | collective-permute-start | bytes 1572872 | tf_op jit(solution)/shard_map/ppermute | solution.py:672
  40.2 1.5 %collective-permute-done.10.pair_ref = f32[1024,128]{1,0:T(8,128)S(1)} collective-permute-done((f32[1024,128]{1,0:T(8,128)S(1)}, f32[1024,128]{1,0:T(8,128)S(1)}, u32[]{:S(2)}, u32[]{:S(2)}) %collective-permute-start.10) | collective-permute-done | bytes 524320 | tf_op jit(solution)/shard_map/ppermute | solution.py:672
  41.7 0.0 collective-permute-done.11.refs_4_
  41.7 0.0 collective-permute-done.12.refs_5_
  41.7 3.2 %window_grads.1 = (f32[1024,128]{1,0:T(8,128)S(1)}, f32[1024,128]{1,0:T(8,128)S(1)}, f32[1024,128]{1,0:T(8,128)S(1)}, f32[128,256]{1,0:T(8,128)S(1)}, f32[128,25...) custom-call(s32[5]{0:T(128)S(1)} %stack.20.info_ref.idx_ref, ...), custom_call_target="tpu_custom_call" | custom-call | flops 671088640 | bytes 2359296 | tf_op jit(solution)/shard_map/window_grads/pallas_call | solution.py:428
  44.9 1.0 %collective-permute-start.13 = (f32[128,256]{1,0:T(8,128)S(1)}, f32[128,256]{1,0:T(8,128)S(1)}, u32[]{:S(2)}, u32[]{:S(2)}) collective-permute-start(f32[128,256]{1,0:T(8,128)S(1)} %get-tuple-element.76), channel_id=1, source_target_pairs={{0,32},{32,64},{64,96},{96,0},{1,33},{33,65},{65,97},{97,1},{2,34}... | collective-permute-start | bytes 393224 | tf_op jit(solution)/shard_map/ppermute | solution.py:672
  45.9 1.7 %collective-permute-start.14 = (f32[128,256]{1,0:T(8,128)S(1)}, f32[128,256]{1,0:T(8,128)S(1)}, u32[]{:S(2)}, u32[]{:S(2)}) collective-permute-start(f32[128,256]{1,0:T(8,128)S(1)} %get-tuple-element.77), channel_id=1, source_target_pairs={{0,96},{32,0},{64,32},{96,64},{1,97},{33,1},{65,33},{97,65},{2,98}... | collective-permute-start | bytes 393224 | tf_op jit(solution)/shard_map/ppermute | solution.py:672
  47.7 0.3 collective-permute-start.15
  47.9 0.0 copy-done.1
  47.9 0.0 copy-done.2
  47.9 0.0 copy-start
  47.9 4.4 %cache_grads_0.1 = (f32[1024,128]{1,0:T(8,128)S(1)}, bf16[8,512,1024]{2,1,0:T(8,128)(2,1)S(1)}, bf16[8,256,512]{2,1,0:T(8,128)(2,1)S(1)}) custom-call(s32[5]{0:T(128)S(1)} %stack.20.info_ref.idx_ref, bf16[8192,512]{1,0:T(8,128)(2,1)} %refs_0_.1, bf16[64,8192]{1,0:T(8,128)(2,1)S(1)} %bitcast.8, bf16[64,8192]{1,0:T(8,128)(2,1)S(1)} %bitcast.10, ...), custom_call_target="tpu_custom_call" | custom-call | flops 2013265920 | bytes 3407872 | tf_op jit(solution)/shard_map/cache_grads_0/pallas_call | solution.py:502
  52.4 0.0 collective-permute-done.13.b_ref
  52.4 0.0 collective-permute-done.14.c_ref
  52.4 1.0 %collective-permute-done.15.d_ref = f32[128,256]{1,0:T(8,128)S(1)} collective-permute-done((f32[128,256]{1,0:T(8,128)S(1)}, f32[128,256]{1,0:T(8,128)S(1)}, u32[]{:S(2)}, u32[]{:S(2)}) %collective-permute-start.15) | collective-permute-done | bytes 131104 | tf_op jit(solution)/shard_map/ppermute | solution.py:672
  53.4 0.6 sum_parts.1
  54.0 2.8 %collective-permute-start.16 = (f32[64,256]{1,0:T(8,128)S(1)}, f32[64,256]{1,0:T(8,128)S(1)}, u32[]{:S(2)}, u32[]{:S(2)}) collective-permute-start(f32[64,256]{1,0:T(8,128)S(1)} %get-tuple-element.90), channel_id=1, source_target_pairs={{0,16},{16,0},{1,17},{17,1},{2,18},{18,2},{3,19},{19,3},{4,20},{20... | collective-permute-start | bytes 196616 | tf_op jit(solution)/shard_map/ppermute | solution.py:672
  56.8 3.9 %cache_grads_5.1.dq_ref = f32[1024,128]{1,0:T(8,128)S(1)} custom-call(s32[5]{0:T(128)S(1)} %stack.20.info_ref.idx_ref, bf16[576,256]{1,0:T(8,128)(2,1)S(1)} %collective-permute-done.3.refs_1_.refs_7_.refs_0_, bf16[576,256]{1,0:T(8,128)(2,1)S(1)} %collective-permute-done.1.refs_0_.refs_1_, bf16[576,256]{1,0:T(8,128)(2,1)S(1)} %collective-permute-done.4.refs_1_.refs_2_, ...), custom_call_target="tpu_custom_call" | custom-call | flops 1207959552 | bytes 2883584 | tf_op jit(solution)/shard_map/cache_grads_5/pallas_call | solution.py:502
  60.7 0.0 collective-permute-done.16.other_ref
  60.8 2.1 %collective-permute-start.17 = (f32[1024,128]{1,0:T(8,128)S(1)}, f32[1024,128]{1,0:T(8,128)S(1)}, u32[]{:S(2)}, u32[]{:S(2)}) collective-permute-start(f32[1024,128]{1,0:T(8,128)S(1)} %cache_grads_5.1.dq_ref), channel_id=1, source_target_pairs={{0,1},{1,0},{2,3},{3,2},{4,5},{5,4},{6,7},{7,6},{8,9},{9,8},{10,11... | collective-permute-start | bytes 1572872 | tf_op jit(solution)/shard_map/ppermute | solution.py:672
  62.9 0.0 copy-done
  62.9 0.6 own_kv.1.kv_ref
  63.5 0.1 collective-permute-start.18
  63.6 1.2 %collective-permute-done.18.pair_kv_ref = bf16[64,256]{1,0:T(8,128)(2,1)S(1)} collective-permute-done((bf16[64,256]{1,0:T(8,128)(2,1)S(1)}, bf16[64,256]{1,0:T(8,128)(2,1)S(1)}, u32[]{:S(2)}, u32[]{:S(2)}) %collective-permute-start.18) | collective-permute-done | bytes 32800 | tf_op jit(solution)/shard_map/ppermute | solution.py:672
  64.8 0.0 collective-permute-done.17.pair_dq_ref
  64.8 3.9 %project.1 = bf16[8,512,128]{2,1,0:T(8,128)(2,1)S(1)} custom-call(s32[5]{0:T(128)S(1)} %stack.20.info_ref.idx_ref, f32[1024,128]{1,0:T(8,128)S(1)} %cache_grads_5.1.dq_ref, f32[1024,128]{1,0:T(8,128)S(1)} %collective-permute-done.17.pair_dq_ref, bf16[128,512]{1,0:T(8,128)(2,1)S(1)} %get-tuple-element.57.refs_4_.q_ref, ...), custom_call_target="tpu_custom_call" | custom-call | flops 1342177280 | bytes 12000000 | tf_op jit(solution)/shard_map/project/pallas_call | solution.py:606
  68.7 18.4 %all_to_all.10.pieces_ref = bf16[8,512,128]{2,1,0:T(8,128)(2,1)S(1)} all-to-all(bf16[8,512,128]{2,1,0:T(8,128)(2,1)S(1)} %project.1), channel_id=1, replica_groups=mesh['z'=4,'xh'=2,'xl'=2,'y'=4,'c'=2] {'xl','y'}, dimensions={0} | all-to-all | bytes 2097152 | tf_op jit(solution)/shard_map/all_to_all | solution.py:748
  87.1 0.2 row_sums.1
  87.3 10.6 %all_to_all.11.sums_ref = f32[16,8,128]{2,1,0:T(8,128)S(1)} all-to-all(f32[16,8,128]{2,1,0:T(8,128)S(1)} %broadcast_in_dim.2), channel_id=1, replica_groups=mesh['z'=4,'xh'=2,'xl'=2,'y'=4,'c'=2] {'xl','y','c'}, dimensions={0} | all-to-all | bytes 131072 | tf_op jit(solution)/shard_map/all_to_all | solution.py:750
  98.0 0.9 last_norm.1
  (1 shorter events, 0.0 us)
Async XLA Ops:
  0.0 18.9 %collective-permute-start.9 = (bf16[8192,512]{1,0:T(8,128)(2,1)}, bf16[8192,512]{1,0:T(8,128)(2,1)}, u32[]{:S(2)}, u32[]{:S(2)}) collective-permute-start(bf16[8192,512]{1,0:T(8,128)(2,1)} %refs_0_.1), channel_id=1, source_target_pairs={{0,1},{1,0},{2,3},{3,2},{4,5},{5,4},{6,7},{7,6},{8,9},{9,8},{10,11... | collective-permute-start | bytes 25165832 | tf_op jit(solution)/shard_map/ppermute | solution.py:672
  2.2 0.7 copy-start.3
  2.8 45.1 %copy-start.1 = (bf16[8192,64]{0,1:T(8,128)(2,1)S(1)}, bf16[8192,64]{0,1:T(8,128)(2,1)}, u32[]{:S(2)}) copy-start(bf16[8192,64]{0,1:T(8,128)(2,1)} %param.16) | copy-start | bytes 3145732
  2.8 45.1 %copy-start.2 = (bf16[8192,64]{0,1:T(8,128)(2,1)S(1)}, bf16[8192,64]{0,1:T(8,128)(2,1)}, u32[]{:S(2)}) copy-start(bf16[8192,64]{0,1:T(8,128)(2,1)} %param.17) | copy-start | bytes 3145732
  4.9 10.2 %collective-permute-start.2 = (bf16[576,256]{1,0:T(8,128)(2,1)S(1)}, bf16[576,256]{1,0:T(8,128)(2,1)S(1)}, u32[]{:S(2)}, u32[]{:S(2)}) collective-permute-start(bf16[576,256]{1,0:T(8,128)(2,1)S(1)} %get-tuple-element.53.refs_0_.refs_2_.refs_6_), channel_id=1, source_target_pairs={{0,16},{16,0},{1,17},{17,1},{2,18},{18,2},{3,19},{19,3},{4,20},{20... | collective-permute-start | bytes 884744 | tf_op jit(solution)/shard_map/ppermute | solution.py:672
  7.8 11.6 %collective-permute-start.5 = (bf16[576,256]{1,0:T(8,128)(2,1)S(1)}, bf16[576,256]{1,0:T(8,128)(2,1)S(1)}, u32[]{:S(2)}, u32[]{:S(2)}) collective-permute-start(bf16[576,256]{1,0:T(8,128)(2,1)S(1)} %get-tuple-element.53.refs_0_.refs_2_.refs_6_), channel_id=1, source_target_pairs={{0,32},{32,64},{64,96},{96,0},{1,33},{33,65},{65,97},{97,1},{2,34}... | collective-permute-start | bytes 884744 | tf_op jit(solution)/shard_map/ppermute | solution.py:672
  9.4 10.3 %collective-permute-start = (bf16[576,256]{1,0:T(8,128)(2,1)S(1)}, bf16[576,256]{1,0:T(8,128)(2,1)S(1)}, u32[]{:S(2)}, u32[]{:S(2)}) collective-permute-start(bf16[576,256]{1,0:T(8,128)(2,1)S(1)} %get-tuple-element.53.refs_0_.refs_2_.refs_6_), channel_id=1, source_target_pairs={{0,96},{32,0},{64,32},{96,64},{1,97},{33,1},{65,33},{97,65},{2,98}... | collective-permute-start | bytes 884744 | tf_op jit(solution)/shard_map/ppermute | solution.py:672
  15.1 10.4 %collective-permute-start.3 = (bf16[576,256]{1,0:T(8,128)(2,1)S(1)}, bf16[576,256]{1,0:T(8,128)(2,1)S(1)}, u32[]{:S(2)}, u32[]{:S(2)}) collective-permute-start(bf16[576,256]{1,0:T(8,128)(2,1)S(1)} %collective-permute-done.2.refs_1_.refs_3_.refs_7_), channel_id=1, source_target_pairs={{0,32},{32,64},{64,96},{96,0},{1,33},{33,65},{65,97},{97,1},{2,34}... | collective-permute-start | bytes 884744 | tf_op jit(solution)/shard_map/ppermute | solution.py:672
  16.8 2.1 %collective-permute-start.8 = (bf16[128,512]{1,0:T(8,128)(2,1)S(1)}, bf16[128,512]{1,0:T(8,128)(2,1)S(1)}, u32[]{:S(2)}, u32[]{:S(2)}) collective-permute-start(bf16[128,512]{1,0:T(8,128)(2,1)S(1)} %get-tuple-element.58.refs_5_), channel_id=1, source_target_pairs={{0,1},{1,0},{2,3},{3,2},{4,5},{5,4},{6,7},{7,6},{8,9},{9,8},{10,11... | collective-permute-start | bytes 393224 | tf_op jit(solution)/shard_map/ppermute | solution.py:672
  18.9 22.8 %collective-permute-start.11 = (bf16[64,8192]{1,0:T(8,128)(2,1)}, bf16[64,8192]{1,0:T(8,128)(2,1)S(1)}, u32[]{:S(2)}, u32[]{:S(2)}) collective-permute-start(bf16[64,8192]{1,0:T(8,128)(2,1)} %bitcast.7), channel_id=1, source_target_pairs={{0,1},{1,0},{2,3},{3,2},{4,5},{5,4},{6,7},{7,6},{8,9},{9,8},{10,11... | collective-permute-start | bytes 3145736 | tf_op jit(solution)/shard_map/ppermute | solution.py:672
  19.3 22.4 %collective-permute-start.12 = (bf16[64,8192]{1,0:T(8,128)(2,1)}, bf16[64,8192]{1,0:T(8,128)(2,1)S(1)}, u32[]{:S(2)}, u32[]{:S(2)}) collective-permute-start(bf16[64,8192]{1,0:T(8,128)(2,1)} %bitcast.9), channel_id=1, source_target_pairs={{0,1},{1,0},{2,3},{3,2},{4,5},{5,4},{6,7},{7,6},{8,9},{9,8},{10,11... | collective-permute-start | bytes 3145736 | tf_op jit(solution)/shard_map/ppermute | solution.py:672
  19.4 2.5 %collective-permute-start.7 = (bf16[128,512]{1,0:T(8,128)(2,1)S(1)}, bf16[128,512]{1,0:T(8,128)(2,1)S(1)}, u32[]{:S(2)}, u32[]{:S(2)}) collective-permute-start(bf16[128,512]{1,0:T(8,128)(2,1)S(1)} %get-tuple-element.57.refs_4_.q_ref), channel_id=1, source_target_pairs={{0,1},{1,0},{2,3},{3,2},{4,5},{5,4},{6,7},{7,6},{8,9},{9,8},{10,11... | collective-permute-start | bytes 393224 | tf_op jit(solution)/shard_map/ppermute | solution.py:672
  19.8 8.8 %collective-permute-start.6 = (bf16[576,256]{1,0:T(8,128)(2,1)S(1)}, bf16[576,256]{1,0:T(8,128)(2,1)S(1)}, u32[]{:S(2)}, u32[]{:S(2)}) collective-permute-start(bf16[576,256]{1,0:T(8,128)(2,1)S(1)} %collective-permute-done.2.refs_1_.refs_3_.refs_7_), channel_id=1, source_target_pairs={{0,96},{32,0},{64,32},{96,64},{1,97},{33,1},{65,33},{97,65},{2,98}... | collective-permute-start | bytes 884744 | tf_op jit(solution)/shard_map/ppermute | solution.py:672
  21.9 13.0 %collective-permute-start.1 = (bf16[576,256]{1,0:T(8,128)(2,1)S(1)}, bf16[576,256]{1,0:T(8,128)(2,1)S(1)}, u32[]{:S(2)}, u32[]{:S(2)}) collective-permute-start(bf16[576,256]{1,0:T(8,128)(2,1)S(1)} %collective-permute-done.refs_2_.refs_4_.refs_8_), channel_id=1, source_target_pairs={{0,96},{32,0},{64,32},{96,64},{1,97},{33,1},{65,33},{97,65},{2,98}... | collective-permute-start | bytes 884744 | tf_op jit(solution)/shard_map/ppermute | solution.py:672
  25.6 9.4 %collective-permute-start.4 = (bf16[576,256]{1,0:T(8,128)(2,1)S(1)}, bf16[576,256]{1,0:T(8,128)(2,1)S(1)}, u32[]{:S(2)}, u32[]{:S(2)}) collective-permute-start(bf16[576,256]{1,0:T(8,128)(2,1)S(1)} %collective-permute-done.3.refs_1_.refs_7_.refs_0_), channel_id=1, source_target_pairs={{0,32},{32,64},{64,96},{96,0},{1,33},{33,65},{65,97},{97,1},{2,34}... | collective-permute-start | bytes 884744 | tf_op jit(solution)/shard_map/ppermute | solution.py:672
  25.6 0.7 copy-start.4
  38.6 3.1 %collective-permute-start.10 = (f32[1024,128]{1,0:T(8,128)S(1)}, f32[1024,128]{1,0:T(8,128)S(1)}, u32[]{:S(2)}, u32[]{:S(2)}) collective-permute-start(f32[1024,128]{1,0:T(8,128)S(1)} %get-tuple-element.68.mine_ref), channel_id=1, source_target_pairs={{0,1},{1,0},{2,3},{3,2},{4,5},{5,4},{6,7},{7,6},{8,9},{9,8},{10,11... | collective-permute-start | bytes 1572872 | tf_op jit(solution)/shard_map/ppermute | solution.py:672
  44.9 7.5 %collective-permute-start.13 = (f32[128,256]{1,0:T(8,128)S(1)}, f32[128,256]{1,0:T(8,128)S(1)}, u32[]{:S(2)}, u32[]{:S(2)}) collective-permute-start(f32[128,256]{1,0:T(8,128)S(1)} %get-tuple-element.76), channel_id=1, source_target_pairs={{0,32},{32,64},{64,96},{96,0},{1,33},{33,65},{65,97},{97,1},{2,34}... | collective-permute-start | bytes 393224 | tf_op jit(solution)/shard_map/ppermute | solution.py:672
  45.9 6.5 %collective-permute-start.14 = (f32[128,256]{1,0:T(8,128)S(1)}, f32[128,256]{1,0:T(8,128)S(1)}, u32[]{:S(2)}, u32[]{:S(2)}) collective-permute-start(f32[128,256]{1,0:T(8,128)S(1)} %get-tuple-element.77), channel_id=1, source_target_pairs={{0,96},{32,0},{64,32},{96,64},{1,97},{33,1},{65,33},{97,65},{2,98}... | collective-permute-start | bytes 393224 | tf_op jit(solution)/shard_map/ppermute | solution.py:672
  47.7 5.8 %collective-permute-start.15 = (f32[128,256]{1,0:T(8,128)S(1)}, f32[128,256]{1,0:T(8,128)S(1)}, u32[]{:S(2)}, u32[]{:S(2)}) collective-permute-start(f32[128,256]{1,0:T(8,128)S(1)} %get-tuple-element.78), channel_id=1, source_target_pairs={{0,64},{32,96},{64,0},{96,32},{1,65},{33,97},{65,1},{97,33},{2,66}... | collective-permute-start | bytes 393224 | tf_op jit(solution)/shard_map/ppermute | solution.py:672
  47.9 14.9 %copy-start = (bf16[128,1024]{1,0:T(8,128)(2,1)S(1)}, bf16[128,1024]{1,0:T(8,128)(2,1)}, u32[]{:S(2)}) copy-start(bf16[128,1024]{1,0:T(8,128)(2,1)} %raw_ref.1) | copy-start | bytes 786436
  54.0 6.7 %collective-permute-start.16 = (f32[64,256]{1,0:T(8,128)S(1)}, f32[64,256]{1,0:T(8,128)S(1)}, u32[]{:S(2)}, u32[]{:S(2)}) collective-permute-start(f32[64,256]{1,0:T(8,128)S(1)} %get-tuple-element.90), channel_id=1, source_target_pairs={{0,16},{16,0},{1,17},{17,1},{2,18},{18,2},{3,19},{19,3},{4,20},{20... | collective-permute-start | bytes 196616 | tf_op jit(solution)/shard_map/ppermute | solution.py:672
  60.8 4.1 %collective-permute-start.17 = (f32[1024,128]{1,0:T(8,128)S(1)}, f32[1024,128]{1,0:T(8,128)S(1)}, u32[]{:S(2)}, u32[]{:S(2)}) collective-permute-start(f32[1024,128]{1,0:T(8,128)S(1)} %cache_grads_5.1.dq_ref), channel_id=1, source_target_pairs={{0,1},{1,0},{2,3},{3,2},{4,5},{5,4},{6,7},{7,6},{8,9},{9,8},{10,11... | collective-permute-start | bytes 1572872 | tf_op jit(solution)/shard_map/ppermute | solution.py:672
  63.5 1.3 %collective-permute-start.18 = (bf16[64,256]{1,0:T(8,128)(2,1)S(1)}, bf16[64,256]{1,0:T(8,128)(2,1)S(1)}, u32[]{:S(2)}, u32[]{:S(2)}) collective-permute-start(bf16[64,256]{1,0:T(8,128)(2,1)S(1)} %own_kv.1.kv_ref), channel_id=1, source_target_pairs={{0,1},{1,0},{2,3},{3,2},{4,5},{5,4},{6,7},{7,6},{8,9},{9,8},{10,11... | collective-permute-start | bytes 98312 | tf_op jit(solution)/shard_map/ppermute | solution.py:672

commit v5 on v4

--- a/solution.py
+++ b/solution.py
@@ -99,6 +99,7 @@
     dh_out,
     q_out,
     do_out,
+    gain_out,
     ck_s,
     kr_s,
     resid_s,
@@ -122,10 +123,12 @@
         pltpu.make_async_copy(dh_ref, dh_s, sems.at[5]),
         pltpu.make_async_copy(q_ref, q_out, sems.at[6]),
         pltpu.make_async_copy(do_ref, do_out, sems.at[7]),
+        pltpu.make_async_copy(gain_ref, gain_out, sems.at[8]),
     ]
     for copy in copies:
         copy.start()
-    gain = gain_ref[...]
+    copies[8].wait()
+    gain = gain_out[...]
     copies[0].wait()
     out_ref[:HALF_CACHE, :HD] = unit_rows(ck_s[...].astype(jnp.float32), gain).astype(jnp.bfloat16)
     copies[1].wait()
@@ -149,15 +152,16 @@
             SHAPE((FEAT, TOK), jnp.bfloat16),
             SHAPE((TOK, COLS), jnp.bfloat16),
             SHAPE((TOK, COLS), jnp.bfloat16),
+            SHAPE((1, HD), jnp.float32),
         ],
-        in_specs=[SM] + [HB] * 8 + [VM],
-        out_specs=[VM] * 5,
+        in_specs=[SM] + [HB] * 9,
+        out_specs=[VM] * 6,
         scratch_shapes=[
             pltpu.VMEM((HALF_CACHE, HD), jnp.bfloat16),
             pltpu.VMEM((HALF_WIN, HD), jnp.bfloat16),
             pltpu.VMEM((TOK, FEAT), jnp.bfloat16),
             pltpu.VMEM((TOK, FEAT), jnp.bfloat16),
-            pltpu.SemaphoreType.DMA((8,)),
+            pltpu.SemaphoreType.DMA((9,)),
         ],
         compiler_params=SMALL,
         name="pack_rows",
@@ -700,11 +704,10 @@
             CACHE - cache_live[0],
         ]
     ).astype(jnp.int32)
-    gain = s_qk.reshape(1, HD)
-
     sources = [cache_k, cache_v, k_raw, v_win, residual_in, dh_rest, q_raw, d_attn]
+    sources.append(s_qk.reshape(1, HD))
     sources = [pltpu.with_memory_space_constraint(array, pltpu.HBM) for array in sources]
-    here, resid_t, dh_t, q_own, do_own = pack_rows(info, *sources, gain)
+    here, resid_t, dh_t, q_own, do_own, gain = pack_rows(info, *sources)
     there = swap(here, "xh")
     up = shift(here, "z", -1)
     down = shift(here, "z", 1)

time: 99.1 us -> 98.6 us (level)
  local copies, waits for them, and re-layouts: 1.42 us -> 0.1 us
    unnamed x10 -> x6, local copies, waits for them, and re-layouts: 1.32 us -> 0.01 us
  transfers between devices with their start and end apart: 19 -> 19, of which waited for: 9 -> 9; matrix products, arithmetic and copies ran while one was open for 0% -> 0% of each run, Pallas kernels for 19% -> 20%
where the time goes in v5:
time: 98.6 us; the launch traced here: 98.3 us
  blocking collectives  29 us (29%)
  Pallas kernels  28 us (28%)
  starting transfers between devices  25 us (25%)
  waiting for transfers between devices  15.4 us (16%)
    ppermute x19, starting transfers between devices, shift(): lax.ppermute(block, axis, [(i, (i + by) % count) for i in range(count)])  25 us
    all_to_all x1, blocking collectives, on_device(): pieces = lax.all_to_all(partial, CHIP_AXES, 0, 0)  18.4 us
    ppermute x19, waiting for transfers between devices, shift(): lax.ppermute(block, axis, [(i, (i + by) % count) for i in range(count)])  15.4 us
    all_to_all x1, blocking collectives, on_device(): lax.all_to_all(jnp.broadcast_to(sums[None], (2 * CHIPS, 8, TOK)), TP_AXES...  10.7 us
    pallas_call x2, Pallas kernels, cache_call(): pl.pallas_call(functools.partial(cache_kernel, first, [len(group) for gro...  8.35 us
    pallas_call x3, Pallas kernels, stats_call(): pl.pallas_call(functools.partial(stats_kernel, first, [len(group) for gro...  8.06 us
    pallas_call x1, Pallas kernels, project(): pl.pallas_call(project_kernel, out_shape=SHAPE((CHIPS, FEAT, TOK), jnp.bf...  3.91 us
    pallas_call x1, Pallas kernels, window_call(): pl.pallas_call(window_kernel, out_shape=out, in_specs=[SM] + [VM] * 6, ou...  3.19 us
  transfers between devices with their start and end apart: 19, of which 9 were waited for; matrix products, arithmetic and copies ran while one was open for 0% of the time, Pallas kernels for 20%

profile of v5, /device:TPU:1, one launch (start us, length us, event | category | flops | bytes accessed | tf_op | source)
XLA Modules:
  0.0 98.3 jit_solution(1772380295704909363)
XLA Ops:
  0.0 1.4 %collective-permute-start.9 = (bf16[8192,512]{1,0:T(8,128)(2,1)}, bf16[8192,512]{1,0:T(8,128)(2,1)}, u32[]{:S(2)}, u32[]{:S(2)}) collective-permute-start(bf16[8192,512]{1,0:T(8,128)(2,1)} %refs_0_.1), channel_id=1, source_target_pairs={{0,1},{1,0},{2,3},{3,2},{4,5},{5,4},{6,7},{7,6},{8,9},{9,8},{10,11... | collective-permute-start | bytes 25165832 | tf_op jit(solution)/shard_map/ppermute | solution.py:676
  2.1 0.1 stack.20.info_ref.idx_ref
  2.2 0.0 copy-start.1
  2.2 0.0 copy-start.2
  2.2 2.2 %pack_rows.1 = (bf16[576,256]{1,0:T(8,128)(2,1)S(1)}, bf16[512,128]{1,0:T(8,128)(2,1)S(1)}, bf16[512,128]{1,0:T(8,128)(2,1)S(1)}, bf16[128,512]{1,0:T(8,128)(2,1...) custom-call(s32[5]{0:T(128)S(1)} %stack.20.info_ref.idx_ref, bf16[1024,1024]{1,0:T(8,128)(2,1)} %ck_ref.1, ...), custom_call_target="tpu_custom_call" | custom-call | tf_op jit(solution)/shard_map/pack_rows/pallas_call | solution.py:147
  4.4 2.9 %collective-permute-start.2 = (bf16[576,256]{1,0:T(8,128)(2,1)S(1)}, bf16[576,256]{1,0:T(8,128)(2,1)S(1)}, u32[]{:S(2)}, u32[]{:S(2)}) collective-permute-start(bf16[576,256]{1,0:T(8,128)(2,1)S(1)} %get-tuple-element.54.refs_0_.refs_2_.refs_6_), channel_id=1, source_target_pairs={{0,16},{16,0},{1,17},{17,1},{2,18},{18,2},{3,19},{19,3},{4,20},{20... | collective-permute-start | bytes 884744 | tf_op jit(solution)/shard_map/ppermute | solution.py:676
  7.3 1.6 %collective-permute-start.5 = (bf16[576,256]{1,0:T(8,128)(2,1)S(1)}, bf16[576,256]{1,0:T(8,128)(2,1)S(1)}, u32[]{:S(2)}, u32[]{:S(2)}) collective-permute-start(bf16[576,256]{1,0:T(8,128)(2,1)S(1)} %get-tuple-element.54.refs_0_.refs_2_.refs_6_), channel_id=1, source_target_pairs={{0,32},{32,64},{64,96},{96,0},{1,33},{33,65},{65,97},{97,1},{2,34}... | collective-permute-start | bytes 884744 | tf_op jit(solution)/shard_map/ppermute | solution.py:676
  8.9 2.1 %collective-permute-start = (bf16[576,256]{1,0:T(8,128)(2,1)S(1)}, bf16[576,256]{1,0:T(8,128)(2,1)S(1)}, u32[]{:S(2)}, u32[]{:S(2)}) collective-permute-start(bf16[576,256]{1,0:T(8,128)(2,1)S(1)} %get-tuple-element.54.refs_0_.refs_2_.refs_6_), channel_id=1, source_target_pairs={{0,96},{32,0},{64,32},{96,64},{1,97},{33,1},{65,33},{97,65},{2,98}... | collective-permute-start | bytes 884744 | tf_op jit(solution)/shard_map/ppermute | solution.py:676
  11.0 3.6 %collective-permute-done.2.refs_1_.refs_3_.refs_7_ = bf16[576,256]{1,0:T(8,128)(2,1)S(1)} collective-permute-done((bf16[576,256]{1,0:T(8,128)(2,1)S(1)}, bf16[576,256]{1,0:T(8,128)(2,1)S(1)}, u32[]{:S(2)}, u32[]{:S(2)}) %collective-permute-start.2) | collective-permute-done | bytes 294944 | tf_op jit(solution)/shard_map/ppermute | solution.py:676
  14.6 1.7 %collective-permute-start.3 = (bf16[576,256]{1,0:T(8,128)(2,1)S(1)}, bf16[576,256]{1,0:T(8,128)(2,1)S(1)}, u32[]{:S(2)}, u32[]{:S(2)}) collective-permute-start(bf16[576,256]{1,0:T(8,128)(2,1)S(1)} %collective-permute-done.2.refs_1_.refs_3_.refs_7_), channel_id=1, source_target_pairs={{0,32},{32,64},{64,96},{96,0},{1,33},{33,65},{65,97},{97,1},{2,34}... | collective-permute-start | bytes 884744 | tf_op jit(solution)/shard_map/ppermute | solution.py:676
  16.3 1.1 %collective-permute-start.8 = (bf16[128,512]{1,0:T(8,128)(2,1)S(1)}, bf16[128,512]{1,0:T(8,128)(2,1)S(1)}, u32[]{:S(2)}, u32[]{:S(2)}) collective-permute-start(bf16[128,512]{1,0:T(8,128)(2,1)S(1)} %get-tuple-element.59.refs_5_), channel_id=1, source_target_pairs={{0,1},{1,0},{2,3},{3,2},{4,5},{5,4},{6,7},{7,6},{8,9},{9,8},{10,11... | collective-permute-start | bytes 393224 | tf_op jit(solution)/shard_map/ppermute | solution.py:676
  17.4 1.0 %collective-permute-done.8.refs_7_ = bf16[128,512]{1,0:T(8,128)(2,1)S(1)} collective-permute-done((bf16[128,512]{1,0:T(8,128)(2,1)S(1)}, bf16[128,512]{1,0:T(8,128)(2,1)S(1)}, u32[]{:S(2)}, u32[]{:S(2)}) %collective-permute-start.8) | collective-permute-done | bytes 131104 | tf_op jit(solution)/shard_map/ppermute | solution.py:676
  18.4 0.0 collective-permute-done.9.refs_3_
  18.4 0.4 collective-permute-start.11
  18.7 0.1 collective-permute-start.12
  18.9 0.0 collective-permute-done.5.refs_3_.refs_5_.refs_9_
  18.9 0.4 collective-permute-start.7
  19.3 0.0 collective-permute-done.refs_2_.refs_4_.refs_8_
  19.3 1.8 %collective-permute-start.6 = (bf16[576,256]{1,0:T(8,128)(2,1)S(1)}, bf16[576,256]{1,0:T(8,128)(2,1)S(1)}, u32[]{:S(2)}, u32[]{:S(2)}) collective-permute-start(bf16[576,256]{1,0:T(8,128)(2,1)S(1)} %collective-permute-done.2.refs_1_.refs_3_.refs_7_), channel_id=1, source_target_pairs={{0,96},{32,0},{64,32},{96,64},{1,97},{33,1},{65,33},{97,65},{2,98}... | collective-permute-start | bytes 884744 | tf_op jit(solution)/shard_map/ppermute | solution.py:676
  21.1 0.3 collective-permute-done.7.refs_6_.pair_q_ref
  21.4 1.8 %collective-permute-start.1 = (bf16[576,256]{1,0:T(8,128)(2,1)S(1)}, bf16[576,256]{1,0:T(8,128)(2,1)S(1)}, u32[]{:S(2)}, u32[]{:S(2)}) collective-permute-start(bf16[576,256]{1,0:T(8,128)(2,1)S(1)} %collective-permute-done.refs_2_.refs_4_.refs_8_), channel_id=1, source_target_pairs={{0,96},{32,0},{64,32},{96,64},{1,97},{33,1},{65,33},{97,65},{2,98}... | collective-permute-start | bytes 884744 | tf_op jit(solution)/shard_map/ppermute | solution.py:676
  23.3 1.8 %collective-permute-done.3.refs_1_.refs_7_.refs_0_ = bf16[576,256]{1,0:T(8,128)(2,1)S(1)} collective-permute-done((bf16[576,256]{1,0:T(8,128)(2,1)S(1)}, bf16[576,256]{1,0:T(8,128)(2,1)S(1)}, u32[]{:S(2)}, u32[]{:S(2)}) %collective-permute-start.3) | collective-permute-done | bytes 294944 | tf_op jit(solution)/shard_map/ppermute | solution.py:676
  25.0 0.0 collective-permute-start.4
  25.1 2.0 %stats_0.1 = (bf16[1024,128]{1,0:T(8,128)(2,1)S(1)}, bf16[1024,128]{1,0:T(8,128)(2,1)S(1)}, f32[1024,128]{1,0:T(8,128)S(1)}, f32[1024,128]{1,0:T(8,128)S(1)}, f32[1024,128]{1,0:T(8,128)S(1)}) custom-call(s32[5]{0:T(128)S(1)} %stack.20.info_ref.idx_ref, bf16[576,256]{1,0:T(8,128)(2,1)S(1)} %get-tuple-element.54.refs_0_.refs_2_.refs_6_, ...), custom_call_target="tpu_custom_call" | custom-call | flops 1073741824 | bytes 3145728 | tf_op jit(solution)/shard_map/stats_0/pallas_call | solution.py:369
  27.0 1.1 %collective-permute-done.6.refs_0_.refs_6_.refs_10_ = bf16[576,256]{1,0:T(8,128)(2,1)S(1)} collective-permute-done((bf16[576,256]{1,0:T(8,128)(2,1)S(1)}, bf16[576,256]{1,0:T(8,128)(2,1)S(1)}, u32[]{:S(2)}, u32[]{:S(2)}) %collective-permute-start.6) | collective-permute-done | bytes 294944 | tf_op jit(solution)/shard_map/ppermute | solution.py:676
  28.1 2.4 %stats_4.1 = (f32[1024,128]{1,0:T(8,128)S(1)}, f32[1024,128]{1,0:T(8,128)S(1)}, f32[1024,128]{1,0:T(8,128)S(1)}) custom-call(s32[5]{0:T(128)S(1)} %stack.20.info_ref.idx_ref, bf16[576,256]{1,0:T(8,128)(2,1)S(1)} %collective-permute-done.6.refs_0_.refs_6_.refs_10_, bf16[576,256]{1,0:T(8,128)(2,1)S(1)} %collective-permute-done.3.refs_1_.refs_7_.refs_0_, ...), custom_call_target="tpu_custom_call" | custom-call | flops 536870912 | bytes 2621440 | tf_op jit(solution)/shard_map/stats_4/pallas_call | solution.py:369
  30.5 3.9 %collective-permute-done.1.refs_0_.refs_1_ = bf16[576,256]{1,0:T(8,128)(2,1)S(1)} collective-permute-done((bf16[576,256]{1,0:T(8,128)(2,1)S(1)}, bf16[576,256]{1,0:T(8,128)(2,1)S(1)}, u32[]{:S(2)}, u32[]{:S(2)}) %collective-permute-start.1) | collective-permute-done | bytes 294944 | tf_op jit(solution)/shard_map/ppermute | solution.py:676
  34.4 0.0 collective-permute-done.4.refs_1_.refs_2_
  34.4 3.7 %stats_6.1 = (f32[1024,128]{1,0:T(8,128)S(1)}, bf16[512,128]{1,0:T(8,128)(2,1)S(1)}, bf16[512,128]{1,0:T(8,128)(2,1)S(1)}) custom-call(s32[5]{0:T(128)S(1)} %stack.20.info_ref.idx_ref, bf16[576,256]{1,0:T(8,128)(2,1)S(1)} %collective-permute-done.1.refs_0_.refs_1_, bf16[576,256]{1,0:T(8,128)(2,1)S(1)} %collective-permute-done.4.refs_1_.refs_2_, ...), custom_call_target="tpu_custom_call" | custom-call | flops 805306368 | bytes 2883584 | tf_op jit(solution)/shard_map/stats_6/pallas_call | solution.py:369
  38.1 1.5 %collective-permute-start.10 = (f32[1024,128]{1,0:T(8,128)S(1)}, f32[1024,128]{1,0:T(8,128)S(1)}, u32[]{:S(2)}, u32[]{:S(2)}) collective-permute-start(f32[1024,128]{1,0:T(8,128)S(1)} %get-tuple-element.70.mine_ref), channel_id=1, source_target_pairs={{0,1},{1,0},{2,3},{3,2},{4,5},{5,4},{6,7},{7,6},{8,9},{9,8},{10,11... | collective-permute-start | bytes 1572872 | tf_op jit(solution)/shard_map/ppermute | solution.py:676
  39.6 1.5 %collective-permute-done.10.pair_ref = f32[1024,128]{1,0:T(8,128)S(1)} collective-permute-done((f32[1024,128]{1,0:T(8,128)S(1)}, f32[1024,128]{1,0:T(8,128)S(1)}, u32[]{:S(2)}, u32[]{:S(2)}) %collective-permute-start.10) | collective-permute-done | bytes 524320 | tf_op jit(solution)/shard_map/ppermute | solution.py:676
  41.2 0.0 collective-permute-done.11.refs_4_
  41.2 0.0 collective-permute-done.12.refs_5_
  41.2 3.2 %window_grads.1 = (f32[1024,128]{1,0:T(8,128)S(1)}, f32[1024,128]{1,0:T(8,128)S(1)}, f32[1024,128]{1,0:T(8,128)S(1)}, f32[128,256]{1,0:T(8,128)S(1)}, f32[128,25...) custom-call(s32[5]{0:T(128)S(1)} %stack.20.info_ref.idx_ref, ...), custom_call_target="tpu_custom_call" | custom-call | flops 671088640 | bytes 2359296 | tf_op jit(solution)/shard_map/window_grads/pallas_call | solution.py:432
  44.4 1.0 %collective-permute-start.13 = (f32[128,256]{1,0:T(8,128)S(1)}, f32[128,256]{1,0:T(8,128)S(1)}, u32[]{:S(2)}, u32[]{:S(2)}) collective-permute-start(f32[128,256]{1,0:T(8,128)S(1)} %get-tuple-element.78), channel_id=1, source_target_pairs={{0,32},{32,64},{64,96},{96,0},{1,33},{33,65},{65,97},{97,1},{2,34}... | collective-permute-start | bytes 393224 | tf_op jit(solution)/shard_map/ppermute | solution.py:676
  45.4 1.7 %collective-permute-start.14 = (f32[128,256]{1,0:T(8,128)S(1)}, f32[128,256]{1,0:T(8,128)S(1)}, u32[]{:S(2)}, u32[]{:S(2)}) collective-permute-start(f32[128,256]{1,0:T(8,128)S(1)} %get-tuple-element.79), channel_id=1, source_target_pairs={{0,96},{32,0},{64,32},{96,64},{1,97},{33,1},{65,33},{97,65},{2,98}... | collective-permute-start | bytes 393224 | tf_op jit(solution)/shard_map/ppermute | solution.py:676
  47.1 0.3 collective-permute-start.15
  47.4 0.0 copy-done.1
  47.4 0.0 copy-done.2
  47.4 0.0 copy-start
  47.4 4.4 %cache_grads_0.1 = (f32[1024,128]{1,0:T(8,128)S(1)}, bf16[8,512,1024]{2,1,0:T(8,128)(2,1)S(1)}, bf16[8,256,512]{2,1,0:T(8,128)(2,1)S(1)}) custom-call(s32[5]{0:T(128)S(1)} %stack.20.info_ref.idx_ref, bf16[8192,512]{1,0:T(8,128)(2,1)} %refs_0_.1, bf16[64,8192]{1,0:T(8,128)(2,1)S(1)} %bitcast.8, bf16[64,8192]{1,0:T(8,128)(2,1)S(1)} %bitcast.10, ...), custom_call_target="tpu_custom_call" | custom-call | flops 2013265920 | bytes 3407872 | tf_op jit(solution)/shard_map/cache_grads_0/pallas_call | solution.py:506
  51.8 0.0 collective-permute-done.13.b_ref
  51.9 0.0 collective-permute-done.14.c_ref
  51.9 1.0 %collective-permute-done.15.d_ref = f32[128,256]{1,0:T(8,128)S(1)} collective-permute-done((f32[128,256]{1,0:T(8,128)S(1)}, f32[128,256]{1,0:T(8,128)S(1)}, u32[]{:S(2)}, u32[]{:S(2)}) %collective-permute-start.15) | collective-permute-done | bytes 131104 | tf_op jit(solution)/shard_map/ppermute | solution.py:676
  52.9 0.6 sum_parts.1
  53.5 2.8 %collective-permute-start.16 = (f32[64,256]{1,0:T(8,128)S(1)}, f32[64,256]{1,0:T(8,128)S(1)}, u32[]{:S(2)}, u32[]{:S(2)}) collective-permute-start(f32[64,256]{1,0:T(8,128)S(1)} %get-tuple-element.92), channel_id=1, source_target_pairs={{0,16},{16,0},{1,17},{17,1},{2,18},{18,2},{3,19},{19,3},{4,20},{20... | collective-permute-start | bytes 196616 | tf_op jit(solution)/shard_map/ppermute | solution.py:676
  56.3 3.9 %cache_grads_5.1.dq_ref = f32[1024,128]{1,0:T(8,128)S(1)} custom-call(s32[5]{0:T(128)S(1)} %stack.20.info_ref.idx_ref, bf16[576,256]{1,0:T(8,128)(2,1)S(1)} %collective-permute-done.3.refs_1_.refs_7_.refs_0_, bf16[576,256]{1,0:T(8,128)(2,1)S(1)} %collective-permute-done.1.refs_0_.refs_1_, bf16[576,256]{1,0:T(8,128)(2,1)S(1)} %collective-permute-done.4.refs_1_.refs_2_, ...), custom_call_target="tpu_custom_call" | custom-call | flops 1207959552 | bytes 2883584 | tf_op jit(solution)/shard_map/cache_grads_5/pallas_call | solution.py:506
  60.2 0.0 collective-permute-done.16.other_ref
  60.2 2.1 %collective-permute-start.17 = (f32[1024,128]{1,0:T(8,128)S(1)}, f32[1024,128]{1,0:T(8,128)S(1)}, u32[]{:S(2)}, u32[]{:S(2)}) collective-permute-start(f32[1024,128]{1,0:T(8,128)S(1)} %cache_grads_5.1.dq_ref), channel_id=1, source_target_pairs={{0,1},{1,0},{2,3},{3,2},{4,5},{5,4},{6,7},{7,6},{8,9},{9,8},{10,11... | collective-permute-start | bytes 1572872 | tf_op jit(solution)/shard_map/ppermute | solution.py:676
  62.3 0.0 copy-done
  62.3 0.6 own_kv.1.kv_ref
  63.0 0.1 collective-permute-start.18
  63.1 1.2 %collective-permute-done.18.pair_kv_ref = bf16[64,256]{1,0:T(8,128)(2,1)S(1)} collective-permute-done((bf16[64,256]{1,0:T(8,128)(2,1)S(1)}, bf16[64,256]{1,0:T(8,128)(2,1)S(1)}, u32[]{:S(2)}, u32[]{:S(2)}) %collective-permute-start.18) | collective-permute-done | bytes 32800 | tf_op jit(solution)/shard_map/ppermute | solution.py:676
  64.3 0.0 collective-permute-done.17.pair_dq_ref
  64.3 3.9 %project.1 = bf16[8,512,128]{2,1,0:T(8,128)(2,1)S(1)} custom-call(s32[5]{0:T(128)S(1)} %stack.20.info_ref.idx_ref, f32[1024,128]{1,0:T(8,128)S(1)} %cache_grads_5.1.dq_ref, f32[1024,128]{1,0:T(8,128)S(1)} %collective-permute-done.17.pair_dq_ref, bf16[128,512]{1,0:T(8,128)(2,1)S(1)} %get-tuple-element.58.refs_4_.q_ref, ...), custom_call_target="tpu_custom_call" | custom-call | flops 1342177280 | bytes 12000000 | tf_op jit(solution)/shard_map/project/pallas_call | solution.py:610
  68.2 18.4 %all_to_all.10.pieces_ref = bf16[8,512,128]{2,1,0:T(8,128)(2,1)S(1)} all-to-all(bf16[8,512,128]{2,1,0:T(8,128)(2,1)S(1)} %project.1), channel_id=1, replica_groups=mesh['z'=4,'xh'=2,'xl'=2,'y'=4,'c'=2] {'xl','y'}, dimensions={0} | all-to-all | bytes 2097152 | tf_op jit(solution)/shard_map/all_to_all | solution.py:751
  86.5 0.2 row_sums.1
  86.8 10.7 %all_to_all.11.sums_ref = f32[16,8,128]{2,1,0:T(8,128)S(1)} all-to-all(f32[16,8,128]{2,1,0:T(8,128)S(1)} %broadcast_in_dim.2), channel_id=1, replica_groups=mesh['z'=4,'xh'=2,'xl'=2,'y'=4,'c'=2] {'xl','y','c'}, dimensions={0} | all-to-all | bytes 131072 | tf_op jit(solution)/shard_map/all_to_all | solution.py:753
  97.4 0.9 last_norm.1
  (1 shorter events, 0.0 us)
Async XLA Ops:
  0.0 18.4 %collective-permute-start.9 = (bf16[8192,512]{1,0:T(8,128)(2,1)}, bf16[8192,512]{1,0:T(8,128)(2,1)}, u32[]{:S(2)}, u32[]{:S(2)}) collective-permute-start(bf16[8192,512]{1,0:T(8,128)(2,1)} %refs_0_.1), channel_id=1, source_target_pairs={{0,1},{1,0},{2,3},{3,2},{4,5},{5,4},{6,7},{7,6},{8,9},{9,8},{10,11... | collective-permute-start | bytes 25165832 | tf_op jit(solution)/shard_map/ppermute | solution.py:676
  2.2 45.2 %copy-start.1 = (bf16[8192,64]{0,1:T(8,128)(2,1)S(1)}, bf16[8192,64]{0,1:T(8,128)(2,1)}, u32[]{:S(2)}) copy-start(bf16[8192,64]{0,1:T(8,128)(2,1)} %param.16) | copy-start | bytes 3145732
  2.2 45.2 %copy-start.2 = (bf16[8192,64]{0,1:T(8,128)(2,1)S(1)}, bf16[8192,64]{0,1:T(8,128)(2,1)}, u32[]{:S(2)}) copy-start(bf16[8192,64]{0,1:T(8,128)(2,1)} %param.17) | copy-start | bytes 3145732
  4.4 10.2 %collective-permute-start.2 = (bf16[576,256]{1,0:T(8,128)(2,1)S(1)}, bf16[576,256]{1,0:T(8,128)(2,1)S(1)}, u32[]{:S(2)}, u32[]{:S(2)}) collective-permute-start(bf16[576,256]{1,0:T(8,128)(2,1)S(1)} %get-tuple-element.54.refs_0_.refs_2_.refs_6_), channel_id=1, source_target_pairs={{0,16},{16,0},{1,17},{17,1},{2,18},{18,2},{3,19},{19,3},{4,20},{20... | collective-permute-start | bytes 884744 | tf_op jit(solution)/shard_map/ppermute | solution.py:676
  7.3 11.6 %collective-permute-start.5 = (bf16[576,256]{1,0:T(8,128)(2,1)S(1)}, bf16[576,256]{1,0:T(8,128)(2,1)S(1)}, u32[]{:S(2)}, u32[]{:S(2)}) collective-permute-start(bf16[576,256]{1,0:T(8,128)(2,1)S(1)} %get-tuple-element.54.refs_0_.refs_2_.refs_6_), channel_id=1, source_target_pairs={{0,32},{32,64},{64,96},{96,0},{1,33},{33,65},{65,97},{97,1},{2,34}... | collective-permute-start | bytes 884744 | tf_op jit(solution)/shard_map/ppermute | solution.py:676
  8.9 10.3 %collective-permute-start = (bf16[576,256]{1,0:T(8,128)(2,1)S(1)}, bf16[576,256]{1,0:T(8,128)(2,1)S(1)}, u32[]{:S(2)}, u32[]{:S(2)}) collective-permute-start(bf16[576,256]{1,0:T(8,128)(2,1)S(1)} %get-tuple-element.54.refs_0_.refs_2_.refs_6_), channel_id=1, source_target_pairs={{0,96},{32,0},{64,32},{96,64},{1,97},{33,1},{65,33},{97,65},{2,98}... | collective-permute-start | bytes 884744 | tf_op jit(solution)/shard_map/ppermute | solution.py:676
  14.6 10.4 %collective-permute-start.3 = (bf16[576,256]{1,0:T(8,128)(2,1)S(1)}, bf16[576,256]{1,0:T(8,128)(2,1)S(1)}, u32[]{:S(2)}, u32[]{:S(2)}) collective-permute-start(bf16[576,256]{1,0:T(8,128)(2,1)S(1)} %collective-permute-done.2.refs_1_.refs_3_.refs_7_), channel_id=1, source_target_pairs={{0,32},{32,64},{64,96},{96,0},{1,33},{33,65},{65,97},{97,1},{2,34}... | collective-permute-start | bytes 884744 | tf_op jit(solution)/shard_map/ppermute | solution.py:676
  16.3 2.1 %collective-permute-start.8 = (bf16[128,512]{1,0:T(8,128)(2,1)S(1)}, bf16[128,512]{1,0:T(8,128)(2,1)S(1)}, u32[]{:S(2)}, u32[]{:S(2)}) collective-permute-start(bf16[128,512]{1,0:T(8,128)(2,1)S(1)} %get-tuple-element.59.refs_5_), channel_id=1, source_target_pairs={{0,1},{1,0},{2,3},{3,2},{4,5},{5,4},{6,7},{7,6},{8,9},{9,8},{10,11... | collective-permute-start | bytes 393224 | tf_op jit(solution)/shard_map/ppermute | solution.py:676
  18.4 22.8 %collective-permute-start.11 = (bf16[64,8192]{1,0:T(8,128)(2,1)}, bf16[64,8192]{1,0:T(8,128)(2,1)S(1)}, u32[]{:S(2)}, u32[]{:S(2)}) collective-permute-start(bf16[64,8192]{1,0:T(8,128)(2,1)} %bitcast.7), channel_id=1, source_target_pairs={{0,1},{1,0},{2,3},{3,2},{4,5},{5,4},{6,7},{7,6},{8,9},{9,8},{10,11... | collective-permute-start | bytes 3145736 | tf_op jit(solution)/shard_map/ppermute | solution.py:676
  18.7 22.4 %collective-permute-start.12 = (bf16[64,8192]{1,0:T(8,128)(2,1)}, bf16[64,8192]{1,0:T(8,128)(2,1)S(1)}, u32[]{:S(2)}, u32[]{:S(2)}) collective-permute-start(bf16[64,8192]{1,0:T(8,128)(2,1)} %bitcast.9), channel_id=1, source_target_pairs={{0,1},{1,0},{2,3},{3,2},{4,5},{5,4},{6,7},{7,6},{8,9},{9,8},{10,11... | collective-permute-start | bytes 3145736 | tf_op jit(solution)/shard_map/ppermute | solution.py:676
  18.9 2.5 %collective-permute-start.7 = (bf16[128,512]{1,0:T(8,128)(2,1)S(1)}, bf16[128,512]{1,0:T(8,128)(2,1)S(1)}, u32[]{:S(2)}, u32[]{:S(2)}) collective-permute-start(bf16[128,512]{1,0:T(8,128)(2,1)S(1)} %get-tuple-element.58.refs_4_.q_ref), channel_id=1, source_target_pairs={{0,1},{1,0},{2,3},{3,2},{4,5},{5,4},{6,7},{7,6},{8,9},{9,8},{10,11... | collective-permute-start | bytes 393224 | tf_op jit(solution)/shard_map/ppermute | solution.py:676
  19.3 8.8 %collective-permute-start.6 = (bf16[576,256]{1,0:T(8,128)(2,1)S(1)}, bf16[576,256]{1,0:T(8,128)(2,1)S(1)}, u32[]{:S(2)}, u32[]{:S(2)}) collective-permute-start(bf16[576,256]{1,0:T(8,128)(2,1)S(1)} %collective-permute-done.2.refs_1_.refs_3_.refs_7_), channel_id=1, source_target_pairs={{0,96},{32,0},{64,32},{96,64},{1,97},{33,1},{65,33},{97,65},{2,98}... | collective-permute-start | bytes 884744 | tf_op jit(solution)/shard_map/ppermute | solution.py:676
  21.4 13.0 %collective-permute-start.1 = (bf16[576,256]{1,0:T(8,128)(2,1)S(1)}, bf16[576,256]{1,0:T(8,128)(2,1)S(1)}, u32[]{:S(2)}, u32[]{:S(2)}) collective-permute-start(bf16[576,256]{1,0:T(8,128)(2,1)S(1)} %collective-permute-done.refs_2_.refs_4_.refs_8_), channel_id=1, source_target_pairs={{0,96},{32,0},{64,32},{96,64},{1,97},{33,1},{65,33},{97,65},{2,98}... | collective-permute-start | bytes 884744 | tf_op jit(solution)/shard_map/ppermute | solution.py:676
  25.0 9.4 %collective-permute-start.4 = (bf16[576,256]{1,0:T(8,128)(2,1)S(1)}, bf16[576,256]{1,0:T(8,128)(2,1)S(1)}, u32[]{:S(2)}, u32[]{:S(2)}) collective-permute-start(bf16[576,256]{1,0:T(8,128)(2,1)S(1)} %collective-permute-done.3.refs_1_.refs_7_.refs_0_), channel_id=1, source_target_pairs={{0,32},{32,64},{64,96},{96,0},{1,33},{33,65},{65,97},{97,1},{2,34}... | collective-permute-start | bytes 884744 | tf_op jit(solution)/shard_map/ppermute | solution.py:676
  38.1 3.1 %collective-permute-start.10 = (f32[1024,128]{1,0:T(8,128)S(1)}, f32[1024,128]{1,0:T(8,128)S(1)}, u32[]{:S(2)}, u32[]{:S(2)}) collective-permute-start(f32[1024,128]{1,0:T(8,128)S(1)} %get-tuple-element.70.mine_ref), channel_id=1, source_target_pairs={{0,1},{1,0},{2,3},{3,2},{4,5},{5,4},{6,7},{7,6},{8,9},{9,8},{10,11... | collective-permute-start | bytes 1572872 | tf_op jit(solution)/shard_map/ppermute | solution.py:676
  44.4 7.5 %collective-permute-start.13 = (f32[128,256]{1,0:T(8,128)S(1)}, f32[128,256]{1,0:T(8,128)S(1)}, u32[]{:S(2)}, u32[]{:S(2)}) collective-permute-start(f32[128,256]{1,0:T(8,128)S(1)} %get-tuple-element.78), channel_id=1, source_target_pairs={{0,32},{32,64},{64,96},{96,0},{1,33},{33,65},{65,97},{97,1},{2,34}... | collective-permute-start | bytes 393224 | tf_op jit(solution)/shard_map/ppermute | solution.py:676
  45.4 6.5 %collective-permute-start.14 = (f32[128,256]{1,0:T(8,128)S(1)}, f32[128,256]{1,0:T(8,128)S(1)}, u32[]{:S(2)}, u32[]{:S(2)}) collective-permute-start(f32[128,256]{1,0:T(8,128)S(1)} %get-tuple-element.79), channel_id=1, source_target_pairs={{0,96},{32,0},{64,32},{96,64},{1,97},{33,1},{65,33},{97,65},{2,98}... | collective-permute-start | bytes 393224 | tf_op jit(solution)/shard_map/ppermute | solution.py:676
  47.1 5.8 %collective-permute-start.15 = (f32[128,256]{1,0:T(8,128)S(1)}, f32[128,256]{1,0:T(8,128)S(1)}, u32[]{:S(2)}, u32[]{:S(2)}) collective-permute-start(f32[128,256]{1,0:T(8,128)S(1)} %get-tuple-element.80), channel_id=1, source_target_pairs={{0,64},{32,96},{64,0},{96,32},{1,65},{33,97},{65,1},{97,33},{2,66}... | collective-permute-start | bytes 393224 | tf_op jit(solution)/shard_map/ppermute | solution.py:676
  47.4 14.9 %copy-start = (bf16[128,1024]{1,0:T(8,128)(2,1)S(1)}, bf16[128,1024]{1,0:T(8,128)(2,1)}, u32[]{:S(2)}) copy-start(bf16[128,1024]{1,0:T(8,128)(2,1)} %raw_ref.1) | copy-start | bytes 786436
  53.5 6.7 %collective-permute-start.16 = (f32[64,256]{1,0:T(8,128)S(1)}, f32[64,256]{1,0:T(8,128)S(1)}, u32[]{:S(2)}, u32[]{:S(2)}) collective-permute-start(f32[64,256]{1,0:T(8,128)S(1)} %get-tuple-element.92), channel_id=1, source_target_pairs={{0,16},{16,0},{1,17},{17,1},{2,18},{18,2},{3,19},{19,3},{4,20},{20... | collective-permute-start | bytes 196616 | tf_op jit(solution)/shard_map/ppermute | solution.py:676
  60.2 4.1 %collective-permute-start.17 = (f32[1024,128]{1,0:T(8,128)S(1)}, f32[1024,128]{1,0:T(8,128)S(1)}, u32[]{:S(2)}, u32[]{:S(2)}) collective-permute-start(f32[1024,128]{1,0:T(8,128)S(1)} %cache_grads_5.1.dq_ref), channel_id=1, source_target_pairs={{0,1},{1,0},{2,3},{3,2},{4,5},{5,4},{6,7},{7,6},{8,9},{9,8},{10,11... | collective-permute-start | bytes 1572872 | tf_op jit(solution)/shard_map/ppermute | solution.py:676
  63.0 1.3 %collective-permute-start.18 = (bf16[64,256]{1,0:T(8,128)(2,1)S(1)}, bf16[64,256]{1,0:T(8,128)(2,1)S(1)}, u32[]{:S(2)}, u32[]{:S(2)}) collective-permute-start(bf16[64,256]{1,0:T(8,128)(2,1)S(1)} %own_kv.1.kv_ref), channel_id=1, source_target_pairs={{0,1},{1,0},{2,3},{3,2},{4,5},{5,4},{6,7},{7,6},{8,9},{9,8},{10,11... | collective-permute-start | bytes 98312 | tf_op jit(solution)/shard_map/ppermute | solution.py:676

commit v6 on v5

--- a/solution.py
+++ b/solution.py
@@ -737,12 +737,12 @@
     lse, delta, dq, *parts = window_call(info, stat, pair_stat, query, dout, win_k, win_v)
     parts = [parts[0]] + [shift(parts[dz], "z", dz) for dz in (1, 3, 2)]
     dq, w_own, w_kv = cache_call(
-        0, info, groups[:5], query, dout, lse, delta, dq, [*weights, *pair_weights]
+        0, info, groups[:6], query, dout, lse, delta, dq, [*weights, *pair_weights]
     )
     parts, dq = lax.optimization_barrier((parts, dq))
     keep, send = sum_parts(info, parts)
     other = swap(send, "xh")
-    (dq,) = cache_call(5, info, groups[5:], query, dout, lse, delta, dq)
+    (dq,) = cache_call(6, info, groups[6:], query, dout, lse, delta, dq)
     other, dq = lax.optimization_barrier((other, dq))
     pair_dq = swap(dq, "c")
     kv = own_kv(info, keep, other, k_raw, gain)

time: 98.6 us -> 99.9 us (1.013); the launches traced: 98.3 us -> 101 us
  Pallas kernels: 28 us -> 33.1 us
  waiting for transfers between devices: 15.4 us -> 11.9 us
    ppermute x19, waiting for transfers between devices: 15.4 us -> 11.9 us  [shift(): lax.ppermute(block, axis, [(i, (i + by) % count) for i in range(count)])]
    pallas_call x2, Pallas kernels: 8.35 us -> 11 us  [cache_call(): pl.pallas_call(functools.partial(cache_kernel, first, [len(group) for gro...]
    pallas_call x3, Pallas kernels: 8.06 us -> 10.5 us  [stats_call(): pl.pallas_call(functools.partial(stats_kernel, first, [len(group) for gro...]
  transfers between devices with their start and end apart: 19 -> 19, of which waited for: 9 -> 7; matrix products, arithmetic and copies ran while one was open for 0% -> 0% of each run, Pallas kernels for 20% -> 24%
where the time goes in v6:
time: 99.9 us; the launch traced here: 101 us
  Pallas kernels  33.1 us (33%)
  blocking collectives  29.8 us (30%)
  starting transfers between devices  25.8 us (26%)
  waiting for transfers between devices  11.9 us (12%)
    ppermute x19, starting transfers between devices, shift(): lax.ppermute(block, axis, [(i, (i + by) % count) for i in range(count)])  25.8 us
    all_to_all x1, blocking collectives, on_device(): pieces = lax.all_to_all(partial, CHIP_AXES, 0, 0)  19.1 us
    ppermute x19, waiting for transfers between devices, shift(): lax.ppermute(block, axis, [(i, (i + by) % count) for i in range(count)])  11.9 us
    pallas_call x2, Pallas kernels, cache_call(): pl.pallas_call(functools.partial(cache_kernel, first, [len(group) for gro...  11 us
    all_to_all x1, blocking collectives, on_device(): lax.all_to_all(jnp.broadcast_to(sums[None], (2 * CHIPS, 8, TOK)), TP_AXES...  10.7 us
    pallas_call x3, Pallas kernels, stats_call(): pl.pallas_call(functools.partial(stats_kernel, first, [len(group) for gro...  10.5 us
    pallas_call x1, Pallas kernels, project(): pl.pallas_call(project_kernel, out_shape=SHAPE((CHIPS, FEAT, TOK), jnp.bf...  3.9 us
    pallas_call x1, Pallas kernels, window_call(): pl.pallas_call(window_kernel, out_shape=out, in_specs=[SM] + [VM] * 6, ou...  3.19 us
  transfers between devices with their start and end apart: 19, of which 7 were waited for; matrix products, arithmetic and copies ran while one was open for 0% of the time, Pallas kernels for 24%

profile of v6, /device:TPU:1, one launch (start us, length us, event | category | flops | bytes accessed | tf_op | source)
XLA Modules:
  0.0 101.5 jit_solution(12173220604347493847)
XLA Ops:
  0.0 1.4 %collective-permute-start.9 = (bf16[8192,512]{1,0:T(8,128)(2,1)}, bf16[8192,512]{1,0:T(8,128)(2,1)}, u32[]{:S(2)}, u32[]{:S(2)}) collective-permute-start(bf16[8192,512]{1,0:T(8,128)(2,1)} %refs_0_.1), channel_id=1, source_target_pairs={{0,1},{1,0},{2,3},{3,2},{4,5},{5,4},{6,7},{7,6},{8,9},{9,8},{10,11... | collective-permute-start | bytes 25165832 | tf_op jit(solution)/shard_map/ppermute | solution.py:676
  2.1 0.1 stack.20.info_ref.idx_ref
  2.2 0.0 copy-start.1
  2.2 0.0 copy-start.2
  2.2 2.2 %pack_rows.1 = (bf16[576,256]{1,0:T(8,128)(2,1)S(1)}, bf16[512,128]{1,0:T(8,128)(2,1)S(1)}, bf16[512,128]{1,0:T(8,128)(2,1)S(1)}, bf16[128,512]{1,0:T(8,128)(2,1...) custom-call(s32[5]{0:T(128)S(1)} %stack.20.info_ref.idx_ref, bf16[1024,1024]{1,0:T(8,128)(2,1)} %ck_ref.1, ...), custom_call_target="tpu_custom_call" | custom-call | tf_op jit(solution)/shard_map/pack_rows/pallas_call | solution.py:147
  4.4 2.9 %collective-permute-start.2 = (bf16[576,256]{1,0:T(8,128)(2,1)S(1)}, bf16[576,256]{1,0:T(8,128)(2,1)S(1)}, u32[]{:S(2)}, u32[]{:S(2)}) collective-permute-start(bf16[576,256]{1,0:T(8,128)(2,1)S(1)} %get-tuple-element.54.refs_0_.refs_2_.refs_6_), channel_id=1, source_target_pairs={{0,16},{16,0},{1,17},{17,1},{2,18},{18,2},{3,19},{19,3},{4,20},{20... | collective-permute-start | bytes 884744 | tf_op jit(solution)/shard_map/ppermute | solution.py:676
  7.3 1.6 %collective-permute-start.5 = (bf16[576,256]{1,0:T(8,128)(2,1)S(1)}, bf16[576,256]{1,0:T(8,128)(2,1)S(1)}, u32[]{:S(2)}, u32[]{:S(2)}) collective-permute-start(bf16[576,256]{1,0:T(8,128)(2,1)S(1)} %get-tuple-element.54.refs_0_.refs_2_.refs_6_), channel_id=1, source_target_pairs={{0,32},{32,64},{64,96},{96,0},{1,33},{33,65},{65,97},{97,1},{2,34}... | collective-permute-start | bytes 884744 | tf_op jit(solution)/shard_map/ppermute | solution.py:676
  8.9 2.1 %collective-permute-start = (bf16[576,256]{1,0:T(8,128)(2,1)S(1)}, bf16[576,256]{1,0:T(8,128)(2,1)S(1)}, u32[]{:S(2)}, u32[]{:S(2)}) collective-permute-start(bf16[576,256]{1,0:T(8,128)(2,1)S(1)} %get-tuple-element.54.refs_0_.refs_2_.refs_6_), channel_id=1, source_target_pairs={{0,96},{32,0},{64,32},{96,64},{1,97},{33,1},{65,33},{97,65},{2,98}... | collective-permute-start | bytes 884744 | tf_op jit(solution)/shard_map/ppermute | solution.py:676
  11.0 3.6 %collective-permute-done.2.refs_1_.refs_3_.refs_7_ = bf16[576,256]{1,0:T(8,128)(2,1)S(1)} collective-permute-done((bf16[576,256]{1,0:T(8,128)(2,1)S(1)}, bf16[576,256]{1,0:T(8,128)(2,1)S(1)}, u32[]{:S(2)}, u32[]{:S(2)}) %collective-permute-start.2) | collective-permute-done | bytes 294944 | tf_op jit(solution)/shard_map/ppermute | solution.py:676
  14.6 1.7 %collective-permute-start.3 = (bf16[576,256]{1,0:T(8,128)(2,1)S(1)}, bf16[576,256]{1,0:T(8,128)(2,1)S(1)}, u32[]{:S(2)}, u32[]{:S(2)}) collective-permute-start(bf16[576,256]{1,0:T(8,128)(2,1)S(1)} %collective-permute-done.2.refs_1_.refs_3_.refs_7_), channel_id=1, source_target_pairs={{0,32},{32,64},{64,96},{96,0},{1,33},{33,65},{65,97},{97,1},{2,34}... | collective-permute-start | bytes 884744 | tf_op jit(solution)/shard_map/ppermute | solution.py:676
  16.3 1.1 %collective-permute-start.8 = (bf16[128,512]{1,0:T(8,128)(2,1)S(1)}, bf16[128,512]{1,0:T(8,128)(2,1)S(1)}, u32[]{:S(2)}, u32[]{:S(2)}) collective-permute-start(bf16[128,512]{1,0:T(8,128)(2,1)S(1)} %get-tuple-element.59.refs_5_), channel_id=1, source_target_pairs={{0,1},{1,0},{2,3},{3,2},{4,5},{5,4},{6,7},{7,6},{8,9},{9,8},{10,11... | collective-permute-start | bytes 393224 | tf_op jit(solution)/shard_map/ppermute | solution.py:676
  17.4 1.0 collective-permute-done.8.refs_7_
  18.4 0.0 collective-permute-done.9.refs_3_
  18.4 0.4 collective-permute-start.11
  18.7 0.1 collective-permute-start.12
  18.9 0.0 collective-permute-done.5.refs_3_.refs_5_.refs_9_
  18.9 0.4 collective-permute-start.7
  19.3 0.0 collective-permute-done.refs_2_.refs_4_.refs_8_
  19.3 1.8 %collective-permute-start.6 = (bf16[576,256]{1,0:T(8,128)(2,1)S(1)}, bf16[576,256]{1,0:T(8,128)(2,1)S(1)}, u32[]{:S(2)}, u32[]{:S(2)}) collective-permute-start(bf16[576,256]{1,0:T(8,128)(2,1)S(1)} %collective-permute-done.2.refs_1_.refs_3_.refs_7_), channel_id=1, source_target_pairs={{0,96},{32,0},{64,32},{96,64},{1,97},{33,1},{65,33},{97,65},{2,98}... | collective-permute-start | bytes 884744 | tf_op jit(solution)/shard_map/ppermute | solution.py:676
  21.1 0.3 collective-permute-done.7.refs_6_.pair_q_ref
  21.4 1.8 %collective-permute-start.1 = (bf16[576,256]{1,0:T(8,128)(2,1)S(1)}, bf16[576,256]{1,0:T(8,128)(2,1)S(1)}, u32[]{:S(2)}, u32[]{:S(2)}) collective-permute-start(bf16[576,256]{1,0:T(8,128)(2,1)S(1)} %collective-permute-done.refs_2_.refs_4_.refs_8_), channel_id=1, source_target_pairs={{0,96},{32,0},{64,32},{96,64},{1,97},{33,1},{65,33},{97,65},{2,98}... | collective-permute-start | bytes 884744 | tf_op jit(solution)/shard_map/ppermute | solution.py:676
  23.3 1.8 %collective-permute-done.3.refs_1_.refs_7_.refs_11_ = bf16[576,256]{1,0:T(8,128)(2,1)S(1)} collective-permute-done((bf16[576,256]{1,0:T(8,128)(2,1)S(1)}, bf16[576,256]{1,0:T(8,128)(2,1)S(1)}, u32[]{:S(2)}, u32[]{:S(2)}) %collective-permute-start.3) | collective-permute-done | bytes 294944 | tf_op jit(solution)/shard_map/ppermute | solution.py:676
  25.0 0.0 collective-permute-start.4
  25.1 4.4 %stats_0.1 = (bf16[1024,128]{1,0:T(8,128)(2,1)S(1)}, bf16[1024,128]{1,0:T(8,128)(2,1)S(1)}, f32[1024,128]{1,0:T(8,128)S(1)}, f32[1024,128]{1,0:T(8,128)S(1)}, f32[1024,128]{1,0:T(8,128)S(1)}) custom-call(s32[5]{0:T(128)S(1)} %stack.20.info_ref.idx_ref, bf16[576,256]{1,0:T(8,128)(2,1)S(1)} %get-tuple-element.54.refs_0_.refs_2_.refs_6_, ...), custom_call_target="tpu_custom_call" | custom-call | flops 1073741824 | bytes 3145728 | tf_op jit(solution)/shard_map/stats_0/pallas_call | solution.py:369
  29.5 0.0 collective-permute-done.6.refs_0_.refs_6_.refs_10_
  29.5 2.4 %stats_4.1 = (f32[1024,128]{1,0:T(8,128)S(1)}, f32[1024,128]{1,0:T(8,128)S(1)}, f32[1024,128]{1,0:T(8,128)S(1)}) custom-call(s32[5]{0:T(128)S(1)} %stack.20.info_ref.idx_ref, bf16[576,256]{1,0:T(8,128)(2,1)S(1)} %collective-permute-done.6.refs_0_.refs_6_.refs_10_, bf16[576,256]{1,0:T(8,128)(2,1)S(1)} %collective-permute-done.3.refs_1_.refs_7_.refs_11_, ...), custom_call_target="tpu_custom_call" | custom-call | flops 536870912 | bytes 2621440 | tf_op jit(solution)/shard_map/stats_4/pallas_call | solution.py:369
  31.9 2.5 %collective-permute-done.1.refs_0_ = bf16[576,256]{1,0:T(8,128)(2,1)S(1)} collective-permute-done((bf16[576,256]{1,0:T(8,128)(2,1)S(1)}, bf16[576,256]{1,0:T(8,128)(2,1)S(1)}, u32[]{:S(2)}, u32[]{:S(2)}) %collective-permute-start.1) | collective-permute-done | bytes 294944 | tf_op jit(solution)/shard_map/ppermute | solution.py:676
  34.4 0.0 collective-permute-done.4.refs_1_
  34.4 3.7 %stats_6.1 = (f32[1024,128]{1,0:T(8,128)S(1)}, bf16[512,128]{1,0:T(8,128)(2,1)S(1)}, bf16[512,128]{1,0:T(8,128)(2,1)S(1)}) custom-call(s32[5]{0:T(128)S(1)} %stack.20.info_ref.idx_ref, bf16[576,256]{1,0:T(8,128)(2,1)S(1)} %collective-permute-done.1.refs_0_, bf16[576,256]{1,0:T(8,128)(2,1)S(1)} %collective-permute-done.4.refs_1_, ...), custom_call_target="tpu_custom_call" | custom-call | flops 805306368 | bytes 2883584 | tf_op jit(solution)/shard_map/stats_6/pallas_call | solution.py:369
  38.1 1.5 %collective-permute-start.10 = (f32[1024,128]{1,0:T(8,128)S(1)}, f32[1024,128]{1,0:T(8,128)S(1)}, u32[]{:S(2)}, u32[]{:S(2)}) collective-permute-start(f32[1024,128]{1,0:T(8,128)S(1)} %get-tuple-element.70.mine_ref), channel_id=1, source_target_pairs={{0,1},{1,0},{2,3},{3,2},{4,5},{5,4},{6,7},{7,6},{8,9},{9,8},{10,11... | collective-permute-start | bytes 1572872 | tf_op jit(solution)/shard_map/ppermute | solution.py:676
  39.6 1.5 %collective-permute-done.10.pair_ref = f32[1024,128]{1,0:T(8,128)S(1)} collective-permute-done((f32[1024,128]{1,0:T(8,128)S(1)}, f32[1024,128]{1,0:T(8,128)S(1)}, u32[]{:S(2)}, u32[]{:S(2)}) %collective-permute-start.10) | collective-permute-done | bytes 524320 | tf_op jit(solution)/shard_map/ppermute | solution.py:676
  41.2 0.0 collective-permute-done.11.refs_4_
  41.2 0.0 collective-permute-done.12.refs_5_
  41.2 3.2 %window_grads.1 = (f32[1024,128]{1,0:T(8,128)S(1)}, f32[1024,128]{1,0:T(8,128)S(1)}, f32[1024,128]{1,0:T(8,128)S(1)}, f32[128,256]{1,0:T(8,128)S(1)}, f32[128,25...) custom-call(s32[5]{0:T(128)S(1)} %stack.20.info_ref.idx_ref, ...), custom_call_target="tpu_custom_call" | custom-call | flops 671088640 | bytes 2359296 | tf_op jit(solution)/shard_map/window_grads/pallas_call | solution.py:432
  44.4 1.0 %collective-permute-start.13 = (f32[128,256]{1,0:T(8,128)S(1)}, f32[128,256]{1,0:T(8,128)S(1)}, u32[]{:S(2)}, u32[]{:S(2)}) collective-permute-start(f32[128,256]{1,0:T(8,128)S(1)} %get-tuple-element.78), channel_id=1, source_target_pairs={{0,32},{32,64},{64,96},{96,0},{1,33},{33,65},{65,97},{97,1},{2,34}... | collective-permute-start | bytes 393224 | tf_op jit(solution)/shard_map/ppermute | solution.py:676
  45.4 1.7 %collective-permute-start.14 = (f32[128,256]{1,0:T(8,128)S(1)}, f32[128,256]{1,0:T(8,128)S(1)}, u32[]{:S(2)}, u32[]{:S(2)}) collective-permute-start(f32[128,256]{1,0:T(8,128)S(1)} %get-tuple-element.79), channel_id=1, source_target_pairs={{0,96},{32,0},{64,32},{96,64},{1,97},{33,1},{65,33},{97,65},{2,98}... | collective-permute-start | bytes 393224 | tf_op jit(solution)/shard_map/ppermute | solution.py:676
  47.1 1.6 %collective-permute-start.15 = (f32[128,256]{1,0:T(8,128)S(1)}, f32[128,256]{1,0:T(8,128)S(1)}, u32[]{:S(2)}, u32[]{:S(2)}) collective-permute-start(f32[128,256]{1,0:T(8,128)S(1)} %get-tuple-element.80), channel_id=1, source_target_pairs={{0,64},{32,96},{64,0},{96,32},{1,65},{33,97},{65,1},{97,33},{2,66}... | collective-permute-start | bytes 393224 | tf_op jit(solution)/shard_map/ppermute | solution.py:676
  48.7 0.0 copy-done.1
  48.7 0.0 copy-done.2
  48.7 0.0 copy-start
  48.7 8.2 %cache_grads_0.1 = (f32[1024,128]{1,0:T(8,128)S(1)}, bf16[8,512,1024]{2,1,0:T(8,128)(2,1)S(1)}, bf16[8,256,512]{2,1,0:T(8,128)(2,1)S(1)}) custom-call(s32[5]{0:T(128)S(1)} %stack.20.info_ref.idx_ref, bf16[8192,512]{1,0:T(8,128)(2,1)} %refs_0_.1, bf16[64,8192]{1,0:T(8,128)(2,1)S(1)} %bitcast.8, bf16[64,8192]{1,0:T(8,128)(2,1)S(1)} %bitcast.10, ...), custom_call_target="tpu_custom_call" | custom-call | flops 2415919104 | bytes 3670016 | tf_op jit(solution)/shard_map/cache_grads_0/pallas_call | solution.py:506
  56.9 0.0 collective-permute-done.13.b_ref
  56.9 0.0 collective-permute-done.14.c_ref
  57.0 0.0 collective-permute-done.15.d_ref
  57.0 0.6 sum_parts.1
  57.5 2.8 %collective-permute-start.16 = (f32[64,256]{1,0:T(8,128)S(1)}, f32[64,256]{1,0:T(8,128)S(1)}, u32[]{:S(2)}, u32[]{:S(2)}) collective-permute-start(f32[64,256]{1,0:T(8,128)S(1)} %get-tuple-element.92), channel_id=1, source_target_pairs={{0,16},{16,0},{1,17},{17,1},{2,18},{18,2},{3,19},{19,3},{4,20},{20... | collective-permute-start | bytes 196616 | tf_op jit(solution)/shard_map/ppermute | solution.py:676
  60.4 2.8 %cache_grads_6.1.dq_ref = f32[1024,128]{1,0:T(8,128)S(1)} custom-call(s32[5]{0:T(128)S(1)} %stack.20.info_ref.idx_ref, bf16[576,256]{1,0:T(8,128)(2,1)S(1)} %collective-permute-done.1.refs_0_, bf16[576,256]{1,0:T(8,128)(2,1)S(1)} %collective-permute-done.4.refs_1_, bf16[1024,128]{1,0:T(8,128)(2,1)S(1)} %get-tuple-element.62.refs_2_.refs_8_.q_s.refs_12_, ...), custom_call_target="tpu_custom_call" | custom-call | flops 805306368 | bytes 2621440 | tf_op jit(solution)/shard_map/cache_grads_6/pallas_call | solution.py:506
  63.2 0.0 collective-permute-done.16.other_ref
  63.2 1.6 %collective-permute-start.17 = (f32[1024,128]{1,0:T(8,128)S(1)}, f32[1024,128]{1,0:T(8,128)S(1)}, u32[]{:S(2)}, u32[]{:S(2)}) collective-permute-start(f32[1024,128]{1,0:T(8,128)S(1)} %cache_grads_6.1.dq_ref), channel_id=1, source_target_pairs={{0,1},{1,0},{2,3},{3,2},{4,5},{5,4},{6,7},{7,6},{8,9},{9,8},{10,11... | collective-permute-start | bytes 1572872 | tf_op jit(solution)/shard_map/ppermute | solution.py:676
  64.8 0.0 copy-done
  64.8 0.6 own_kv.1.kv_ref
  65.4 0.1 collective-permute-start.18
  65.5 1.2 %collective-permute-done.18.pair_kv_ref = bf16[64,256]{1,0:T(8,128)(2,1)S(1)} collective-permute-done((bf16[64,256]{1,0:T(8,128)(2,1)S(1)}, bf16[64,256]{1,0:T(8,128)(2,1)S(1)}, u32[]{:S(2)}, u32[]{:S(2)}) %collective-permute-start.18) | collective-permute-done | bytes 32800 | tf_op jit(solution)/shard_map/ppermute | solution.py:676
  66.7 0.0 collective-permute-done.17.pair_dq_ref
  66.7 3.9 %project.1 = bf16[8,512,128]{2,1,0:T(8,128)(2,1)S(1)} custom-call(s32[5]{0:T(128)S(1)} %stack.20.info_ref.idx_ref, f32[1024,128]{1,0:T(8,128)S(1)} %cache_grads_6.1.dq_ref, f32[1024,128]{1,0:T(8,128)S(1)} %collective-permute-done.17.pair_dq_ref, bf16[128,512]{1,0:T(8,128)(2,1)S(1)} %get-tuple-element.58.refs_4_.q_ref, ...), custom_call_target="tpu_custom_call" | custom-call | flops 1342177280 | bytes 12000000 | tf_op jit(solution)/shard_map/project/pallas_call | solution.py:610
  70.6 19.1 %all_to_all.10.pieces_ref = bf16[8,512,128]{2,1,0:T(8,128)(2,1)S(1)} all-to-all(bf16[8,512,128]{2,1,0:T(8,128)(2,1)S(1)} %project.1), channel_id=1, replica_groups=mesh['z'=4,'xh'=2,'xl'=2,'y'=4,'c'=2] {'xl','y'}, dimensions={0} | all-to-all | bytes 2097152 | tf_op jit(solution)/shard_map/all_to_all | solution.py:751
  89.7 0.2 row_sums.1
  90.0 10.7 %all_to_all.11.sums_ref = f32[16,8,128]{2,1,0:T(8,128)S(1)} all-to-all(f32[16,8,128]{2,1,0:T(8,128)S(1)} %broadcast_in_dim.2), channel_id=1, replica_groups=mesh['z'=4,'xh'=2,'xl'=2,'y'=4,'c'=2] {'xl','y','c'}, dimensions={0} | all-to-all | bytes 131072 | tf_op jit(solution)/shard_map/all_to_all | solution.py:753
  100.6 0.9 last_norm.1
  (1 shorter events, 0.0 us)
Async XLA Ops:
  0.0 18.4 %collective-permute-start.9 = (bf16[8192,512]{1,0:T(8,128)(2,1)}, bf16[8192,512]{1,0:T(8,128)(2,1)}, u32[]{:S(2)}, u32[]{:S(2)}) collective-permute-start(bf16[8192,512]{1,0:T(8,128)(2,1)} %refs_0_.1), channel_id=1, source_target_pairs={{0,1},{1,0},{2,3},{3,2},{4,5},{5,4},{6,7},{7,6},{8,9},{9,8},{10,11... | collective-permute-start | bytes 25165832 | tf_op jit(solution)/shard_map/ppermute | solution.py:676
  2.2 46.5 %copy-start.1 = (bf16[8192,64]{0,1:T(8,128)(2,1)S(1)}, bf16[8192,64]{0,1:T(8,128)(2,1)}, u32[]{:S(2)}) copy-start(bf16[8192,64]{0,1:T(8,128)(2,1)} %param.16) | copy-start | bytes 3145732
  2.2 46.5 %copy-start.2 = (bf16[8192,64]{0,1:T(8,128)(2,1)S(1)}, bf16[8192,64]{0,1:T(8,128)(2,1)}, u32[]{:S(2)}) copy-start(bf16[8192,64]{0,1:T(8,128)(2,1)} %param.17) | copy-start | bytes 3145732
  4.4 10.2 %collective-permute-start.2 = (bf16[576,256]{1,0:T(8,128)(2,1)S(1)}, bf16[576,256]{1,0:T(8,128)(2,1)S(1)}, u32[]{:S(2)}, u32[]{:S(2)}) collective-permute-start(bf16[576,256]{1,0:T(8,128)(2,1)S(1)} %get-tuple-element.54.refs_0_.refs_2_.refs_6_), channel_id=1, source_target_pairs={{0,16},{16,0},{1,17},{17,1},{2,18},{18,2},{3,19},{19,3},{4,20},{20... | collective-permute-start | bytes 884744 | tf_op jit(solution)/shard_map/ppermute | solution.py:676
  7.3 11.6 %collective-permute-start.5 = (bf16[576,256]{1,0:T(8,128)(2,1)S(1)}, bf16[576,256]{1,0:T(8,128)(2,1)S(1)}, u32[]{:S(2)}, u32[]{:S(2)}) collective-permute-start(bf16[576,256]{1,0:T(8,128)(2,1)S(1)} %get-tuple-element.54.refs_0_.refs_2_.refs_6_), channel_id=1, source_target_pairs={{0,32},{32,64},{64,96},{96,0},{1,33},{33,65},{65,97},{97,1},{2,34}... | collective-permute-start | bytes 884744 | tf_op jit(solution)/shard_map/ppermute | solution.py:676
  8.9 10.3 %collective-permute-start = (bf16[576,256]{1,0:T(8,128)(2,1)S(1)}, bf16[576,256]{1,0:T(8,128)(2,1)S(1)}, u32[]{:S(2)}, u32[]{:S(2)}) collective-permute-start(bf16[576,256]{1,0:T(8,128)(2,1)S(1)} %get-tuple-element.54.refs_0_.refs_2_.refs_6_), channel_id=1, source_target_pairs={{0,96},{32,0},{64,32},{96,64},{1,97},{33,1},{65,33},{97,65},{2,98}... | collective-permute-start | bytes 884744 | tf_op jit(solution)/shard_map/ppermute | solution.py:676
  14.6 10.4 %collective-permute-start.3 = (bf16[576,256]{1,0:T(8,128)(2,1)S(1)}, bf16[576,256]{1,0:T(8,128)(2,1)S(1)}, u32[]{:S(2)}, u32[]{:S(2)}) collective-permute-start(bf16[576,256]{1,0:T(8,128)(2,1)S(1)} %collective-permute-done.2.refs_1_.refs_3_.refs_7_), channel_id=1, source_target_pairs={{0,32},{32,64},{64,96},{96,0},{1,33},{33,65},{65,97},{97,1},{2,34}... | collective-permute-start | bytes 884744 | tf_op jit(solution)/shard_map/ppermute | solution.py:676
  16.3 2.1 %collective-permute-start.8 = (bf16[128,512]{1,0:T(8,128)(2,1)S(1)}, bf16[128,512]{1,0:T(8,128)(2,1)S(1)}, u32[]{:S(2)}, u32[]{:S(2)}) collective-permute-start(bf16[128,512]{1,0:T(8,128)(2,1)S(1)} %get-tuple-element.59.refs_5_), channel_id=1, source_target_pairs={{0,1},{1,0},{2,3},{3,2},{4,5},{5,4},{6,7},{7,6},{8,9},{9,8},{10,11... | collective-permute-start | bytes 393224 | tf_op jit(solution)/shard_map/ppermute | solution.py:676
  18.4 22.8 %collective-permute-start.11 = (bf16[64,8192]{1,0:T(8,128)(2,1)}, bf16[64,8192]{1,0:T(8,128)(2,1)S(1)}, u32[]{:S(2)}, u32[]{:S(2)}) collective-permute-start(bf16[64,8192]{1,0:T(8,128)(2,1)} %bitcast.7), channel_id=1, source_target_pairs={{0,1},{1,0},{2,3},{3,2},{4,5},{5,4},{6,7},{7,6},{8,9},{9,8},{10,11... | collective-permute-start | bytes 3145736 | tf_op jit(solution)/shard_map/ppermute | solution.py:676
  18.7 22.4 %collective-permute-start.12 = (bf16[64,8192]{1,0:T(8,128)(2,1)}, bf16[64,8192]{1,0:T(8,128)(2,1)S(1)}, u32[]{:S(2)}, u32[]{:S(2)}) collective-permute-start(bf16[64,8192]{1,0:T(8,128)(2,1)} %bitcast.9), channel_id=1, source_target_pairs={{0,1},{1,0},{2,3},{3,2},{4,5},{5,4},{6,7},{7,6},{8,9},{9,8},{10,11... | collective-permute-start | bytes 3145736 | tf_op jit(solution)/shard_map/ppermute | solution.py:676
  18.9 2.5 %collective-permute-start.7 = (bf16[128,512]{1,0:T(8,128)(2,1)S(1)}, bf16[128,512]{1,0:T(8,128)(2,1)S(1)}, u32[]{:S(2)}, u32[]{:S(2)}) collective-permute-start(bf16[128,512]{1,0:T(8,128)(2,1)S(1)} %get-tuple-element.58.refs_4_.q_ref), channel_id=1, source_target_pairs={{0,1},{1,0},{2,3},{3,2},{4,5},{5,4},{6,7},{7,6},{8,9},{9,8},{10,11... | collective-permute-start | bytes 393224 | tf_op jit(solution)/shard_map/ppermute | solution.py:676
  19.3 10.2 %collective-permute-start.6 = (bf16[576,256]{1,0:T(8,128)(2,1)S(1)}, bf16[576,256]{1,0:T(8,128)(2,1)S(1)}, u32[]{:S(2)}, u32[]{:S(2)}) collective-permute-start(bf16[576,256]{1,0:T(8,128)(2,1)S(1)} %collective-permute-done.2.refs_1_.refs_3_.refs_7_), channel_id=1, source_target_pairs={{0,96},{32,0},{64,32},{96,64},{1,97},{33,1},{65,33},{97,65},{2,98}... | collective-permute-start | bytes 884744 | tf_op jit(solution)/shard_map/ppermute | solution.py:676
  21.4 13.0 %collective-permute-start.1 = (bf16[576,256]{1,0:T(8,128)(2,1)S(1)}, bf16[576,256]{1,0:T(8,128)(2,1)S(1)}, u32[]{:S(2)}, u32[]{:S(2)}) collective-permute-start(bf16[576,256]{1,0:T(8,128)(2,1)S(1)} %collective-permute-done.refs_2_.refs_4_.refs_8_), channel_id=1, source_target_pairs={{0,96},{32,0},{64,32},{96,64},{1,97},{33,1},{65,33},{97,65},{2,98}... | collective-permute-start | bytes 884744 | tf_op jit(solution)/shard_map/ppermute | solution.py:676
  25.0 9.4 %collective-permute-start.4 = (bf16[576,256]{1,0:T(8,128)(2,1)S(1)}, bf16[576,256]{1,0:T(8,128)(2,1)S(1)}, u32[]{:S(2)}, u32[]{:S(2)}) collective-permute-start(bf16[576,256]{1,0:T(8,128)(2,1)S(1)} %collective-permute-done.3.refs_1_.refs_7_.refs_11_), channel_id=1, source_target_pairs={{0,32},{32,64},{64,96},{96,0},{1,33},{33,65},{65,97},{97,1},{2,34}... | collective-permute-start | bytes 884744 | tf_op jit(solution)/shard_map/ppermute | solution.py:676
  38.1 3.1 %collective-permute-start.10 = (f32[1024,128]{1,0:T(8,128)S(1)}, f32[1024,128]{1,0:T(8,128)S(1)}, u32[]{:S(2)}, u32[]{:S(2)}) collective-permute-start(f32[1024,128]{1,0:T(8,128)S(1)} %get-tuple-element.70.mine_ref), channel_id=1, source_target_pairs={{0,1},{1,0},{2,3},{3,2},{4,5},{5,4},{6,7},{7,6},{8,9},{9,8},{10,11... | collective-permute-start | bytes 1572872 | tf_op jit(solution)/shard_map/ppermute | solution.py:676
  44.4 12.6 %collective-permute-start.13 = (f32[128,256]{1,0:T(8,128)S(1)}, f32[128,256]{1,0:T(8,128)S(1)}, u32[]{:S(2)}, u32[]{:S(2)}) collective-permute-start(f32[128,256]{1,0:T(8,128)S(1)} %get-tuple-element.78), channel_id=1, source_target_pairs={{0,32},{32,64},{64,96},{96,0},{1,33},{33,65},{65,97},{97,1},{2,34}... | collective-permute-start | bytes 393224 | tf_op jit(solution)/shard_map/ppermute | solution.py:676
  45.4 11.5 %collective-permute-start.14 = (f32[128,256]{1,0:T(8,128)S(1)}, f32[128,256]{1,0:T(8,128)S(1)}, u32[]{:S(2)}, u32[]{:S(2)}) collective-permute-start(f32[128,256]{1,0:T(8,128)S(1)} %get-tuple-element.79), channel_id=1, source_target_pairs={{0,96},{32,0},{64,32},{96,64},{1,97},{33,1},{65,33},{97,65},{2,98}... | collective-permute-start | bytes 393224 | tf_op jit(solution)/shard_map/ppermute | solution.py:676
  47.1 9.8 %collective-permute-start.15 = (f32[128,256]{1,0:T(8,128)S(1)}, f32[128,256]{1,0:T(8,128)S(1)}, u32[]{:S(2)}, u32[]{:S(2)}) collective-permute-start(f32[128,256]{1,0:T(8,128)S(1)} %get-tuple-element.80), channel_id=1, source_target_pairs={{0,64},{32,96},{64,0},{96,32},{1,65},{33,97},{65,1},{97,33},{2,66}... | collective-permute-start | bytes 393224 | tf_op jit(solution)/shard_map/ppermute | solution.py:676
  48.7 16.1 %copy-start = (bf16[128,1024]{1,0:T(8,128)(2,1)S(1)}, bf16[128,1024]{1,0:T(8,128)(2,1)}, u32[]{:S(2)}) copy-start(bf16[128,1024]{1,0:T(8,128)(2,1)} %raw_ref.1) | copy-start | bytes 786436
  57.5 5.6 %collective-permute-start.16 = (f32[64,256]{1,0:T(8,128)S(1)}, f32[64,256]{1,0:T(8,128)S(1)}, u32[]{:S(2)}, u32[]{:S(2)}) collective-permute-start(f32[64,256]{1,0:T(8,128)S(1)} %get-tuple-element.92), channel_id=1, source_target_pairs={{0,16},{16,0},{1,17},{17,1},{2,18},{18,2},{3,19},{19,3},{4,20},{20... | collective-permute-start | bytes 196616 | tf_op jit(solution)/shard_map/ppermute | solution.py:676
  63.2 3.5 %collective-permute-start.17 = (f32[1024,128]{1,0:T(8,128)S(1)}, f32[1024,128]{1,0:T(8,128)S(1)}, u32[]{:S(2)}, u32[]{:S(2)}) collective-permute-start(f32[1024,128]{1,0:T(8,128)S(1)} %cache_grads_6.1.dq_ref), channel_id=1, source_target_pairs={{0,1},{1,0},{2,3},{3,2},{4,5},{5,4},{6,7},{7,6},{8,9},{9,8},{10,11... | collective-permute-start | bytes 1572872 | tf_op jit(solution)/shard_map/ppermute | solution.py:676
  65.4 1.3 %collective-permute-start.18 = (bf16[64,256]{1,0:T(8,128)(2,1)S(1)}, bf16[64,256]{1,0:T(8,128)(2,1)S(1)}, u32[]{:S(2)}, u32[]{:S(2)}) collective-permute-start(bf16[64,256]{1,0:T(8,128)(2,1)S(1)} %own_kv.1.kv_ref), channel_id=1, source_target_pairs={{0,1},{1,0},{2,3},{3,2},{4,5},{5,4},{6,7},{7,6},{8,9},{9,8},{10,11... | collective-permute-start | bytes 98312 | tf_op jit(solution)/shard_map/ppermute | solution.py:676
